TPU v7x, 512 devices: a whole 4x8x8 slice. The times are simulated.
512 devices in a mesh: ens: 4 (over y_lo), oy: 32 (over y_hi, z, core), ox: 4 (over x).
Axes of the slice: x: 4, y: 8 (y_hi: 2, y_lo: 4; y = y_hi * 4 + y_lo), z: 8, core: 2. Of those that a mesh axis runs over, the one named last changes fastest.
Arguments:
- state: bfloat16 [4, 128, 512, 256], P('ens', 'oy', 'ox'), may hold values from -6 to 6
- state_cot: bfloat16 [4, 128, 512, 256], P('ens', 'oy', 'ox'), may hold values from -6 to 6
- flux_cot: bfloat16 [4, 8192, 4, 128], P('ens', ('oy', 'ox')), may hold values from -6 to 6
- conv_weight: bfloat16 [9, 256, 256], replicated, may hold values from -0.125 to 0.125
- mix_weight: bfloat16 [256, 256], replicated, may hold values from -0.375 to 0.375
- flux_weight: bfloat16 [4, 256], replicated, may hold values from -3 to 3
- regrid_weights: bfloat16 [16, 128, 128], replicated, may hold values from -0.5 to 0.5
- intersection_atm: int32 [128, 4, 4], replicated, may hold values from 0 to 8191, as said below
- intersection_offset: int32 [128, 4, 4], replicated, may hold values from 0 to 15
- wet_rows: int32 [32, 4], P('oy', 'ox'), may hold values from 1 to 4
Outputs:
- input_grad: bfloat16 [4, 128, 512, 256], P('ens', 'oy', 'ox')
- weight_grads: float32 [2560, 256], P(('oy', 'ox'))
- flux_grad: float32 [4, 256], replicated
Inputs may be any that keep to these rules, and one draw needn't show every extreme that they name: `intersection_atm`: atmosphere block a lies on device a // 64, numbered oy 4 + ox. The intersections of the ocean blocks of device (oy, ox), that is of latitude rows oy 4 to oy 4 + 3 and longitude block ox, lie on exactly four atmosphere devices, two with index oy and two with index (oy + 1) mod 32 along oy. At most 5 of that device's 4 x 4 intersections lie on one atmosphere device, and for every ocean device exactly 5 lie on one of them.
All inputs are finite; a program needn't handle non-finite values.
Results may differ from a plain program's by a relative error of at most 0.0085.
Values may be sent and summed in bfloat16 or wider, within the bound.
No kernel may reach another device: no remote copies, remote signals or barrier semaphores. Data moves between devices by JAX's collectives and lax.ppermute only.
A program may use at most 64 MiB of HBM per device.

v0:
```python
import math

import jax
import jax.numpy as jnp
from jax import lax
from jax.sharding import PartitionSpec as P

CAP = 5


def with_halo(cells, sides, width):
    for axis, dim in sides:
        count = lax.axis_size(axis)
        head = lax.slice_in_dim(cells, 0, width, axis=dim)
        tail = lax.slice_in_dim(cells, cells.shape[dim] - width, cells.shape[dim], axis=dim)
        cells = jnp.concatenate(
            [
                lax.ppermute(tail, axis, [(i, (i + 1) % count) for i in range(count)]),
                cells,
                lax.ppermute(head, axis, [((i + 1) % count, i) for i in range(count)]),
            ],
            axis=dim,
        )
    return cells


def shifted(value, axis, steps):
    count = lax.axis_size(axis)
    pairs = [(source, (source + steps) % count) for source in range(count)]
    return lax.ppermute(value, axis, pairs)


def zero_ends(padded, row_index, lat_tiles):
    top_keep = jnp.where(row_index > 0, 1.0, 0.0).astype(padded.dtype)
    bottom = jnp.where(row_index < lat_tiles - 1, 1.0, 0.0).astype(padded.dtype)
    return jnp.concatenate([padded[:1] * top_keep, padded[1:-1], padded[-1:] * bottom], axis=0)


def owner_rank(owners):
    entry_count = owners.shape[-1]
    same_owner = owners[..., :, None] == owners[..., None, :]
    earlier = jnp.arange(entry_count)[None, :] < jnp.arange(entry_count)[:, None]
    return jnp.sum(jnp.logical_and(same_owner, earlier), axis=-1)


def body(
    state,
    state_cot,
    flux_cot,
    conv_weight,
    mix_weight,
    flux_weight,
    regrid_weights,
    intersection_atm,
    intersection_offset,
    wet_rows,
):
    lat_tiles = lax.axis_size("oy")
    lon_tiles = lax.axis_size("ox")
    members = lax.axis_size("ens")
    row_index = lax.axis_index("oy")
    col_index = lax.axis_index("ox")
    tile_state = state[0]
    tile_rows, block_cells, channels = tile_state.shape
    cot_flat = state_cot[0].reshape(-1, channels)
    grad_scale = 1.0 / math.sqrt(members * lat_tiles * tile_rows * lon_tiles * block_cells)
    padded = with_halo(tile_state, (("oy", 0), ("ox", 1)), 1)
    padded = zero_ends(padded, row_index, lat_tiles)
    hidden = jnp.zeros((tile_rows * block_cells, channels), jnp.float32)
    for tap_index in range(9):
        tap_row, tap_col = (tap_index // 3, tap_index % 3)
        patch_rows = padded[tap_row : tap_row + tile_rows, tap_col : tap_col + block_cells].reshape(
            -1, channels
        )
        hidden = hidden + jnp.dot(
            patch_rows, conv_weight[tap_index], preferred_element_type=jnp.float32
        )
    activation = jax.nn.silu(hidden).astype(jnp.bfloat16)
    atm_dev = flux_cot.shape[1]
    cot_blocks = flux_cot[0]
    flux_fields = cot_blocks.shape[1]
    intersections = intersection_atm.shape[2]
    entries = tile_rows * intersections
    per_dev = (
        intersection_atm.reshape(lat_tiles, tile_rows, lon_tiles, intersections)
        .transpose(0, 2, 1, 3)
        .reshape(lat_tiles, lon_tiles, entries)
    )
    per_dev_offset = (
        intersection_offset.reshape(lat_tiles, tile_rows, lon_tiles, intersections)
        .transpose(0, 2, 1, 3)
        .reshape(lat_tiles, lon_tiles, entries)
    )
    band_rows = jnp.stack([row_index, (row_index + lat_tiles - 1) % lat_tiles])
    candidate = jnp.take(per_dev, band_rows, axis=0)
    candidate_offset = jnp.take(per_dev_offset, band_rows, axis=0)
    flat_index = row_index * lon_tiles + col_index
    candidate_owner = candidate // atm_dev
    is_mine = candidate_owner == flat_index
    slot_rank = owner_rank(candidate_owner)
    local_block = jnp.where(is_mine, candidate % atm_dev, 0)
    picked_cot = cot_blocks[local_block]
    picked_maps = regrid_weights[candidate_offset]
    products = jnp.einsum(
        "qsefa,qseoa->qsefo", picked_cot, picked_maps, preferred_element_type=jnp.float32
    )
    one_hot = jnp.logical_and(
        slot_rank[..., None] == jnp.arange(CAP)[None, None, None, :], is_mine[..., None]
    ).astype(jnp.float32)
    outbound = jnp.einsum("qsec,qsefo->qscfo", one_hot, products).astype(jnp.bfloat16)
    own_entries = per_dev[row_index, col_index]
    own_owner = own_entries // atm_dev
    own_slot = owner_rank(own_owner)
    same_in, next_in = (
        lax.all_to_all(outbound[0], "ox", split_axis=0, concat_axis=0, tiled=True),
        lax.all_to_all(outbound[1], "ox", split_axis=0, concat_axis=0, tiled=True),
    )
    next_in = shifted(next_in, "oy", -1)
    arrived = jnp.concatenate([same_in, next_in], axis=0).reshape(-1, flux_fields, block_cells)
    in_next = (own_owner // lon_tiles != row_index).astype(jnp.int32)
    slot_index = (in_next * lon_tiles + own_owner % lon_tiles) * CAP + own_slot
    values = (
        arrived[slot_index]
        .astype(jnp.float32)
        .reshape(tile_rows, intersections, flux_fields, block_cells)
    )
    wet_mask = (jnp.arange(tile_rows) < wet_rows[0, 0]).astype(jnp.float32)
    flux_cells = jnp.sum(values, axis=1) * wet_mask[:, None, None]
    act_grad = lax.dot_general(
        cot_flat, mix_weight, (((1,), (1,)), ((), ())), preferred_element_type=jnp.float32
    )
    act_grad = act_grad + jnp.einsum(
        "rfb,fc->rbc", flux_cells, flux_weight.astype(jnp.float32)
    ).reshape(-1, channels)
    gate_sig = jax.nn.sigmoid(hidden)
    hidden_grad = (act_grad * gate_sig * (1.0 + hidden * (1.0 - gate_sig))).astype(jnp.bfloat16)
    padded_grad = with_halo(
        hidden_grad.reshape(tile_rows, block_cells, channels), (("oy", 0), ("ox", 1)), 1
    )
    padded_grad = zero_ends(padded_grad, row_index, lat_tiles)
    input_grad = cot_flat.astype(jnp.float32)
    tap_grads = []
    for tap_index in range(9):
        tap_row, tap_col = (tap_index // 3, tap_index % 3)
        back_rows = padded_grad[
            2 - tap_row : 2 - tap_row + tile_rows, 2 - tap_col : 2 - tap_col + block_cells
        ].reshape(-1, channels)
        input_grad = input_grad + lax.dot_general(
            back_rows,
            conv_weight[tap_index],
            (((1,), (1,)), ((), ())),
            preferred_element_type=jnp.float32,
        )
        patch_rows = padded[tap_row : tap_row + tile_rows, tap_col : tap_col + block_cells].reshape(
            -1, channels
        )
        tap_grads.append(
            lax.dot_general(
                patch_rows,
                hidden_grad,
                (((0,), (0,)), ((), ())),
                preferred_element_type=jnp.float32,
            )
        )
    tap_grads.append(
        lax.dot_general(
            activation, cot_flat, (((0,), (0,)), ((), ())), preferred_element_type=jnp.float32
        )
    )
    weight_term = jnp.concatenate(tap_grads, axis=0) * grad_scale
    flux_term = (
        jnp.einsum(
            "rfb,rbc->fc",
            flux_cells,
            activation.reshape(tile_rows, block_cells, channels).astype(jnp.float32),
        )
        * grad_scale
    )
    share_rows = weight_term.shape[0] // (lat_tiles * lon_tiles)
    grad_total, flux_total = lax.psum((weight_term, flux_term), ("ens", "oy", "ox"))
    share_index = lax.axis_index(("oy", "ox"))
    weight_out = lax.dynamic_slice_in_dim(grad_total, share_index * share_rows, share_rows, 0)
    input_out = input_grad.reshape(1, tile_rows, block_cells, channels).astype(jnp.bfloat16)
    return (input_out, weight_out, flux_total)


def solution(mesh):
    in_specs = (
        P("ens", "oy", "ox", None),
        P("ens", "oy", "ox", None),
        P("ens", ("oy", "ox"), None, None),
        P(),
        P(),
        P(),
        P(),
        P(),
        P(),
        P("oy", "ox"),
    )
    out_specs = (P("ens", "oy", "ox", None), P(("oy", "ox"), None), P())
    return jax.shard_map(body, mesh=mesh, in_specs=in_specs, out_specs=out_specs, check_vma=False)
```

profile of v0, /device:TPU:24, one launch (start us, length us, event | category | flops | bytes accessed | tf_op | source)
XLA Modules:
  0.0 370.8 jit_solution(12591947772248203212)
XLA Ops:
  8.1 1.9 collective-permute-start.1
  10.1 13.0 %collective-permute-start.2 = (bf16[1,128,256]{2,1,0:T(8,128)(2,1)S(1)}, bf16[1,128,256]{2,1,0:T(8,128)(2,1)S(1)}, u32[]{:S(2)}, u32[]{:S(2)}) collective-permute-start(bf16[1,128,256]{2,1,0:T(8,128)(2,1)S(1)} %get-tuple-element.42), channel_id=1, source_target_pairs={{4,0},{8,4},{12,8},{16,12},{20,16},{24,20},{28,24},{32,28},{36,32}... | collective-permute-start | bytes 196616 | tf_op jit(solution)/shard_map/ppermute | solution.py:20
  23.1 1.0 reshape.342
  24.4 1.0 reshape.340
  27.0 3.0 gather_fusion.1
  30.8 4.4 %fusion.75 = bf16[2,4,16,4,128]{4,3,2,1,0:T(4,128)(2,1)S(1)} fusion(bf16[2,4,16,4,128]{4,3,2,1,0:T(4,128)(2,1)S(1)} %bitcast.217, bf16[2,4,16,128,128]{4,3,2,1,0:T(8,128)(2,1)} %bitcast.180), kind=kOutput, calls=%fused_computation.201 | convolution fusion | flops 16777216 | bytes 4456448 | tf_op jit(solution)/shard_map/qsefa,qseoa->qsefo/dot_general | solution.py:104
  36.4 4.3 %all-to-all-start.1 = ((bf16[4,5,4,128]{3,2,1,0:T(4,128)(2,1)}), bf16[4,5,4,128]{3,2,1,0:T(4,128)(2,1)S(1)}, u32[]{:S(2)}, u32[]{:S(2)}) async-start(bf16[4,5,4,128]{3,2,1,0:T(4,128)(2,1)} %copy.41), calls=%async_computation.1 | async-start | bytes 40960 | tf_op jit(solution)/shard_map/all_to_all | solution.py:116
  42.6 3.5 all-to-all-done.1
  46.1 3.3 all-to-all-start
  49.4 1.9 collective-permute-start
  51.3 3.3 all-to-all-done
  55.4 2.5 collective-permute-start.3
  57.9 4.6 %collective-permute-start.4 = (bf16[6,1,256]{2,1,0:T(2,128)(2,1)S(1)}, bf16[6,1,256]{2,1,0:T(2,128)(2,1)S(1)}, u32[]{:S(2)}, u32[]{:S(2)}) collective-permute-start(bf16[6,1,256]{2,1,0:T(2,128)(2,1)S(1)} %get-tuple-element.20), channel_id=1, source_target_pairs={{1,0},{2,1},{3,2},{0,3},{5,4},{6,5},{7,6},{4,7},{9,8},{10,9},{11,1... | collective-permute-start | bytes 9224 | tf_op jit(solution)/shard_map/ppermute | solution.py:20
  62.8 1.0 collective-permute-done.4
  69.9 1.7 broadcast_multiply_fusion
  71.6 1.9 collective-permute-start.5
  73.5 9.7 %collective-permute-start.6 = (bf16[1,128,256]{2,1,0:T(8,128)(2,1)S(1)}, bf16[1,128,256]{2,1,0:T(8,128)(2,1)S(1)}, u32[]{:S(2)}, u32[]{:S(2)}) collective-permute-start(bf16[1,128,256]{2,1,0:T(8,128)(2,1)S(1)} %get-tuple-element.40), channel_id=1, source_target_pairs={{4,0},{8,4},{12,8},{16,12},{20,16},{24,20},{28,24},{32,28},{36,32}... | collective-permute-start | bytes 196616 | tf_op jit(solution)/shard_map/ppermute | solution.py:20
  83.9 1.8 collective-permute-done.6
  85.7 2.4 collective-permute-start.7
  88.1 4.9 %collective-permute-start.8 = (bf16[6,1,256]{2,1,0:T(2,128)(2,1)S(1)}, bf16[6,1,256]{2,1,0:T(2,128)(2,1)S(1)}, u32[]{:S(2)}, u32[]{:S(2)}) collective-permute-start(bf16[6,1,256]{2,1,0:T(2,128)(2,1)S(1)} %get-tuple-element.16), channel_id=1, source_target_pairs={{1,0},{2,1},{3,2},{0,3},{5,4},{6,5},{7,6},{4,7},{9,8},{10,9},{11,1... | collective-permute-start | bytes 9224 | tf_op jit(solution)/shard_map/ppermute | solution.py:20
  93.2 100.4 %psum.15 = f32[4,256]{1,0:T(4,128)} all-reduce(f32[4,256]{1,0:T(4,128)S(1)} %fusion.9), channel_id=1, replica_groups=mesh['ens'=4,'oy'=32,'ox'=4] {'ens','oy','ox'}, use_global_device_ids=true, to_apply=%region_4.6 | all-reduce | flops 1024 | bytes 8192 | tf_op jit(solution)/shard_map/psum | solution.py:180
  196.1 1.0 fusion.7
  197.1 165.6 %all-reduce.2.cloned.1.call-done = f32[2560,256]{1,0:T(8,128)} async-done(((f32[2560,256]{1,0:T(8,128)}), f32[2560,256]{1,0:T(8,128)}) %all-reduce.2.cloned.1.call-update) | async-done | bytes 2621456 | tf_op jit(solution)/shard_map/psum | solution.py:180
  362.6 1.4 constant_dynamic-slice_fusion
  (95 shorter events, 16.4 us)
Async XLA Ops:
  7.2 19.9 %copy-start = (bf16[16,128,128]{2,1,0:T(8,128)(2,1)S(1)}, bf16[16,128,128]{2,1,0:T(8,128)(2,1)}, u32[]{:S(2)}) copy-start(bf16[16,128,128]{2,1,0:T(8,128)(2,1)} %param.18) | copy-start | bytes 1572868
  8.1 47.2 %collective-permute-start.1 = (bf16[1,128,256]{2,1,0:T(8,128)(2,1)S(1)}, bf16[1,128,256]{2,1,0:T(8,128)(2,1)S(1)}, u32[]{:S(2)}, u32[]{:S(2)}) collective-permute-start(bf16[1,128,256]{2,1,0:T(8,128)(2,1)S(1)} %get-tuple-element.41), channel_id=1, source_target_pairs={{0,4},{4,8},{8,12},{12,16},{16,20},{20,24},{24,28},{28,32},{32,36}... | collective-permute-start | bytes 196616 | tf_op jit(solution)/shard_map/ppermute | solution.py:18
  10.1 45.3 %collective-permute-start.2 = (bf16[1,128,256]{2,1,0:T(8,128)(2,1)S(1)}, bf16[1,128,256]{2,1,0:T(8,128)(2,1)S(1)}, u32[]{:S(2)}, u32[]{:S(2)}) collective-permute-start(bf16[1,128,256]{2,1,0:T(8,128)(2,1)S(1)} %get-tuple-element.42), channel_id=1, source_target_pairs={{4,0},{8,4},{12,8},{16,12},{20,16},{24,20},{28,24},{32,28},{36,32}... | collective-permute-start | bytes 196616 | tf_op jit(solution)/shard_map/ppermute | solution.py:20
  27.0 3.1 copy-start.4
  30.1 11.0 %copy-start.1 = (bf16[1,4,128,256]{3,2,1,0:T(8,128)(2,1)S(1)}, bf16[1,4,128,256]{3,2,1,0:T(8,128)(2,1)}, u32[]{:S(2)}) copy-start(bf16[1,4,128,256]{3,2,1,0:T(8,128)(2,1)} %param.12) | copy-start | bytes 786436
  30.1 11.0 %copy-start.2 = (bf16[9,256,256]{2,1,0:T(8,128)(2,1)S(1)}, bf16[9,256,256]{2,1,0:T(8,128)(2,1)}, u32[]{:S(2)}) copy-start(bf16[9,256,256]{2,1,0:T(8,128)(2,1)} %param.15) | copy-start | bytes 3538948
  30.8 31.6 %copy-start.5 = (bf16[4,256]{1,0:T(4,128)(2,1)S(1)}, bf16[4,256]{1,0:T(4,128)(2,1)}, u32[]{:S(2)}) copy-start(bf16[4,256]{1,0:T(4,128)(2,1)} %param.17) | copy-start | bytes 6148
  36.4 9.7 %all-to-all-start.1 = ((bf16[4,5,4,128]{3,2,1,0:T(4,128)(2,1)}), bf16[4,5,4,128]{3,2,1,0:T(4,128)(2,1)S(1)}, u32[]{:S(2)}, u32[]{:S(2)}) async-start(bf16[4,5,4,128]{3,2,1,0:T(4,128)(2,1)} %copy.41), calls=%async_computation.1 | async-start | bytes 40960 | tf_op jit(solution)/shard_map/all_to_all | solution.py:116
  46.1 8.6 %all-to-all-start = ((bf16[4,5,4,128]{3,2,1,0:T(4,128)(2,1)}), bf16[4,5,4,128]{3,2,1,0:T(4,128)(2,1)S(1)}, u32[]{:S(2)}, u32[]{:S(2)}) async-start(bf16[4,5,4,128]{3,2,1,0:T(4,128)(2,1)} %copy.40), calls=%async_computation | async-start | bytes 40960 | tf_op jit(solution)/shard_map/all_to_all | solution.py:115
  49.3 313.3 %all-reduce.2.cloned.1.call-start = ((), (), s32[]{:S(2)}) async-start(), calls=%async_computation.2 | async-start | bytes 5242880 | tf_op jit(solution)/shard_map/psum | solution.py:180
  49.4 5.3 %collective-permute-start = (bf16[4,5,4,128]{3,2,1,0:T(4,128)(2,1)S(1)}, bf16[4,5,4,128]{3,2,1,0:T(4,128)(2,1)S(1)}, u32[]{:S(2)}, u32[]{:S(2)}) collective-permute-start(bf16[4,5,4,128]{3,2,1,0:T(4,128)(2,1)S(1)} %all-to-all-done.1), channel_id=1, source_target_pairs={{0,124},{4,0},{8,4},{12,8},{16,12},{20,16},{24,20},{28,24},{32,28}... | collective-permute-start | bytes 61448 | tf_op jit(solution)/shard_map/ppermute | solution.py:30
  55.4 7.4 %collective-permute-start.3 = (bf16[6,1,256]{2,1,0:T(2,128)(2,1)S(1)}, bf16[6,1,256]{2,1,0:T(2,128)(2,1)S(1)}, u32[]{:S(2)}, u32[]{:S(2)}) collective-permute-start(bf16[6,1,256]{2,1,0:T(2,128)(2,1)S(1)} %get-tuple-element.19), channel_id=1, source_target_pairs={{0,1},{1,2},{2,3},{3,0},{4,5},{5,6},{6,7},{7,4},{8,9},{9,10},{10,1... | collective-permute-start | bytes 9224 | tf_op jit(solution)/shard_map/ppermute | solution.py:18
  57.9 5.9 %collective-permute-start.4 = (bf16[6,1,256]{2,1,0:T(2,128)(2,1)S(1)}, bf16[6,1,256]{2,1,0:T(2,128)(2,1)S(1)}, u32[]{:S(2)}, u32[]{:S(2)}) collective-permute-start(bf16[6,1,256]{2,1,0:T(2,128)(2,1)S(1)} %get-tuple-element.20), channel_id=1, source_target_pairs={{1,0},{2,1},{3,2},{0,3},{5,4},{6,5},{7,6},{4,7},{9,8},{10,9},{11,1... | collective-permute-start | bytes 9224 | tf_op jit(solution)/shard_map/ppermute | solution.py:20
  65.8 1.0 copy-start.3
  65.8 1.0 copy-start.6
  71.6 12.3 %collective-permute-start.5 = (bf16[1,128,256]{2,1,0:T(8,128)(2,1)S(1)}, bf16[1,128,256]{2,1,0:T(8,128)(2,1)S(1)}, u32[]{:S(2)}, u32[]{:S(2)}) collective-permute-start(bf16[1,128,256]{2,1,0:T(8,128)(2,1)S(1)} %get-tuple-element.39), channel_id=1, source_target_pairs={{0,4},{4,8},{8,12},{12,16},{16,20},{20,24},{24,28},{28,32},{32,36}... | collective-permute-start | bytes 196616 | tf_op jit(solution)/shard_map/ppermute | solution.py:18
  73.5 12.2 %collective-permute-start.6 = (bf16[1,128,256]{2,1,0:T(8,128)(2,1)S(1)}, bf16[1,128,256]{2,1,0:T(8,128)(2,1)S(1)}, u32[]{:S(2)}, u32[]{:S(2)}) collective-permute-start(bf16[1,128,256]{2,1,0:T(8,128)(2,1)S(1)} %get-tuple-element.40), channel_id=1, source_target_pairs={{4,0},{8,4},{12,8},{16,12},{20,16},{24,20},{28,24},{32,28},{36,32}... | collective-permute-start | bytes 196616 | tf_op jit(solution)/shard_map/ppermute | solution.py:20
  85.7 107.9 %collective-permute-start.7 = (bf16[6,1,256]{2,1,0:T(2,128)(2,1)S(1)}, bf16[6,1,256]{2,1,0:T(2,128)(2,1)S(1)}, u32[]{:S(2)}, u32[]{:S(2)}) collective-permute-start(bf16[6,1,256]{2,1,0:T(2,128)(2,1)S(1)} %get-tuple-element.15), channel_id=1, source_target_pairs={{0,1},{1,2},{2,3},{3,0},{4,5},{5,6},{6,7},{7,4},{8,9},{9,10},{10,1... | collective-permute-start | bytes 9224 | tf_op jit(solution)/shard_map/ppermute | solution.py:18
  88.1 105.5 %collective-permute-start.8 = (bf16[6,1,256]{2,1,0:T(2,128)(2,1)S(1)}, bf16[6,1,256]{2,1,0:T(2,128)(2,1)S(1)}, u32[]{:S(2)}, u32[]{:S(2)}) collective-permute-start(bf16[6,1,256]{2,1,0:T(2,128)(2,1)S(1)} %get-tuple-element.16), channel_id=1, source_target_pairs={{1,0},{2,1},{3,2},{0,3},{5,4},{6,5},{7,6},{4,7},{9,8},{10,9},{11,1... | collective-permute-start | bytes 9224 | tf_op jit(solution)/shard_map/ppermute | solution.py:20
Sparse Core Ops, SparseCore 0:
  83.6 278.9 all-reduce.1
where the time goes:
time: 372 us; the launch traced here: 371 us
  waiting for transfers between devices  176 us (47%)
  blocking collectives  100 us (27%)
  starting transfers between devices  50.3 us (14%)
  between operations  15.3 us (4%)
  matrix products  13.4 us (4%)
  local copies, waits for them, and re-layouts  12.3 us (3%)
    psum x1, waiting for transfers between devices, body(): lax.psum((weight_term, flux_term), ('ens', 'oy', 'ox'))  166 us
    psum x1, blocking collectives, body(): lax.psum((weight_term, flux_term), ('ens', 'oy', 'ox'))  100 us
    ppermute x4, starting transfers between devices, with_halo(): lax.ppermute(head, axis, [((i + 1) % count, i) for i in range(count)])  32.1 us
    ppermute x4, starting transfers between devices, with_halo(): lax.ppermute(tail, axis, [(i, (i + 1) % count) for i in range(count)])  8.72 us
  transfers between devices with their start and end apart: 12, of which 6 were waited for; matrix products, arithmetic and copies ran while one was open for 5% of the time, Pallas kernels for 0%

commit v1 on v0

v1 whole, which is shorter than its diff:
```python
import math

import jax
import jax.numpy as jnp
from jax import lax
from jax.experimental import pallas as pl
from jax.experimental.pallas import tpu as pltpu
from jax.sharding import Mesh, PartitionSpec as P

BF = jnp.bfloat16
F32 = jnp.float32
OY = ("yh", "z", "core")
ROWS = 4
CELLS = 128
CH = 256
NLON = 4
ENTRIES = 16
SHARE = 20
VM = pl.BlockSpec(memory_space=pltpu.VMEM)
SM = pl.BlockSpec(memory_space=pltpu.SMEM)


def oy_index():
    return lax.axis_index("yh") * 16 + lax.axis_index("z") * 2 + lax.axis_index("core")


def call(kernel, outs, scratch=(), specs=None, n_in=None):
    return pl.pallas_call(
        kernel,
        out_shape=outs,
        in_specs=specs if specs is not None else [VM] * n_in,
        out_specs=jax.tree.map(lambda _: VM, outs),
        scratch_shapes=list(scratch),
    )


def struct(shape, dtype):
    return jax.ShapeDtypeStruct(shape, dtype)


def split_two(value):
    high = value.astype(BF)
    low = (value - high.astype(F32)).astype(BF)
    return high, low


def dot(a, b, dims):
    return lax.dot_general(a, b, (dims, ((), ())), preferred_element_type=F32)


def edge_rows(mid, above, below, edge):
    at = 0 if edge == 0 else 15
    base = 0 if edge == 0 else CELLS - 16
    rows = [above[base : base + 16, :].astype(F32)[at : at + 1]]
    for r in range(ROWS):
        rows.append(mid[r * CELLS + base : r * CELLS + base + 16, :].astype(F32)[at : at + 1])
    rows.append(below[base : base + 16, :].astype(F32)[at : at + 1])
    rows.append(jnp.zeros((2, CH), F32))
    return jnp.concatenate(rows, axis=0)


def pack_kernel(iatm, state, below, above, flux_own, out):
    oy = oy_index()
    ox = lax.axis_index("ox")
    me = (oy * NLON + ox) * 64
    nxt = (lax.rem(oy + 1, 32) * NLON + ox) * 64
    row = lax.broadcasted_iota(jnp.int32, (64, 128), 0)
    lane = lax.broadcasted_iota(jnp.int32, (64, 128), 1)
    target = jnp.zeros((64, 128), jnp.int32)
    for d in range(NLON):
        for r in range(ROWS):
            for k in range(4):
                value = iatm[((oy * ROWS + r) * NLON + d) * 4 + k]
                target = jnp.where(row == d * 16 + r * 4 + k, value, target)
    wanted = jnp.where(lane < 64, lane + me, lane - 64 + nxt)
    pick = jnp.where(target == wanted, 1.0, 0.0).astype(BF)
    for h in range(2):
        source = jnp.concatenate(
            [flux_own[h * 64 : h * 64 + 64, :], below[128 + h * 64 : 192 + h * 64, :]], axis=0
        )
        got = dot(pick, source, ((1,), (0,))).astype(BF)
        for d in range(NLON):
            out[d, h * 16 : h * 16 + 16, :] = got[d * 16 : d * 16 + 16]
    top_keep = jnp.where(oy > 0, 1.0, 0.0)
    bottom_keep = jnp.where(oy < 31, 1.0, 0.0)
    part = lax.broadcasted_iota(jnp.int32, (8, CH), 0)
    keep = jnp.where(part == 0, top_keep, jnp.where(part == ROWS + 1, bottom_keep, 1.0))
    first = edge_rows(state, above, below, 0) * keep
    last = edge_rows(state, above, below, 1) * keep
    for d in range(NLON):
        to_right = jnp.where(lax.rem(ox + 1, NLON) == d, 1.0, 0.0)
        to_left = jnp.where(lax.rem(ox + NLON - 1, NLON) == d, 1.0, 0.0)
        halo = last * to_right + first * to_left
        out[d, 32:48, :] = jnp.concatenate([halo, jnp.zeros((8, CH), F32)], axis=0).astype(BF)


def build_shifts(shifted, mid, above, below, left, right, top_keep, bottom_keep):
    cell = lax.broadcasted_iota(jnp.int32, (CELLS, CH), 0)
    for r in range(ROWS + 2):
        if r == 0:
            value = above[0:CELLS, :].astype(F32) * top_keep
        elif r == ROWS + 1:
            value = below[0:CELLS, :].astype(F32) * bottom_keep
        else:
            value = mid[(r - 1) * CELLS : r * CELLS, :].astype(F32)
        shifted[1, r * CELLS : (r + 1) * CELLS, :] = value.astype(BF)
        plus = jnp.where(cell == CELLS - 1, right[r : r + 1, :], pltpu.roll(value, CELLS - 1, 0))
        minus = jnp.where(cell == 0, left[r : r + 1, :], pltpu.roll(value, 1, 0))
        shifted[2, r * CELLS : (r + 1) * CELLS, :] = plus.astype(BF)
        shifted[0, r * CELLS : (r + 1) * CELLS, :] = minus.astype(BF)


def main_kernel(
    ioff,
    wet,
    state,
    below,
    above,
    arrived,
    cot,
    conv,
    mix,
    flux_weight,
    regrid,
    hg_out,
    send_out,
    keep_out,
    zrow_out,
    shifted,
    turned,
    hidden,
    grads,
):
    oy = oy_index()
    ox = lax.axis_index("ox")
    core = lax.axis_index("core")
    top_keep = jnp.where(oy > 0, 1.0, 0.0)
    bottom_keep = jnp.where(oy < 31, 1.0, 0.0)
    left = arrived[lax.rem(ox + NLON - 1, NLON), 32:48, :].astype(F32)
    right = arrived[lax.rem(ox + 1, NLON), 32:48, :].astype(F32)
    build_shifts(shifted, state, above, below, left, right, top_keep, bottom_keep)
    for half in range(2):
        acc = jnp.zeros((256, CH), F32)
        for t in range(9):
            start = (t // 3) * CELLS + half * 256
            acc = acc + dot(shifted[t % 3, start : start + 256, :], conv[t], ((1,), (0,)))
        hidden[half * 256 : half * 256 + 256, :] = acc
    flux = [
        sum(arrived[s, h * 16 : h * 16 + 16, :].astype(F32) for s in range(NLON)) for h in range(2)
    ]
    blocks = jnp.concatenate(
        [flux[f // 2][:, (f % 2) * 128 : (f % 2) * 128 + 128] for f in range(4)], axis=0
    ).astype(BF)
    row = lax.broadcasted_iota(jnp.int32, (64, 128), 0)
    offset = jnp.zeros((64, 128), jnp.int32)
    for r in range(ROWS):
        for k in range(4):
            value = ioff[((oy * ROWS + r) * NLON + ox) * 4 + k]
            offset = jnp.where(lax.rem(row, 16) == r * 4 + k, value, offset)
    contribution = jnp.zeros((64, 128), F32)
    for m in range(16):
        product = dot(blocks, regrid[m], ((1,), (1,)))
        contribution = jnp.where(offset == m, product, contribution)
    contribution = contribution.astype(BF)
    out_row = lax.broadcasted_iota(jnp.int32, (16, 64), 0)
    in_row = lax.broadcasted_iota(jnp.int32, (16, 64), 1)
    same_field = lax.rem(out_row, 4) == in_row // 16
    same_row = out_row // 4 == lax.rem(in_row, 16) // 4
    is_wet = out_row // 4 < wet[0, 0]
    gather = jnp.where(
        jnp.logical_and(jnp.logical_and(same_field, same_row), is_wet), 1.0, 0.0
    ).astype(BF)
    cells = dot(gather, contribution, ((1,), (0,)))
    cells_high, cells_low = split_two(cells)
    cells_pair = jnp.concatenate([cells_high, cells_low], axis=0)
    pair_row = lax.broadcasted_iota(jnp.int32, (32, CH), 0)
    field_weights = jnp.concatenate([flux_weight[...].astype(F32)] * 8, axis=0)
    flux_part = jnp.zeros((32, CH), F32)
    for r in range(ROWS):
        lo, hi = r * CELLS, (r + 1) * CELLS
        mine = lax.rem(pair_row, 16) // 4 == r
        weights = jnp.where(mine, field_weights, 0.0).astype(BF)
        act_grad = dot(cot[lo:hi, :], mix[...], ((1,), (1,)))
        act_grad = act_grad + dot(cells_pair, weights, ((0,), (0,)))
        value = hidden[lo:hi, :]
        gate = jax.nn.sigmoid(value)
        activation = (value * gate).astype(BF)
        grad = (act_grad * gate * (1.0 + value * (1.0 - gate))).astype(BF)
        hg_out[lo:hi, :] = grad
        turned[3, :, lo:hi] = activation.T
        flux_part = flux_part + jnp.where(
            mine, dot(cells_pair, activation, ((1,), (0,))), 0.0
        )
    scale = 1.0 / 512.0
    flux_total = jnp.zeros((4, CH), F32)
    for part in range(8):
        flux_total = flux_total + flux_part[part * 4 : part * 4 + 4]
    flux_high, flux_low = split_two(flux_total * scale)
    flux_rows = jnp.concatenate([flux_high.astype(F32), flux_low.astype(F32)], axis=0)
    for q in range(3):
        turned[q] = shifted[q].T
    for t in range(9):
        start = (t // 3) * CELLS
        product = dot(turned[t % 3, :, start : start + 512], hg_out[...], ((1,), (0,)))
        grads[t * CH : (t + 1) * CH, :] = product * scale
    product = dot(turned[3, :, 0:512], cot[...], ((1,), (0,)))
    grads[9 * CH : 10 * CH, :] = product * scale
    for m in range(16):
        mine = pl.multiple_of(m * 160 + core * 80, 8)
        other = pl.multiple_of(m * 160 + 80 - core * 80, 8)
        keep_out[m * 80 : m * 80 + 80, :] = grads[pl.ds(mine, 80), :]
        send_out[m * 80 : m * 80 + 80, :] = grads[pl.ds(other, 80), :].astype(BF)
    keep_out[1280:1288, :] = flux_rows
    send_out[1280:1296, :] = jnp.concatenate(
        [flux_rows, jnp.zeros((8, CH), F32)], axis=0
    ).astype(BF)
    first, last = hg_out[0:CELLS, :], hg_out[3 * CELLS : 4 * CELLS, :]
    send_out[1296:1424, :] = jnp.where(core == 0, last, first)
    zrow_out[...] = jnp.where(core == 0, first, last)


def merge_kernel(keep, got, zrow, hg, out, rows_out, total, moved):
    oy = oy_index()
    ox = lax.axis_index("ox")
    core = lax.axis_index("core")
    total[...] = keep[0:1280, :] + got[0:1280, :].astype(F32)
    for c in range(NLON):
        for z in range(8):
            for yh in range(2):
                m = yh * 8 + z
                to = c * 320 + (z * 2 + yh) * SHARE
                moved[to : to + SHARE, :] = total[m * 80 + c * SHARE : m * 80 + c * SHARE + SHARE, :]
    flux = keep[1280:1288, :] + got[1280:1296, :].astype(F32)[0:8]
    flux_high, flux_low = split_two(flux[0:4] + flux[4:8])
    top_keep = jnp.where(oy > 0, 1.0, 0.0)
    bottom_keep = jnp.where(oy < 31, 1.0, 0.0)
    inside = got[1296:1424, :].astype(F32)
    across = zrow[...].astype(F32)
    above = (jnp.where(core == 0, across, inside) * top_keep).astype(BF)
    below = (jnp.where(core == 0, inside, across) * bottom_keep).astype(BF)
    rows_out[0:CELLS, :] = above
    rows_out[CELLS : 2 * CELLS, :] = below
    first = edge_rows(hg, above, below, 0)
    last = edge_rows(hg, above, below, 1)
    for c in range(NLON):
        to_right = jnp.where(lax.rem(ox + 1, NLON) == c, 1.0, 0.0)
        to_left = jnp.where(lax.rem(ox + NLON - 1, NLON) == c, 1.0, 0.0)
        halo = last * to_right + first * to_left
        out[c, 0:320, :] = moved[c * 320 : c * 320 + 320, :].astype(BF)
        out[c, 320:336, :] = jnp.concatenate(
            [flux_high.astype(F32), flux_low.astype(F32), halo], axis=0
        ).astype(BF)


def sum_flux(pieces):
    total = pieces[0]
    for piece in pieces[1:]:
        total = total + piece
    return total[0:4] + total[4:8]


def ox_sum_kernel(got, out):
    for z in range(8):
        piece = got[0, z * 40 : z * 40 + 40, :].astype(F32)
        for s in range(1, NLON):
            piece = piece + got[s, z * 40 : z * 40 + 40, :].astype(F32)
        out[z, 0:40, :] = piece.astype(BF)
    flux = sum_flux([got[s, 320:336, :].astype(F32)[0:8] for s in range(NLON)])
    high, low = split_two(flux)
    rows = jnp.concatenate([high.astype(F32), low.astype(F32)], axis=0).astype(BF)
    for z in range(8):
        out[z, 40:48, :] = rows


def z_sum_kernel(got, out):
    piece = got[0].astype(F32)
    for s in range(1, 8):
        piece = piece + got[s].astype(F32)
    high, low = split_two(piece[40:44] + piece[44:48])
    flux = jnp.concatenate([high.astype(F32), low.astype(F32)], axis=0)
    pad = jnp.zeros((4, CH), F32)
    for yh in range(2):
        rows = jnp.concatenate([piece[yh * SHARE : yh * SHARE + SHARE], pad, flux], axis=0).astype(BF)
        for e in range(4):
            out[e * 2 + yh] = rows


def last_sum_kernel(got, weight_out, flux_out):
    piece = got[0].astype(F32)
    for s in range(1, 8):
        piece = piece + got[s].astype(F32)
    weight_out[...] = piece[0:SHARE]
    flux_out[...] = piece[24:28] + piece[28:32]


def input_kernel(hg, rows, arrived, cot, conv, out, shifted):
    ox = lax.axis_index("ox")
    left = arrived[lax.rem(ox + NLON - 1, NLON), 320:336, :].astype(F32)[8:16]
    right = arrived[lax.rem(ox + 1, NLON), 320:336, :].astype(F32)[8:16]
    build_shifts(
        shifted, hg, rows, rows.at[CELLS : 2 * CELLS, :], left, right, 1.0, 1.0
    )
    for half in range(2):
        acc = cot[half * 256 : half * 256 + 256, :].astype(F32)
        for t in range(9):
            start = (2 - t // 3) * CELLS + half * 256
            acc = acc + dot(shifted[2 - t % 3, start : start + 256, :], conv[t], ((1,), (1,)))
        out[half * 256 : half * 256 + 256, :] = acc.astype(BF)


def body(
    state,
    state_cot,
    flux_cot,
    conv_weight,
    mix_weight,
    flux_weight,
    regrid_weights,
    intersection_atm,
    intersection_offset,
    wet_rows,
):
    state = state.reshape(ROWS * CELLS, CH)
    cot = state_cot.reshape(ROWS * CELLS, CH)
    flux_own = (
        flux_cot.reshape(64, 2, CH).transpose(1, 0, 2).reshape(128, CH)
    )
    iatm = intersection_atm.reshape(-1)
    ioff = intersection_offset.reshape(-1)
    up = jnp.concatenate([state[0:CELLS], flux_own], axis=0)
    below = lax.ppermute(up, OY, [((i + 1) % 32, i) for i in range(32)])
    above = lax.ppermute(state[3 * CELLS :], OY, [(i, (i + 1) % 32) for i in range(32)])
    packed = call(
        pack_kernel, struct((NLON, 48, CH), BF), specs=[SM] + [VM] * 4
    )(iatm, state, below, above, flux_own)
    arrived = lax.all_to_all(packed, "ox", 0, 0, tiled=True)
    hg, send, keep, zrow = call(
        main_kernel,
        (
            struct((ROWS * CELLS, CH), BF),
            struct((1424, CH), BF),
            struct((1288, CH), F32),
            struct((CELLS, CH), BF),
        ),
        scratch=[
            pltpu.VMEM((3, 768, CH), BF),
            pltpu.VMEM((4, CH, 768), BF),
            pltpu.VMEM((512, CH), F32),
            pltpu.VMEM((2560, CH), F32),
        ],
        specs=[SM, SM] + [VM] * 9,
    )(ioff, wet_rows, state, below, above, arrived, cot, conv_weight, mix_weight, flux_weight, regrid_weights)
    zgot = lax.ppermute(zrow, OY, [(i, (i - 1) % 32 if i % 2 == 0 else (i + 1) % 32) for i in range(32)])
    got = lax.ppermute(send, "core", [(0, 1), (1, 0)])
    packed, rows = call(
        merge_kernel,
        (struct((NLON, 336, CH), BF), struct((2 * CELLS, CH), BF)),
        scratch=[pltpu.VMEM((1280, CH), F32), pltpu.VMEM((1280, CH), F32)],
        n_in=4,
    )(keep, got, zgot, hg)
    by_ox = lax.all_to_all(packed, "ox", 0, 0, tiled=True)
    packed = call(ox_sum_kernel, struct((8, 48, CH), BF), n_in=1)(by_ox)
    by_z = lax.all_to_all(packed, "z", 0, 0, tiled=True)
    packed = call(z_sum_kernel, struct((8, 32, CH), BF), n_in=1)(by_z)
    by_rest = lax.all_to_all(packed, ("ens", "yh"), 0, 0, tiled=True)
    weight_out, flux_out = call(
        last_sum_kernel, (struct((SHARE, CH), F32), struct((4, CH), F32)), n_in=1
    )(by_rest)
    input_grad = call(
        input_kernel,
        struct((ROWS * CELLS, CH), BF),
        scratch=[pltpu.VMEM((3, 768, CH), BF)],
        n_in=5,
    )(hg, rows, by_ox, cot, conv_weight)
    return (input_grad.reshape(1, ROWS, CELLS, CH), weight_out, flux_out)


def solution(mesh):
    fine = Mesh(mesh.devices.reshape(4, 2, 8, 2, 4), ("ens", "yh", "z", "core", "ox"))
    in_specs = (
        P("ens", OY, "ox", None),
        P("ens", OY, "ox", None),
        P("ens", OY + ("ox",), None, None),
        P(),
        P(),
        P(),
        P(),
        P(),
        P(),
        P(OY, "ox"),
    )
    out_specs = (P("ens", OY, "ox", None), P(OY + ("ox",), None), P())
    return jax.shard_map(body, mesh=fine, in_specs=in_specs, out_specs=out_specs, check_vma=False)
```

time: 372 us -> 112 us (0.30)
  the two profiles are of different devices: /device:TPU:24 before, /device:TPU:8 now
where the time goes in v1:
time: 112 us; the launch traced here: 111 us
  starting transfers between devices  30.1 us (27%)
  blocking collectives  27 us (24%)
  waiting for transfers between devices  26.5 us (24%)
  Pallas kernels  18.9 us (17%)
  local copies, waits for them, and re-layouts  7.4 us (7%)
  between operations  1.39 us (1%)
    ppermute x1, starting transfers between devices, body(): below = lax.ppermute(up, OY, [((i + 1) % 32, i) for i in range(32)])  14.7 us
    all_to_all x1, blocking collectives, body(): by_z = lax.all_to_all(packed, 'z', 0, 0, tiled=True)  13.8 us
    all_to_all x1, blocking collectives, body(): by_ox = lax.all_to_all(packed, 'ox', 0, 0, tiled=True)  13.2 us
    ppermute x1, waiting for transfers between devices, body(): lax.ppermute(zrow, OY, [(i, (i - 1) % 32 if i % 2 == 0 else (i + 1) % 32)...  9.89 us
    ppermute x1, waiting for transfers between devices, body(): lax.ppermute(state[3 * CELLS:], OY, [(i, (i + 1) % 32) for i in range(32)])  8.26 us
    pallas_call x1, Pallas kernels, body(): call(main_kernel, (struct((ROWS * CELLS, CH), BF), struct((1424, CH), BF)...  6.03 us
    all_to_all x1, starting transfers between devices, body(): by_rest = lax.all_to_all(packed, ('ens', 'yh'), 0, 0, tiled=True)  5.33 us
    all_to_all x1, starting transfers between devices, body(): arrived = lax.all_to_all(packed, 'ox', 0, 0, tiled=True)  4.29 us
  transfers between devices with their start and end apart: 6, of which 4 were waited for; matrix products, arithmetic and copies ran while one was open for 2% of the time, Pallas kernels for 3%

profile of v1, /device:TPU:8, one launch (start us, length us, event | category | flops | bytes accessed | tf_op | source)
XLA Modules:
  0.0 111.2 jit_solution(11214675661982675730)
XLA Ops:
  0.6 0.9 reshape.31
  1.6 0.9 slice_bitcast_fusion
  2.5 14.7 %collective-permute-start = (bf16[256,256]{1,0:T(8,128)(2,1)S(1)}, bf16[256,256]{1,0:T(8,128)(2,1)S(1)}, u32[]{:S(2)}, u32[]{:S(2)}) collective-permute-start(bf16[256,256]{1,0:T(8,128)(2,1)S(1)} %pad_maximum_fusion), channel_id=1, source_target_pairs={{4,0},{8,4},{12,8},{16,12},{20,16},{24,20},{28,24},{32,28},{36,32}... | collective-permute-start | bytes 393224 | tf_op jit(solution)/shard_map/ppermute | solution.py:331
  17.2 1.9 %collective-permute-start.1 = (bf16[128,256]{1,0:T(8,128)(2,1)S(1)}, bf16[128,256]{1,0:T(8,128)(2,1)S(1)}, u32[]{:S(2)}, u32[]{:S(2)}) collective-permute-start(bf16[128,256]{1,0:T(8,128)(2,1)S(1)} %get-tuple-element.19), channel_id=1, source_target_pairs={{0,4},{4,8},{8,12},{12,16},{16,20},{20,24},{24,28},{28,32},{32,36}... | collective-permute-start | bytes 196616 | tf_op jit(solution)/shard_map/ppermute | solution.py:332
  19.2 0.9 copy.16
  20.0 0.9 reshape.33.iatm
  20.9 8.3 %collective-permute-done.1.above = bf16[128,256]{1,0:T(8,128)(2,1)S(1)} collective-permute-done((bf16[128,256]{1,0:T(8,128)(2,1)S(1)}, bf16[128,256]{1,0:T(8,128)(2,1)S(1)}, u32[]{:S(2)}, u32[]{:S(2)}) %collective-permute-start.1) | collective-permute-done | bytes 65568 | tf_op jit(solution)/shard_map/ppermute | solution.py:332
  29.8 1.8 %shard_map.121 = bf16[4,48,256]{2,1,0:T(8,128)(2,1)} custom-call(s32[2048]{0:T(1024)} %reshape.33.iatm, bf16[512,256]{1,0:T(8,128)(2,1)} %bitcast.10, bf16[256,256]{1,0:T(8,128)(2,1)} %copy-done.2, bf16[128,256]{1,0:T(8,128)(2,1)} %copy-done.5, bf16[128,256]{1,0:T(8,128)(2,1)} %bitcast.15), custom_call_target="tpu_custom_call" | custom-call | tf_op jit(solution)/shard_map/pallas_call | solution.py:333
  31.7 4.3 %all-to-all-start = ((bf16[4,48,256]{2,1,0:T(8,128)(2,1)}), bf16[4,48,256]{2,1,0:T(8,128)(2,1)S(1)}, u32[]{:S(2)}, u32[]{:S(2)}) async-start(bf16[4,48,256]{2,1,0:T(8,128)(2,1)} %shard_map.121), calls=%async_computation | async-start | bytes 196608 | tf_op jit(solution)/shard_map/all_to_all | solution.py:336
  36.8 0.9 reshape.29.ioff
  37.7 4.1 %all-to-all-done.arrived = bf16[4,48,256]{2,1,0:T(8,128)(2,1)S(1)} async-done(((bf16[4,48,256]{2,1,0:T(8,128)(2,1)}), bf16[4,48,256]{2,1,0:T(8,128)(2,1)S(1)}, u32[]{:S(2)}, u32[]{:S(2)}) %all-to-all-start) | async-done | bytes 98336 | tf_op jit(solution)/shard_map/all_to_all | solution.py:336
  42.4 6.0 %shard_map.122 = (bf16[512,256]{1,0:T(8,128)(2,1)}, bf16[1424,256]{1,0:T(8,128)(2,1)}, f32[1288,256]{1,0:T(8,128)}, bf16[128,256]{1,0:T(8,128)(2,1)}) custom-call(s32[2048]{0:T(1024)} %reshape.29.ioff, s32[1,1]{1,0:T(1,128)S(6)} %copy.17.wet, bf16[512,256]{1,0:T(8,128)(2,1)} %bitcast.11, bf16[256,256]{1,0:T(8,128)(2,1)} %copy-done.2, ...), custom_call_target="tpu_custom_call" | custom-call | tf_op jit(solution)/shard_map/pallas_call | solution.py:337
  48.5 1.9 %collective-permute-start.2 = (bf16[1424,256]{1,0:T(8,128)(2,1)}, bf16[1424,256]{1,0:T(8,128)(2,1)S(1)}, u32[]{:S(2)}, u32[]{:S(2)}) collective-permute-start(bf16[1424,256]{1,0:T(8,128)(2,1)} %get-tuple-element.13), channel_id=1, source_target_pairs={{0,4},{4,0},{1,5},{5,1},{2,6},{6,2},{3,7},{7,3},{8,12},{12,8},{9,1... | collective-permute-start | bytes 2187272 | tf_op jit(solution)/shard_map/ppermute | solution.py:354
  50.4 1.9 %collective-permute-start.3 = (bf16[128,256]{1,0:T(8,128)(2,1)}, bf16[128,256]{1,0:T(8,128)(2,1)S(1)}, u32[]{:S(2)}, u32[]{:S(2)}) collective-permute-start(bf16[128,256]{1,0:T(8,128)(2,1)} %get-tuple-element.14), channel_id=1, source_target_pairs={{0,124},{4,8},{8,4},{12,16},{16,12},{20,24},{24,20},{28,32},{32,28... | collective-permute-start | bytes 196616 | tf_op jit(solution)/shard_map/ppermute | solution.py:353
  52.3 9.9 %collective-permute-done.3.zrow = bf16[128,256]{1,0:T(8,128)(2,1)S(1)} collective-permute-done((bf16[128,256]{1,0:T(8,128)(2,1)}, bf16[128,256]{1,0:T(8,128)(2,1)S(1)}, u32[]{:S(2)}, u32[]{:S(2)}) %collective-permute-start.3) | collective-permute-done | bytes 65568 | tf_op jit(solution)/shard_map/ppermute | solution.py:353
  63.1 2.8 %shard_map.123 = (bf16[4,336,256]{2,1,0:T(8,128)(2,1)}, bf16[256,256]{1,0:T(8,128)(2,1)}) custom-call(f32[1288,256]{1,0:T(8,128)} %get-tuple-element.12.keep, bf16[1424,256]{1,0:T(8,128)(2,1)} %copy-done, bf16[128,256]{1,0:T(8,128)(2,1)} %copy-done.6, bf16[512,256]{1,0:T(8,128)(2,1)} %get-tuple-element.11.hg), custom_call_target="tpu_custom_call" | custom-call | tf_op jit(solution)/shard_map/pallas_call | solution.py:355
  65.9 13.2 %all_to_all.20.arrived.got = bf16[4,336,256]{2,1,0:T(8,128)(2,1)} all-to-all(bf16[4,336,256]{2,1,0:T(8,128)(2,1)} %get-tuple-element.16), channel_id=1, replica_groups=mesh['ens'=4,'yh'=2,'z'=8,'core'=2,'ox'=4] {'ox'}, dimensions={0} | all-to-all | bytes 1376256 | tf_op jit(solution)/shard_map/all_to_all | solution.py:361
  79.0 1.9 %shard_map.125 = bf16[8,48,256]{2,1,0:T(8,128)(2,1)} custom-call(bf16[4,336,256]{2,1,0:T(8,128)(2,1)} %all_to_all.20.arrived.got), custom_call_target="tpu_custom_call" | custom-call | tf_op jit(solution)/shard_map/pallas_call | solution.py:362
  80.9 13.8 %all_to_all.21.got = bf16[8,48,256]{2,1,0:T(8,128)(2,1)} all-to-all(bf16[8,48,256]{2,1,0:T(8,128)(2,1)} %shard_map.125), channel_id=1, replica_groups=mesh['ens'=4,'yh'=2,'z'=8,'core'=2,'ox'=4] {'z'}, dimensions={0} | all-to-all | bytes 393216 | tf_op jit(solution)/shard_map/all_to_all | solution.py:363
  94.7 1.6 %shard_map.126 = bf16[8,32,256]{2,1,0:T(8,128)(2,1)} custom-call(bf16[8,48,256]{2,1,0:T(8,128)(2,1)} %all_to_all.21.got), custom_call_target="tpu_custom_call" | custom-call | tf_op jit(solution)/shard_map/pallas_call | solution.py:364
  96.3 5.3 %all-to-all-start.3 = ((bf16[8,32,256]{2,1,0:T(8,128)(2,1)}), bf16[8,32,256]{2,1,0:T(8,128)(2,1)S(1)}, u32[]{:S(2)}, u32[]{:S(2)}) async-start(bf16[8,32,256]{2,1,0:T(8,128)(2,1)} %shard_map.126), calls=%async_computation.3 | async-start | bytes 262144 | tf_op jit(solution)/shard_map/all_to_all | solution.py:365
  101.6 3.2 %shard_map.124 = bf16[512,256]{1,0:T(8,128)(2,1)} custom-call(bf16[512,256]{1,0:T(8,128)(2,1)} %get-tuple-element.11.hg, bf16[256,256]{1,0:T(8,128)(2,1)} %get-tuple-element.15.rows, bf16[4,336,256]{2,1,0:T(8,128)(2,1)} %all_to_all.20.arrived.got, bf16[512,256]{1,0:T(8,128)(2,1)} %bitcast.13, bf16[9,256,256]{2,1,0:T(8,128)(2,1)} %conv.3), custom_call_target="tpu_custom_call" | custom-call | tf_op jit(solution)/shard_map/pallas_call | solution.py:369
  104.9 4.2 %all-to-all-done.3.got = bf16[8,32,256]{2,1,0:T(8,128)(2,1)S(1)} async-done(((bf16[8,32,256]{2,1,0:T(8,128)(2,1)}), bf16[8,32,256]{2,1,0:T(8,128)(2,1)S(1)}, u32[]{:S(2)}, u32[]{:S(2)}) %all-to-all-start.3) | async-done | bytes 131104 | tf_op jit(solution)/shard_map/all_to_all | solution.py:365
  109.7 1.5 %shard_map.127 = (f32[20,256]{1,0:T(8,128)}, f32[4,256]{1,0:T(4,128)}) custom-call(bf16[8,32,256]{2,1,0:T(8,128)(2,1)} %copy-done.3), custom_call_target="tpu_custom_call" | custom-call | tf_op jit(solution)/shard_map/pallas_call | solution.py:366
  (21 shorter events, 3.0 us)
Async XLA Ops:
  0.6 36.0 %copy-start.7 = (s32[128,4,4]{0,2,1:T(4,128)S(1)}, s32[128,4,4]{0,2,1:T(4,128)}, u32[]{:S(2)}) copy-start(s32[128,4,4]{0,2,1:T(4,128)} %param.18) | copy-start | bytes 24580
  1.6 27.6 %copy-start.1 = (bf16[64,2,256]{2,0,1:T(8,128)(2,1)}, bf16[64,2,256]{2,0,1:T(8,128)(2,1)S(1)}, u32[]{:S(2)}) copy-start(bf16[64,2,256]{2,0,1:T(8,128)(2,1)S(1)} %copy.15) | copy-start | bytes 196612
  2.5 26.7 %collective-permute-start = (bf16[256,256]{1,0:T(8,128)(2,1)S(1)}, bf16[256,256]{1,0:T(8,128)(2,1)S(1)}, u32[]{:S(2)}, u32[]{:S(2)}) collective-permute-start(bf16[256,256]{1,0:T(8,128)(2,1)S(1)} %pad_maximum_fusion), channel_id=1, source_target_pairs={{4,0},{8,4},{12,8},{16,12},{20,16},{24,20},{28,24},{32,28},{36,32}... | collective-permute-start | bytes 393224 | tf_op jit(solution)/shard_map/ppermute | solution.py:331
  17.2 11.9 %collective-permute-start.1 = (bf16[128,256]{1,0:T(8,128)(2,1)S(1)}, bf16[128,256]{1,0:T(8,128)(2,1)S(1)}, u32[]{:S(2)}, u32[]{:S(2)}) collective-permute-start(bf16[128,256]{1,0:T(8,128)(2,1)S(1)} %get-tuple-element.19), channel_id=1, source_target_pairs={{0,4},{4,8},{8,12},{12,16},{16,20},{20,24},{24,28},{28,32},{32,36}... | collective-permute-start | bytes 196616 | tf_op jit(solution)/shard_map/ppermute | solution.py:332
  29.2 0.6 copy-start.5
  29.2 0.7 copy-start.2
  31.7 10.1 %all-to-all-start = ((bf16[4,48,256]{2,1,0:T(8,128)(2,1)}), bf16[4,48,256]{2,1,0:T(8,128)(2,1)S(1)}, u32[]{:S(2)}, u32[]{:S(2)}) async-start(bf16[4,48,256]{2,1,0:T(8,128)(2,1)} %shard_map.121), calls=%async_computation | async-start | bytes 196608 | tf_op jit(solution)/shard_map/all_to_all | solution.py:336
  41.8 0.6 copy-start.4
  48.5 13.7 %collective-permute-start.2 = (bf16[1424,256]{1,0:T(8,128)(2,1)}, bf16[1424,256]{1,0:T(8,128)(2,1)S(1)}, u32[]{:S(2)}, u32[]{:S(2)}) collective-permute-start(bf16[1424,256]{1,0:T(8,128)(2,1)} %get-tuple-element.13), channel_id=1, source_target_pairs={{0,4},{4,0},{1,5},{5,1},{2,6},{6,2},{3,7},{7,3},{8,12},{12,8},{9,1... | collective-permute-start | bytes 2187272 | tf_op jit(solution)/shard_map/ppermute | solution.py:354
  50.4 11.8 %collective-permute-start.3 = (bf16[128,256]{1,0:T(8,128)(2,1)}, bf16[128,256]{1,0:T(8,128)(2,1)S(1)}, u32[]{:S(2)}, u32[]{:S(2)}) collective-permute-start(bf16[128,256]{1,0:T(8,128)(2,1)} %get-tuple-element.14), channel_id=1, source_target_pairs={{0,124},{4,8},{8,4},{12,16},{16,12},{20,24},{24,20},{28,32},{32,28... | collective-permute-start | bytes 196616 | tf_op jit(solution)/shard_map/ppermute | solution.py:353
  62.2 0.6 copy-start.6
  62.2 0.9 copy-start
  96.3 12.8 %all-to-all-start.3 = ((bf16[8,32,256]{2,1,0:T(8,128)(2,1)}), bf16[8,32,256]{2,1,0:T(8,128)(2,1)S(1)}, u32[]{:S(2)}, u32[]{:S(2)}) async-start(bf16[8,32,256]{2,1,0:T(8,128)(2,1)} %shard_map.126), calls=%async_computation.3 | async-start | bytes 262144 | tf_op jit(solution)/shard_map/all_to_all | solution.py:365
  109.1 0.7 copy-start.3

commit v2 on v1

--- a/solution.py
+++ b/solution.py
@@ -17,6 +17,7 @@
 ENTRIES = 16
 SHARE = 20
 VM = pl.BlockSpec(memory_space=pltpu.VMEM)
+HBM = pl.BlockSpec(memory_space=pltpu.HBM)
 SM = pl.BlockSpec(memory_space=pltpu.SMEM)
 
 
@@ -25,17 +26,29 @@
 
 
 def call(kernel, outs, scratch=(), specs=None, n_in=None):
-    return pl.pallas_call(
+    specs = specs if specs is not None else [VM] * n_in
+    run = pl.pallas_call(
         kernel,
         out_shape=outs,
-        in_specs=specs if specs is not None else [VM] * n_in,
+        in_specs=specs,
         out_specs=jax.tree.map(lambda _: VM, outs),
         scratch_shapes=list(scratch),
+        compiler_params=pltpu.CompilerParams(vmem_limit_bytes=24 << 20),
     )
 
+    def placed(*args):
+        return run(
+            *[
+                pltpu.with_memory_space_constraint(a, s.memory_space) if s is not SM else a
+                for a, s in zip(args, specs)
+            ]
+        )
+
+    return placed
+
 
 def struct(shape, dtype):
-    return jax.ShapeDtypeStruct(shape, dtype)
+    return pltpu.VMEM(shape, dtype)
 
 
 def split_two(value):
@@ -48,18 +61,52 @@
     return lax.dot_general(a, b, (dims, ((), ())), preferred_element_type=F32)
 
 
-def edge_rows(mid, above, below, edge):
-    at = 0 if edge == 0 else 15
-    base = 0 if edge == 0 else CELLS - 16
-    rows = [above[base : base + 16, :].astype(F32)[at : at + 1]]
-    for r in range(ROWS):
-        rows.append(mid[r * CELLS + base : r * CELLS + base + 16, :].astype(F32)[at : at + 1])
-    rows.append(below[base : base + 16, :].astype(F32)[at : at + 1])
-    rows.append(jnp.zeros((2, CH), F32))
+def edge_cells(pieces, edge):
+    at, base = (0, 0) if edge == 0 else (15, CELLS - 16)
+    rows = []
+    for piece in pieces:
+        if piece is None:
+            rows.append(jnp.zeros((1, CH), F32))
+        else:
+            rows.append(piece[base : base + 16, :].astype(F32)[at : at + 1])
     return jnp.concatenate(rows, axis=0)
 
 
-def pack_kernel(iatm, state, below, above, flux_own, out):
+def own_rows(ref):
+    return [ref[r * CELLS : (r + 1) * CELLS, :] for r in range(ROWS)]
+
+
+def joined(ref):
+    return jnp.concatenate([ref[0:CELLS, :], ref[CELLS : 2 * CELLS, :]], axis=1)
+
+
+def first_kernel(state_in, flux_in, up, down, state, flux, planes, sems):
+    copies = [
+        pltpu.make_async_copy(state_in, state, sems.at[0]),
+        pltpu.make_async_copy(flux_in, flux, sems.at[1]),
+    ]
+    for copy in copies:
+        copy.start()
+    for copy in copies:
+        copy.wait()
+    up[0:CELLS, :] = state[0:CELLS, 0:128]
+    up[CELLS : 2 * CELLS, :] = state[0:CELLS, 128:256]
+    down[...] = state[3 * CELLS : 4 * CELLS, :]
+    for b in range(64):
+        block = flux[b].astype(F32)
+        for f in range(4):
+            planes[f * 64 + b : f * 64 + b + 1, :] = block[f : f + 1]
+    up[2 * CELLS : 4 * CELLS, :] = planes[...].astype(BF)
+
+
+def pick_kernel(iatm, ioff, *refs):
+    sources, pick, offset_out, targets, sems = refs[:5], refs[5], refs[6], refs[7:12], refs[12]
+    copies = [
+        pltpu.make_async_copy(source, target, sems.at[n])
+        for n, (source, target) in enumerate(zip(sources, targets))
+    ]
+    for copy in copies:
+        copy.start()
     oy = oy_index()
     ox = lax.axis_index("ox")
     me = (oy * NLON + ox) * 64
@@ -67,43 +114,50 @@
     row = lax.broadcasted_iota(jnp.int32, (64, 128), 0)
     lane = lax.broadcasted_iota(jnp.int32, (64, 128), 1)
     target = jnp.zeros((64, 128), jnp.int32)
-    for d in range(NLON):
-        for r in range(ROWS):
-            for k in range(4):
+    offset = jnp.zeros((64, 128), jnp.int32)
+    for r in range(ROWS):
+        for k in range(4):
+            for d in range(NLON):
                 value = iatm[((oy * ROWS + r) * NLON + d) * 4 + k]
                 target = jnp.where(row == d * 16 + r * 4 + k, value, target)
+            value = ioff[((oy * ROWS + r) * NLON + ox) * 4 + k]
+            offset = jnp.where(lax.rem(row, 16) == r * 4 + k, value, offset)
     wanted = jnp.where(lane < 64, lane + me, lane - 64 + nxt)
-    pick = jnp.where(target == wanted, 1.0, 0.0).astype(BF)
-    for h in range(2):
-        source = jnp.concatenate(
-            [flux_own[h * 64 : h * 64 + 64, :], below[128 + h * 64 : 192 + h * 64, :]], axis=0
-        )
-        got = dot(pick, source, ((1,), (0,))).astype(BF)
+    pick[...] = jnp.where(target == wanted, 1.0, 0.0).astype(BF)
+    offset_out[...] = offset
+    for copy in copies:
+        copy.wait()
+
+
+def pack_kernel(pick, state, below, above, up, out):
+    oy = oy_index()
+    ox = lax.axis_index("ox")
+    for f in range(4):
+        lo = 2 * CELLS + f * 64
+        source = jnp.concatenate([up[lo : lo + 64, :], below[lo : lo + 64, :]], axis=0)
+        got = dot(pick[...], source, ((1,), (0,))).astype(BF)
         for d in range(NLON):
-            out[d, h * 16 : h * 16 + 16, :] = got[d * 16 : d * 16 + 16]
+            to = (f % 2) * 128
+            out[d, (f // 2) * 16 : (f // 2) * 16 + 16, to : to + 128] = got[d * 16 : d * 16 + 16]
     top_keep = jnp.where(oy > 0, 1.0, 0.0)
     bottom_keep = jnp.where(oy < 31, 1.0, 0.0)
-    part = lax.broadcasted_iota(jnp.int32, (8, CH), 0)
+    part = lax.broadcasted_iota(jnp.int32, (6, CH), 0)
     keep = jnp.where(part == 0, top_keep, jnp.where(part == ROWS + 1, bottom_keep, 1.0))
-    first = edge_rows(state, above, below, 0) * keep
-    last = edge_rows(state, above, below, 1) * keep
+    pieces = [above[...]] + own_rows(state) + [joined(below)]
+    first = edge_cells(pieces, 0) * keep
+    last = edge_cells(pieces, 1) * keep
     for d in range(NLON):
         to_right = jnp.where(lax.rem(ox + 1, NLON) == d, 1.0, 0.0)
         to_left = jnp.where(lax.rem(ox + NLON - 1, NLON) == d, 1.0, 0.0)
         halo = last * to_right + first * to_left
-        out[d, 32:48, :] = jnp.concatenate([halo, jnp.zeros((8, CH), F32)], axis=0).astype(BF)
-
-
-def build_shifts(shifted, mid, above, below, left, right, top_keep, bottom_keep):
+        out[d, 32:48, :] = jnp.concatenate([halo, jnp.zeros((10, CH), F32)], axis=0).astype(BF)
+
+
+def build_shifts(shifted, pieces, left, right):
     cell = lax.broadcasted_iota(jnp.int32, (CELLS, CH), 0)
-    for r in range(ROWS + 2):
-        if r == 0:
-            value = above[0:CELLS, :].astype(F32) * top_keep
-        elif r == ROWS + 1:
-            value = below[0:CELLS, :].astype(F32) * bottom_keep
-        else:
-            value = mid[(r - 1) * CELLS : r * CELLS, :].astype(F32)
-        shifted[1, r * CELLS : (r + 1) * CELLS, :] = value.astype(BF)
+    for r, piece in enumerate(pieces):
+        value = piece.astype(F32)
+        shifted[1, r * CELLS : (r + 1) * CELLS, :] = piece.astype(BF)
         plus = jnp.where(cell == CELLS - 1, right[r : r + 1, :], pltpu.roll(value, CELLS - 1, 0))
         minus = jnp.where(cell == 0, left[r : r + 1, :], pltpu.roll(value, 1, 0))
         shifted[2, r * CELLS : (r + 1) * CELLS, :] = plus.astype(BF)
@@ -111,8 +165,8 @@
 
 
 def main_kernel(
-    ioff,
     wet,
+    offset,
     state,
     below,
     above,
@@ -138,7 +192,9 @@
     bottom_keep = jnp.where(oy < 31, 1.0, 0.0)
     left = arrived[lax.rem(ox + NLON - 1, NLON), 32:48, :].astype(F32)
     right = arrived[lax.rem(ox + 1, NLON), 32:48, :].astype(F32)
-    build_shifts(shifted, state, above, below, left, right, top_keep, bottom_keep)
+    top = above[...].astype(F32) * top_keep
+    bottom = joined(below).astype(F32) * bottom_keep
+    build_shifts(shifted, [top] + own_rows(state) + [bottom], left, right)
     for half in range(2):
         acc = jnp.zeros((256, CH), F32)
         for t in range(9):
@@ -151,16 +207,10 @@
     blocks = jnp.concatenate(
         [flux[f // 2][:, (f % 2) * 128 : (f % 2) * 128 + 128] for f in range(4)], axis=0
     ).astype(BF)
-    row = lax.broadcasted_iota(jnp.int32, (64, 128), 0)
-    offset = jnp.zeros((64, 128), jnp.int32)
-    for r in range(ROWS):
-        for k in range(4):
-            value = ioff[((oy * ROWS + r) * NLON + ox) * 4 + k]
-            offset = jnp.where(lax.rem(row, 16) == r * 4 + k, value, offset)
     contribution = jnp.zeros((64, 128), F32)
     for m in range(16):
         product = dot(blocks, regrid[m], ((1,), (1,)))
-        contribution = jnp.where(offset == m, product, contribution)
+        contribution = jnp.where(offset[...] == m, product, contribution)
     contribution = contribution.astype(BF)
     out_row = lax.broadcasted_iota(jnp.int32, (16, 64), 0)
     in_row = lax.broadcasted_iota(jnp.int32, (16, 64), 1)
@@ -219,8 +269,7 @@
     zrow_out[...] = jnp.where(core == 0, first, last)
 
 
-def merge_kernel(keep, got, zrow, hg, out, rows_out, total, moved):
-    oy = oy_index()
+def merge_kernel(keep, got, hg, out, total, moved):
     ox = lax.axis_index("ox")
     core = lax.axis_index("core")
     total[...] = keep[0:1280, :] + got[0:1280, :].astype(F32)
@@ -232,16 +281,12 @@
                 moved[to : to + SHARE, :] = total[m * 80 + c * SHARE : m * 80 + c * SHARE + SHARE, :]
     flux = keep[1280:1288, :] + got[1280:1296, :].astype(F32)[0:8]
     flux_high, flux_low = split_two(flux[0:4] + flux[4:8])
-    top_keep = jnp.where(oy > 0, 1.0, 0.0)
-    bottom_keep = jnp.where(oy < 31, 1.0, 0.0)
-    inside = got[1296:1424, :].astype(F32)
-    across = zrow[...].astype(F32)
-    above = (jnp.where(core == 0, across, inside) * top_keep).astype(BF)
-    below = (jnp.where(core == 0, inside, across) * bottom_keep).astype(BF)
-    rows_out[0:CELLS, :] = above
-    rows_out[CELLS : 2 * CELLS, :] = below
-    first = edge_rows(hg, above, below, 0)
-    last = edge_rows(hg, above, below, 1)
+    inside = got[1296:1424, :]
+    pieces = [inside] + own_rows(hg) + [inside, None, None]
+    part = lax.broadcasted_iota(jnp.int32, (8, CH), 0)
+    drop = jnp.where(core == 0, 0, ROWS + 1)
+    first = jnp.where(part == drop, 0.0, edge_cells(pieces, 0))
+    last = jnp.where(part == drop, 0.0, edge_cells(pieces, 1))
     for c in range(NLON):
         to_right = jnp.where(lax.rem(ox + 1, NLON) == c, 1.0, 0.0)
         to_left = jnp.where(lax.rem(ox + NLON - 1, NLON) == c, 1.0, 0.0)
@@ -250,6 +295,24 @@
         out[c, 320:336, :] = jnp.concatenate(
             [flux_high.astype(F32), flux_low.astype(F32), halo], axis=0
         ).astype(BF)
+
+
+def side_cells(arrived):
+    ox = lax.axis_index("ox")
+    left = arrived[lax.rem(ox + NLON - 1, NLON), 320:336, :].astype(F32)[8:16]
+    right = arrived[lax.rem(ox + 1, NLON), 320:336, :].astype(F32)[8:16]
+    return left, right
+
+
+def corner_kernel(arrived, out):
+    core = lax.axis_index("core")
+    left, right = side_cells(arrived)
+    pair = jnp.where(
+        core == 0,
+        jnp.concatenate([left[1:2], right[1:2]], axis=0),
+        jnp.concatenate([left[4:5], right[4:5]], axis=0),
+    )
+    out[...] = jnp.concatenate([pair, jnp.zeros((14, CH), F32)], axis=0).astype(BF)
 
 
 def sum_flux(pieces):
@@ -293,13 +356,21 @@
     flux_out[...] = piece[24:28] + piece[28:32]
 
 
-def input_kernel(hg, rows, arrived, cot, conv, out, shifted):
-    ox = lax.axis_index("ox")
-    left = arrived[lax.rem(ox + NLON - 1, NLON), 320:336, :].astype(F32)[8:16]
-    right = arrived[lax.rem(ox + 1, NLON), 320:336, :].astype(F32)[8:16]
-    build_shifts(
-        shifted, hg, rows, rows.at[CELLS : 2 * CELLS, :], left, right, 1.0, 1.0
-    )
+def input_kernel(hg, got, across, arrived, corners, cot, conv, out, shifted):
+    oy = oy_index()
+    core = lax.axis_index("core")
+    left, right = side_cells(arrived)
+    exists = jnp.where(jnp.logical_or(oy == 0, oy == 31), 0.0, 1.0)
+    corner = corners[...].astype(F32) * exists
+    part = lax.broadcasted_iota(jnp.int32, (8, CH), 0)
+    at = jnp.where(core == 0, 0, ROWS + 1)
+    left = jnp.where(part == at, corner[0:1], left)
+    right = jnp.where(part == at, corner[1:2], right)
+    inside = got[1296:1424, :].astype(F32)
+    other = across[...].astype(F32) * exists
+    top = jnp.where(core == 0, other, inside)
+    bottom = jnp.where(core == 0, inside, other)
+    build_shifts(shifted, [top] + own_rows(hg) + [bottom], left, right)
     for half in range(2):
         acc = cot[half * 256 : half * 256 + 256, :].astype(F32)
         for t in range(9):
@@ -322,17 +393,33 @@
 ):
     state = state.reshape(ROWS * CELLS, CH)
     cot = state_cot.reshape(ROWS * CELLS, CH)
-    flux_own = (
-        flux_cot.reshape(64, 2, CH).transpose(1, 0, 2).reshape(128, CH)
-    )
     iatm = intersection_atm.reshape(-1)
     ioff = intersection_offset.reshape(-1)
-    up = jnp.concatenate([state[0:CELLS], flux_own], axis=0)
+    up, down, state = call(
+        first_kernel,
+        (
+            struct((4 * CELLS, 128), BF),
+            struct((CELLS, CH), BF),
+            struct((ROWS * CELLS, CH), BF),
+        ),
+        scratch=[
+            pltpu.VMEM((64, 4, 128), BF),
+            pltpu.VMEM((256, 128), F32),
+            pltpu.SemaphoreType.DMA((2,)),
+        ],
+        specs=[HBM] * 2,
+    )(state, flux_cot.reshape(64, 4, 128))
     below = lax.ppermute(up, OY, [((i + 1) % 32, i) for i in range(32)])
-    above = lax.ppermute(state[3 * CELLS :], OY, [(i, (i + 1) % 32) for i in range(32)])
-    packed = call(
-        pack_kernel, struct((NLON, 48, CH), BF), specs=[SM] + [VM] * 4
-    )(iatm, state, below, above, flux_own)
+    above = lax.ppermute(down, OY, [(i, (i + 1) % 32) for i in range(32)])
+    needed = (cot, conv_weight, mix_weight, flux_weight, regrid_weights)
+    pick, offset, cot, conv_weight, mix_weight, flux_weight, regrid_weights = call(
+        pick_kernel,
+        (struct((64, 128), BF), struct((64, 128), jnp.int32))
+        + tuple(struct(a.shape, a.dtype) for a in needed),
+        scratch=[pltpu.SemaphoreType.DMA((5,))],
+        specs=[SM, SM] + [HBM] * 5,
+    )(iatm, ioff, *needed)
+    packed = call(pack_kernel, struct((NLON, 48, CH), BF), n_in=5)(pick, state, below, above, up)
     arrived = lax.all_to_all(packed, "ox", 0, 0, tiled=True)
     hg, send, keep, zrow = call(
         main_kernel,
@@ -348,30 +435,33 @@
             pltpu.VMEM((512, CH), F32),
             pltpu.VMEM((2560, CH), F32),
         ],
-        specs=[SM, SM] + [VM] * 9,
-    )(ioff, wet_rows, state, below, above, arrived, cot, conv_weight, mix_weight, flux_weight, regrid_weights)
-    zgot = lax.ppermute(zrow, OY, [(i, (i - 1) % 32 if i % 2 == 0 else (i + 1) % 32) for i in range(32)])
+        specs=[SM] + [VM] * 10,
+    )(wet_rows, offset, state, below, above, arrived, cot, conv_weight, mix_weight, flux_weight, regrid_weights)
+    swap = [(i, (i - 1) % 32 if i % 2 == 0 else (i + 1) % 32) for i in range(32)]
     got = lax.ppermute(send, "core", [(0, 1), (1, 0)])
-    packed, rows = call(
+    across = lax.ppermute(zrow, OY, swap)
+    packed = call(
         merge_kernel,
-        (struct((NLON, 336, CH), BF), struct((2 * CELLS, CH), BF)),
+        struct((NLON, 336, CH), BF),
         scratch=[pltpu.VMEM((1280, CH), F32), pltpu.VMEM((1280, CH), F32)],
-        n_in=4,
-    )(keep, got, zgot, hg)
+        n_in=3,
+    )(keep, got, hg)
     by_ox = lax.all_to_all(packed, "ox", 0, 0, tiled=True)
+    corners = call(corner_kernel, struct((16, CH), BF), n_in=1)(by_ox)
+    corners = lax.ppermute(corners, OY, swap)
     packed = call(ox_sum_kernel, struct((8, 48, CH), BF), n_in=1)(by_ox)
     by_z = lax.all_to_all(packed, "z", 0, 0, tiled=True)
     packed = call(z_sum_kernel, struct((8, 32, CH), BF), n_in=1)(by_z)
     by_rest = lax.all_to_all(packed, ("ens", "yh"), 0, 0, tiled=True)
     weight_out, flux_out = call(
-        last_sum_kernel, (struct((SHARE, CH), F32), struct((4, CH), F32)), n_in=1
+        last_sum_kernel, (jax.ShapeDtypeStruct((SHARE, CH), F32), jax.ShapeDtypeStruct((4, CH), F32)), n_in=1
     )(by_rest)
     input_grad = call(
         input_kernel,
-        struct((ROWS * CELLS, CH), BF),
+        jax.ShapeDtypeStruct((ROWS * CELLS, CH), BF),
         scratch=[pltpu.VMEM((3, 768, CH), BF)],
-        n_in=5,
-    )(hg, rows, by_ox, cot, conv_weight)
+        n_in=7,
+    )(hg, got, across, by_ox, corners, cot, conv_weight)
     return (input_grad.reshape(1, ROWS, CELLS, CH), weight_out, flux_out)
 
 

time: 112 us -> 95.8 us (0.86)
  the two profiles are of different devices: /device:TPU:8 before, /device:TPU:2 now
where the time goes in v2:
time: 95.8 us; the launch traced here: 95.2 us
  starting transfers between devices  39.3 us (41%)
  blocking collectives  26.7 us (28%)
  waiting for transfers between devices  15.1 us (16%)
  Pallas kernels  10.5 us (11%)
  local copies, waits for them, and re-layouts  2.24 us (2%)
  between operations  1.39 us (1%)
    ppermute x1, starting transfers between devices, body(): below = lax.ppermute(up, OY, [((i + 1) % 32, i) for i in range(32)])  15.6 us
    all_to_all x1, blocking collectives, body(): by_ox = lax.all_to_all(packed, 'ox', 0, 0, tiled=True)  14.2 us
    all_to_all x1, blocking collectives, body(): by_z = lax.all_to_all(packed, 'z', 0, 0, tiled=True)  12.5 us
    pallas_call x10, Pallas kernels, placed(): run(*[pltpu.with_memory_space_constraint(a, s.memory_space) if s is not S...  10.5 us
    ppermute x1, starting transfers between devices, body(): corners = lax.ppermute(corners, OY, swap)  7.77 us
    ppermute x1, waiting for transfers between devices, body(): above = lax.ppermute(down, OY, [(i, (i + 1) % 32) for i in range(32)])  5.71 us
    all_to_all x1, starting transfers between devices, body(): arrived = lax.all_to_all(packed, 'ox', 0, 0, tiled=True)  4.82 us
    ppermute x1, starting transfers between devices, body(): across = lax.ppermute(zrow, OY, swap)  3.81 us
  transfers between devices with their start and end apart: 7, of which 4 were waited for; matrix products, arithmetic and copies ran while one was open for 2% of the time, Pallas kernels for 4%

profile of v2, /device:TPU:2, one launch (start us, length us, event | category | flops | bytes accessed | tf_op | source)
XLA Modules:
  0.0 95.2 jit_solution(8056893511300332026)
XLA Ops:
  0.6 1.1 %shard_map.122 = (bf16[512,128]{1,0:T(8,128)(2,1)S(1)}, bf16[128,256]{1,0:T(8,128)(2,1)S(1)}, bf16[512,256]{1,0:T(8,128)(2,1)S(1)}) custom-call(bf16[512,256]{1,0:T(8,128)(2,1)} %bitcast.5, bf16[64,4,128]{2,1,0:T(4,128)(2,1)} %bitcast.7), custom_call_target="tpu_custom_call" | custom-call | tf_op jit(solution)/shard_map/pallas_call | solution.py:40
  1.7 15.6 %collective-permute-start = (bf16[512,128]{1,0:T(8,128)(2,1)S(1)}, bf16[512,128]{1,0:T(8,128)(2,1)S(1)}, u32[]{:S(2)}, u32[]{:S(2)}) collective-permute-start(bf16[512,128]{1,0:T(8,128)(2,1)S(1)} %get-tuple-element.21.up), channel_id=1, source_target_pairs={{4,0},{8,4},{12,8},{16,12},{20,16},{24,20},{28,24},{32,28},{36,32}... | collective-permute-start | bytes 393224 | tf_op jit(solution)/shard_map/ppermute | solution.py:412
  17.4 1.9 %collective-permute-start.1 = (bf16[128,256]{1,0:T(8,128)(2,1)S(1)}, bf16[128,256]{1,0:T(8,128)(2,1)S(1)}, u32[]{:S(2)}, u32[]{:S(2)}) collective-permute-start(bf16[128,256]{1,0:T(8,128)(2,1)S(1)} %get-tuple-element.22), channel_id=1, source_target_pairs={{0,4},{4,8},{8,12},{12,16},{16,20},{20,24},{24,28},{28,32},{32,36}... | collective-permute-start | bytes 196616 | tf_op jit(solution)/shard_map/ppermute | solution.py:413
  19.3 0.9 copy.13
  20.4 0.9 copy.14
  21.3 0.3 reshape.25.ioff
  21.6 2.4 %shard_map.121 = (bf16[64,128]{1,0:T(8,128)(2,1)S(1)}, s32[64,128]{1,0:T(8,128)S(1)}, bf16[512,256]{1,0:T(8,128)(2,1)S(1)}, bf16[9,256,256]{2,1,0:T(8,128)(2,1)S...) custom-call(s32[2048]{0:T(1024)S(1)} %reshape.24.iatm, ...), custom_call_target="tpu_custom_call" | custom-call | tf_op jit(solution)/shard_map/pallas_call | solution.py:40
  23.9 5.7 %collective-permute-done.1.above = bf16[128,256]{1,0:T(8,128)(2,1)S(1)} collective-permute-done((bf16[128,256]{1,0:T(8,128)(2,1)S(1)}, bf16[128,256]{1,0:T(8,128)(2,1)S(1)}, u32[]{:S(2)}, u32[]{:S(2)}) %collective-permute-start.1) | collective-permute-done | bytes 65568 | tf_op jit(solution)/shard_map/ppermute | solution.py:413
  29.7 0.8 shard_map.123
  30.5 4.8 %all-to-all-start = ((bf16[4,48,256]{2,1,0:T(8,128)(2,1)}), bf16[4,48,256]{2,1,0:T(8,128)(2,1)S(1)}, u32[]{:S(2)}, u32[]{:S(2)}) async-start(bf16[4,48,256]{2,1,0:T(8,128)(2,1)} %shard_map.123), calls=%async_computation | async-start | bytes 196608 | tf_op jit(solution)/shard_map/all_to_all | solution.py:423
  35.9 3.7 %all-to-all-done.arrived = bf16[4,48,256]{2,1,0:T(8,128)(2,1)S(1)} async-done(((bf16[4,48,256]{2,1,0:T(8,128)(2,1)}), bf16[4,48,256]{2,1,0:T(8,128)(2,1)S(1)}, u32[]{:S(2)}, u32[]{:S(2)}) %all-to-all-start) | async-done | bytes 98336 | tf_op jit(solution)/shard_map/all_to_all | solution.py:423
  39.6 2.9 %shard_map.124 = (bf16[512,256]{1,0:T(8,128)(2,1)S(1)}, bf16[1424,256]{1,0:T(8,128)(2,1)S(1)}, f32[1288,256]{1,0:T(8,128)S(1)}, bf16[128,256]{1,0:T(8,128)(2,1)S(1)}) custom-call(s32[1,1]{1,0:T(1,128)S(6)} %copy.15.wet, s32[64,128]{1,0:T(8,128)S(1)} %get-tuple-element.19.offset, bf16[512,256]{1,0:T(8,128)(2,1)S(1)} %get-tuple-element.20.state, ...), custom_call_target="tpu_custom_call" | custom-call | tf_op jit(solution)/shard_map/pallas_call | solution.py:40
  42.6 1.9 %collective-permute-start.2 = (bf16[1424,256]{1,0:T(8,128)(2,1)S(1)}, bf16[1424,256]{1,0:T(8,128)(2,1)S(1)}, u32[]{:S(2)}, u32[]{:S(2)}) collective-permute-start(bf16[1424,256]{1,0:T(8,128)(2,1)S(1)} %get-tuple-element.30), channel_id=1, source_target_pairs={{0,4},{4,0},{1,5},{5,1},{2,6},{6,2},{3,7},{7,3},{8,12},{12,8},{9,1... | collective-permute-start | bytes 2187272 | tf_op jit(solution)/shard_map/ppermute | solution.py:441
  44.5 2.2 %collective-permute-done.2.got = bf16[1424,256]{1,0:T(8,128)(2,1)S(1)} collective-permute-done((bf16[1424,256]{1,0:T(8,128)(2,1)S(1)}, bf16[1424,256]{1,0:T(8,128)(2,1)S(1)}, u32[]{:S(2)}, u32[]{:S(2)}) %collective-permute-start.2) | collective-permute-done | bytes 729120 | tf_op jit(solution)/shard_map/ppermute | solution.py:441
  46.7 0.3 shard_map.125
  47.0 14.2 %all_to_all.20.arrived.got = bf16[4,336,256]{2,1,0:T(8,128)(2,1)S(1)} all-to-all(bf16[4,336,256]{2,1,0:T(8,128)(2,1)S(1)} %shard_map.125), channel_id=1, replica_groups=mesh['ens'=4,'yh'=2,'z'=8,'core'=2,'ox'=4] {'ox'}, dimensions={0} | all-to-all | bytes 1376256 | tf_op jit(solution)/shard_map/all_to_all | solution.py:449
  61.3 12.5 %all_to_all.21.got = bf16[8,48,256]{2,1,0:T(8,128)(2,1)S(1)} all-to-all(bf16[8,48,256]{2,1,0:T(8,128)(2,1)S(1)} %shard_map.128), channel_id=1, replica_groups=mesh['ens'=4,'yh'=2,'z'=8,'core'=2,'ox'=4] {'z'}, dimensions={0} | all-to-all | bytes 393216 | tf_op jit(solution)/shard_map/all_to_all | solution.py:453
  73.8 0.7 shard_map.129
  74.5 3.4 %all-to-all-start.3 = ((bf16[8,32,256]{2,1,0:T(8,128)(2,1)}), bf16[8,32,256]{2,1,0:T(8,128)(2,1)S(1)}, u32[]{:S(2)}, u32[]{:S(2)}) async-start(bf16[8,32,256]{2,1,0:T(8,128)(2,1)} %shard_map.129), calls=%async_computation.3 | async-start | bytes 262144 | tf_op jit(solution)/shard_map/all_to_all | solution.py:455
  77.9 3.8 %collective-permute-start.3 = (bf16[128,256]{1,0:T(8,128)(2,1)S(1)}, bf16[128,256]{1,0:T(8,128)(2,1)S(1)}, u32[]{:S(2)}, u32[]{:S(2)}) collective-permute-start(bf16[128,256]{1,0:T(8,128)(2,1)S(1)} %get-tuple-element.31), channel_id=1, source_target_pairs={{0,124},{4,8},{8,4},{12,16},{16,12},{20,24},{24,20},{28,32},{32,28... | collective-permute-start | bytes 196616 | tf_op jit(solution)/shard_map/ppermute | solution.py:442
  81.7 7.8 %collective-permute-start.4 = (bf16[16,256]{1,0:T(8,128)(2,1)S(1)}, bf16[16,256]{1,0:T(8,128)(2,1)S(1)}, u32[]{:S(2)}, u32[]{:S(2)}) collective-permute-start(bf16[16,256]{1,0:T(8,128)(2,1)S(1)} %shard_map.126), channel_id=1, source_target_pairs={{0,124},{4,8},{8,4},{12,16},{16,12},{20,24},{24,20},{28,32},{32,28... | collective-permute-start | bytes 24584 | tf_op jit(solution)/shard_map/ppermute | solution.py:451
  89.5 3.5 %collective-permute-done.4.corners = bf16[16,256]{1,0:T(8,128)(2,1)S(1)} collective-permute-done((bf16[16,256]{1,0:T(8,128)(2,1)S(1)}, bf16[16,256]{1,0:T(8,128)(2,1)S(1)}, u32[]{:S(2)}, u32[]{:S(2)}) %collective-permute-start.4) | collective-permute-done | bytes 8224 | tf_op jit(solution)/shard_map/ppermute | solution.py:451
  93.0 1.5 %shard_map.127 = bf16[512,256]{1,0:T(8,128)(2,1)} custom-call(bf16[512,256]{1,0:T(8,128)(2,1)S(1)} %get-tuple-element.29.hg, bf16[1424,256]{1,0:T(8,128)(2,1)S(1)} %collective-permute-done.2.got, bf16[128,256]{1,0:T(8,128)(2,1)S(1)} %collective-permute-done.3.across, bf16[4,336,256]{2,1,0:T(8,128)(2,1)S(1)} %all_to_all.20.arrived.got, ...), custom_call_target="tpu_custom_call" | custom-call | tf_op jit(solution)/shard_map/pallas_call | solution.py:40
  94.6 0.6 shard_map.130
  (6 shorter events, 0.4 us)
Async XLA Ops:
  1.7 27.9 %collective-permute-start = (bf16[512,128]{1,0:T(8,128)(2,1)S(1)}, bf16[512,128]{1,0:T(8,128)(2,1)S(1)}, u32[]{:S(2)}, u32[]{:S(2)}) collective-permute-start(bf16[512,128]{1,0:T(8,128)(2,1)S(1)} %get-tuple-element.21.up), channel_id=1, source_target_pairs={{4,0},{8,4},{12,8},{16,12},{20,16},{24,20},{28,24},{32,28},{36,32}... | collective-permute-start | bytes 393224 | tf_op jit(solution)/shard_map/ppermute | solution.py:412
  17.4 12.3 %collective-permute-start.1 = (bf16[128,256]{1,0:T(8,128)(2,1)S(1)}, bf16[128,256]{1,0:T(8,128)(2,1)S(1)}, u32[]{:S(2)}, u32[]{:S(2)}) collective-permute-start(bf16[128,256]{1,0:T(8,128)(2,1)S(1)} %get-tuple-element.22), channel_id=1, source_target_pairs={{0,4},{4,8},{8,12},{12,16},{16,20},{20,24},{24,28},{28,32},{32,36}... | collective-permute-start | bytes 196616 | tf_op jit(solution)/shard_map/ppermute | solution.py:413
  30.5 9.2 %all-to-all-start = ((bf16[4,48,256]{2,1,0:T(8,128)(2,1)}), bf16[4,48,256]{2,1,0:T(8,128)(2,1)S(1)}, u32[]{:S(2)}, u32[]{:S(2)}) async-start(bf16[4,48,256]{2,1,0:T(8,128)(2,1)} %shard_map.123), calls=%async_computation | async-start | bytes 196608 | tf_op jit(solution)/shard_map/all_to_all | solution.py:423
  42.6 4.1 %collective-permute-start.2 = (bf16[1424,256]{1,0:T(8,128)(2,1)S(1)}, bf16[1424,256]{1,0:T(8,128)(2,1)S(1)}, u32[]{:S(2)}, u32[]{:S(2)}) collective-permute-start(bf16[1424,256]{1,0:T(8,128)(2,1)S(1)} %get-tuple-element.30), channel_id=1, source_target_pairs={{0,4},{4,0},{1,5},{5,1},{2,6},{6,2},{3,7},{7,3},{8,12},{12,8},{9,1... | collective-permute-start | bytes 2187272 | tf_op jit(solution)/shard_map/ppermute | solution.py:441
  74.5 20.1 %all-to-all-start.3 = ((bf16[8,32,256]{2,1,0:T(8,128)(2,1)}), bf16[8,32,256]{2,1,0:T(8,128)(2,1)S(1)}, u32[]{:S(2)}, u32[]{:S(2)}) async-start(bf16[8,32,256]{2,1,0:T(8,128)(2,1)} %shard_map.129), calls=%async_computation.3 | async-start | bytes 262144 | tf_op jit(solution)/shard_map/all_to_all | solution.py:455
  77.9 11.6 %collective-permute-start.3 = (bf16[128,256]{1,0:T(8,128)(2,1)S(1)}, bf16[128,256]{1,0:T(8,128)(2,1)S(1)}, u32[]{:S(2)}, u32[]{:S(2)}) collective-permute-start(bf16[128,256]{1,0:T(8,128)(2,1)S(1)} %get-tuple-element.31), channel_id=1, source_target_pairs={{0,124},{4,8},{8,4},{12,16},{16,12},{20,24},{24,20},{28,32},{32,28... | collective-permute-start | bytes 196616 | tf_op jit(solution)/shard_map/ppermute | solution.py:442
  81.7 11.3 %collective-permute-start.4 = (bf16[16,256]{1,0:T(8,128)(2,1)S(1)}, bf16[16,256]{1,0:T(8,128)(2,1)S(1)}, u32[]{:S(2)}, u32[]{:S(2)}) collective-permute-start(bf16[16,256]{1,0:T(8,128)(2,1)S(1)} %shard_map.126), channel_id=1, source_target_pairs={{0,124},{4,8},{8,4},{12,16},{16,12},{20,24},{24,20},{28,32},{32,28... | collective-permute-start | bytes 24584 | tf_op jit(solution)/shard_map/ppermute | solution.py:451

commit v3 on v2

--- a/solution.py
+++ b/solution.py
@@ -1,5 +1,3 @@
-import math
-
 import jax
 import jax.numpy as jnp
 from jax import lax
@@ -7,14 +5,15 @@
 from jax.experimental.pallas import tpu as pltpu
 from jax.sharding import Mesh, PartitionSpec as P
 
+
 BF = jnp.bfloat16
 F32 = jnp.float32
 OY = ("yh", "z", "core")
+SWAP = [(i, (i - 1) % 32 if i % 2 == 0 else (i + 1) % 32) for i in range(32)]
 ROWS = 4
 CELLS = 128
 CH = 256
 NLON = 4
-ENTRIES = 16
 SHARE = 20
 VM = pl.BlockSpec(memory_space=pltpu.VMEM)
 HBM = pl.BlockSpec(memory_space=pltpu.HBM)
@@ -80,6 +79,16 @@
     return jnp.concatenate([ref[0:CELLS, :], ref[CELLS : 2 * CELLS, :]], axis=1)
 
 
+def halo_rows(outer, inner):
+    oy = oy_index()
+    core = lax.axis_index("core")
+    exists = jnp.where(jnp.logical_or(oy == 0, oy == 31), 0.0, 1.0)
+    across, inside = joined(outer).astype(F32) * exists, joined(inner).astype(F32)
+    top = jnp.where(core == 0, across, inside)
+    bottom = jnp.where(core == 0, inside, across)
+    return top.astype(BF), bottom.astype(BF)
+
+
 def first_kernel(state_in, flux_in, up, down, state, flux, planes, sems):
     copies = [
         pltpu.make_async_copy(state_in, state, sems.at[0]),
@@ -89,18 +98,25 @@
         copy.start()
     for copy in copies:
         copy.wait()
-    up[0:CELLS, :] = state[0:CELLS, 0:128]
-    up[CELLS : 2 * CELLS, :] = state[0:CELLS, 128:256]
-    down[...] = state[3 * CELLS : 4 * CELLS, :]
+    core = lax.axis_index("core")
+    first, last = state[0:CELLS, :], state[3 * CELLS : 4 * CELLS, :]
+    outer = jnp.where(core == 0, first, last)
+    inner = jnp.where(core == 0, last, first)
+    for pay, rows in ((up, outer), (down, inner)):
+        pay[0:CELLS, :] = rows[:, 0:128]
+        pay[CELLS : 2 * CELLS, :] = rows[:, 128:256]
     for b in range(64):
         block = flux[b].astype(F32)
         for f in range(4):
             planes[f * 64 + b : f * 64 + b + 1, :] = block[f : f + 1]
-    up[2 * CELLS : 4 * CELLS, :] = planes[...].astype(BF)
-
-
-def pick_kernel(iatm, ioff, *refs):
-    sources, pick, offset_out, targets, sems = refs[:5], refs[5], refs[6], refs[7:12], refs[12]
+    packed = planes[...].astype(BF)
+    up[2 * CELLS : 4 * CELLS, :] = packed
+    down[2 * CELLS : 4 * CELLS, :] = packed
+
+
+def pick_kernel(iatm, ioff, wet, *refs):
+    sources, pick, offset_out, gather_out = refs[:5], refs[5], refs[6], refs[7]
+    targets, sems = refs[8:13], refs[13]
     copies = [
         pltpu.make_async_copy(source, target, sems.at[n])
         for n, (source, target) in enumerate(zip(sources, targets))
@@ -118,34 +134,40 @@
     for r in range(ROWS):
         for k in range(4):
             for d in range(NLON):
-                value = iatm[((oy * ROWS + r) * NLON + d) * 4 + k]
+                value = iatm[d, k, oy * ROWS + r]
                 target = jnp.where(row == d * 16 + r * 4 + k, value, target)
-            value = ioff[((oy * ROWS + r) * NLON + ox) * 4 + k]
+            value = ioff[ox, k, oy * ROWS + r]
             offset = jnp.where(lax.rem(row, 16) == r * 4 + k, value, offset)
     wanted = jnp.where(lane < 64, lane + me, lane - 64 + nxt)
     pick[...] = jnp.where(target == wanted, 1.0, 0.0).astype(BF)
     offset_out[...] = offset
+    out_row = lax.broadcasted_iota(jnp.int32, (16, 64), 0)
+    in_row = lax.broadcasted_iota(jnp.int32, (16, 64), 1)
+    same_field = lax.rem(out_row, 4) == in_row // 16
+    same_row = out_row // 4 == lax.rem(in_row, 16) // 4
+    is_wet = out_row // 4 < wet[0, 0]
+    gather_out[...] = jnp.where(
+        jnp.logical_and(jnp.logical_and(same_field, same_row), is_wet), 1.0, 0.0
+    ).astype(BF)
     for copy in copies:
         copy.wait()
 
 
-def pack_kernel(pick, state, below, above, up, out):
-    oy = oy_index()
+def pack_kernel(pick, state, outer, inner, up, out):
     ox = lax.axis_index("ox")
+    core = lax.axis_index("core")
     for f in range(4):
         lo = 2 * CELLS + f * 64
-        source = jnp.concatenate([up[lo : lo + 64, :], below[lo : lo + 64, :]], axis=0)
+        following = jnp.where(core == 0, inner[lo : lo + 64, :], outer[lo : lo + 64, :])
+        source = jnp.concatenate([up[lo : lo + 64, :], following], axis=0)
         got = dot(pick[...], source, ((1,), (0,))).astype(BF)
         for d in range(NLON):
             to = (f % 2) * 128
             out[d, (f // 2) * 16 : (f // 2) * 16 + 16, to : to + 128] = got[d * 16 : d * 16 + 16]
-    top_keep = jnp.where(oy > 0, 1.0, 0.0)
-    bottom_keep = jnp.where(oy < 31, 1.0, 0.0)
-    part = lax.broadcasted_iota(jnp.int32, (6, CH), 0)
-    keep = jnp.where(part == 0, top_keep, jnp.where(part == ROWS + 1, bottom_keep, 1.0))
-    pieces = [above[...]] + own_rows(state) + [joined(below)]
-    first = edge_cells(pieces, 0) * keep
-    last = edge_cells(pieces, 1) * keep
+    top, bottom = halo_rows(outer, inner)
+    pieces = [top] + own_rows(state) + [bottom]
+    first = edge_cells(pieces, 0)
+    last = edge_cells(pieces, 1)
     for d in range(NLON):
         to_right = jnp.where(lax.rem(ox + 1, NLON) == d, 1.0, 0.0)
         to_left = jnp.where(lax.rem(ox + NLON - 1, NLON) == d, 1.0, 0.0)
@@ -165,11 +187,11 @@
 
 
 def main_kernel(
-    wet,
+    gather,
     offset,
     state,
-    below,
-    above,
+    outer,
+    inner,
     arrived,
     cot,
     conv,
@@ -179,21 +201,16 @@
     hg_out,
     send_out,
     keep_out,
-    zrow_out,
     shifted,
     turned,
     hidden,
     grads,
 ):
-    oy = oy_index()
     ox = lax.axis_index("ox")
     core = lax.axis_index("core")
-    top_keep = jnp.where(oy > 0, 1.0, 0.0)
-    bottom_keep = jnp.where(oy < 31, 1.0, 0.0)
     left = arrived[lax.rem(ox + NLON - 1, NLON), 32:48, :].astype(F32)
     right = arrived[lax.rem(ox + 1, NLON), 32:48, :].astype(F32)
-    top = above[...].astype(F32) * top_keep
-    bottom = joined(below).astype(F32) * bottom_keep
+    top, bottom = halo_rows(outer, inner)
     build_shifts(shifted, [top] + own_rows(state) + [bottom], left, right)
     for half in range(2):
         acc = jnp.zeros((256, CH), F32)
@@ -212,15 +229,7 @@
         product = dot(blocks, regrid[m], ((1,), (1,)))
         contribution = jnp.where(offset[...] == m, product, contribution)
     contribution = contribution.astype(BF)
-    out_row = lax.broadcasted_iota(jnp.int32, (16, 64), 0)
-    in_row = lax.broadcasted_iota(jnp.int32, (16, 64), 1)
-    same_field = lax.rem(out_row, 4) == in_row // 16
-    same_row = out_row // 4 == lax.rem(in_row, 16) // 4
-    is_wet = out_row // 4 < wet[0, 0]
-    gather = jnp.where(
-        jnp.logical_and(jnp.logical_and(same_field, same_row), is_wet), 1.0, 0.0
-    ).astype(BF)
-    cells = dot(gather, contribution, ((1,), (0,)))
+    cells = dot(gather[...], contribution, ((1,), (0,)))
     cells_high, cells_low = split_two(cells)
     cells_pair = jnp.concatenate([cells_high, cells_low], axis=0)
     pair_row = lax.broadcasted_iota(jnp.int32, (32, CH), 0)
@@ -266,7 +275,11 @@
     ).astype(BF)
     first, last = hg_out[0:CELLS, :], hg_out[3 * CELLS : 4 * CELLS, :]
     send_out[1296:1424, :] = jnp.where(core == 0, last, first)
-    zrow_out[...] = jnp.where(core == 0, first, last)
+
+
+def row_kernel(hg, out):
+    core = lax.axis_index("core")
+    out[...] = jnp.where(core == 0, hg[0:CELLS, :], hg[3 * CELLS : 4 * CELLS, :])
 
 
 def merge_kernel(keep, got, hg, out, total, moved):
@@ -356,27 +369,45 @@
     flux_out[...] = piece[24:28] + piece[28:32]
 
 
-def input_kernel(hg, got, across, arrived, corners, cot, conv, out, shifted):
+def spread_kernel(hg, got, across, cot, conv, out, shifted):
     oy = oy_index()
     core = lax.axis_index("core")
-    left, right = side_cells(arrived)
     exists = jnp.where(jnp.logical_or(oy == 0, oy == 31), 0.0, 1.0)
-    corner = corners[...].astype(F32) * exists
-    part = lax.broadcasted_iota(jnp.int32, (8, CH), 0)
-    at = jnp.where(core == 0, 0, ROWS + 1)
-    left = jnp.where(part == at, corner[0:1], left)
-    right = jnp.where(part == at, corner[1:2], right)
     inside = got[1296:1424, :].astype(F32)
     other = across[...].astype(F32) * exists
     top = jnp.where(core == 0, other, inside)
     bottom = jnp.where(core == 0, inside, other)
-    build_shifts(shifted, [top] + own_rows(hg) + [bottom], left, right)
+    nothing = jnp.zeros((8, CH), F32)
+    build_shifts(shifted, [top] + own_rows(hg) + [bottom], nothing, nothing)
     for half in range(2):
         acc = cot[half * 256 : half * 256 + 256, :].astype(F32)
         for t in range(9):
             start = (2 - t // 3) * CELLS + half * 256
             acc = acc + dot(shifted[2 - t % 3, start : start + 256, :], conv[t], ((1,), (1,)))
-        out[half * 256 : half * 256 + 256, :] = acc.astype(BF)
+        out[half * 256 : half * 256 + 256, :] = acc
+
+
+def input_kernel(partial, arrived, corners, conv, out):
+    oy = oy_index()
+    core = lax.axis_index("core")
+    exists = jnp.where(jnp.logical_or(oy == 0, oy == 31), 0.0, 1.0)
+    corner = corners[...].astype(F32) * exists
+    part = lax.broadcasted_iota(jnp.int32, (8, CH), 0)
+    at = jnp.where(core == 0, 0, ROWS + 1)
+    out[...] = partial[...].astype(BF)
+    slab = lax.broadcasted_iota(jnp.int32, (16, CH), 0)
+    for side, cells in enumerate(side_cells(arrived)):
+        cells = jnp.where(part == at, corner[side : side + 1], cells)
+        cells = jnp.concatenate([cells, jnp.zeros((8, CH), F32)], axis=0).astype(BF)
+        added = jnp.zeros((ROWS, CH), F32)
+        for p in (-1, 0, 1):
+            product = dot(cells, conv[3 * (p + 1) + 2 - 2 * side], ((1,), (1,)))
+            added = added + product[1 - p : 1 - p + ROWS]
+        for r in range(ROWS):
+            to = r * CELLS + side * (CELLS - 16)
+            value = partial[to : to + 16, :]
+            value = jnp.where(slab == side * 15, value + added[r : r + 1], value)
+            out[to : to + 16, :] = value.astype(BF)
 
 
 def body(
@@ -393,13 +424,11 @@
 ):
     state = state.reshape(ROWS * CELLS, CH)
     cot = state_cot.reshape(ROWS * CELLS, CH)
-    iatm = intersection_atm.reshape(-1)
-    ioff = intersection_offset.reshape(-1)
     up, down, state = call(
         first_kernel,
         (
             struct((4 * CELLS, 128), BF),
-            struct((CELLS, CH), BF),
+            struct((4 * CELLS, 128), BF),
             struct((ROWS * CELLS, CH), BF),
         ),
         scratch=[
@@ -409,25 +438,29 @@
         ],
         specs=[HBM] * 2,
     )(state, flux_cot.reshape(64, 4, 128))
-    below = lax.ppermute(up, OY, [((i + 1) % 32, i) for i in range(32)])
-    above = lax.ppermute(down, OY, [(i, (i + 1) % 32) for i in range(32)])
+    outer = lax.ppermute(up, OY, SWAP)
+    inner = lax.ppermute(down, "core", [(0, 1), (1, 0)])
     needed = (cot, conv_weight, mix_weight, flux_weight, regrid_weights)
-    pick, offset, cot, conv_weight, mix_weight, flux_weight, regrid_weights = call(
+    pick, offset, gather, cot, conv_weight, mix_weight, flux_weight, regrid_weights = call(
         pick_kernel,
-        (struct((64, 128), BF), struct((64, 128), jnp.int32))
+        (struct((64, 128), BF), struct((64, 128), jnp.int32), struct((16, 64), BF))
         + tuple(struct(a.shape, a.dtype) for a in needed),
         scratch=[pltpu.SemaphoreType.DMA((5,))],
-        specs=[SM, SM] + [HBM] * 5,
-    )(iatm, ioff, *needed)
-    packed = call(pack_kernel, struct((NLON, 48, CH), BF), n_in=5)(pick, state, below, above, up)
+        specs=[SM] * 3 + [HBM] * 5,
+    )(
+        intersection_atm.transpose(1, 2, 0),
+        intersection_offset.transpose(1, 2, 0),
+        wet_rows,
+        *needed,
+    )
+    packed = call(pack_kernel, struct((NLON, 48, CH), BF), n_in=5)(pick, state, outer, inner, up)
     arrived = lax.all_to_all(packed, "ox", 0, 0, tiled=True)
-    hg, send, keep, zrow = call(
+    hg, send, keep = call(
         main_kernel,
         (
             struct((ROWS * CELLS, CH), BF),
             struct((1424, CH), BF),
             struct((1288, CH), F32),
-            struct((CELLS, CH), BF),
         ),
         scratch=[
             pltpu.VMEM((3, 768, CH), BF),
@@ -435,11 +468,11 @@
             pltpu.VMEM((512, CH), F32),
             pltpu.VMEM((2560, CH), F32),
         ],
-        specs=[SM] + [VM] * 10,
-    )(wet_rows, offset, state, below, above, arrived, cot, conv_weight, mix_weight, flux_weight, regrid_weights)
-    swap = [(i, (i - 1) % 32 if i % 2 == 0 else (i + 1) % 32) for i in range(32)]
+        n_in=11,
+    )(gather, offset, state, outer, inner, arrived, cot, conv_weight, mix_weight, flux_weight, regrid_weights)
     got = lax.ppermute(send, "core", [(0, 1), (1, 0)])
-    across = lax.ppermute(zrow, OY, swap)
+    zrow = call(row_kernel, struct((CELLS, CH), BF), n_in=1)(hg)
+    across = lax.ppermute(zrow, OY, SWAP)
     packed = call(
         merge_kernel,
         struct((NLON, 336, CH), BF),
@@ -448,7 +481,7 @@
     )(keep, got, hg)
     by_ox = lax.all_to_all(packed, "ox", 0, 0, tiled=True)
     corners = call(corner_kernel, struct((16, CH), BF), n_in=1)(by_ox)
-    corners = lax.ppermute(corners, OY, swap)
+    corners = lax.ppermute(corners, OY, SWAP)
     packed = call(ox_sum_kernel, struct((8, 48, CH), BF), n_in=1)(by_ox)
     by_z = lax.all_to_all(packed, "z", 0, 0, tiled=True)
     packed = call(z_sum_kernel, struct((8, 32, CH), BF), n_in=1)(by_z)
@@ -456,12 +489,15 @@
     weight_out, flux_out = call(
         last_sum_kernel, (jax.ShapeDtypeStruct((SHARE, CH), F32), jax.ShapeDtypeStruct((4, CH), F32)), n_in=1
     )(by_rest)
-    input_grad = call(
-        input_kernel,
-        jax.ShapeDtypeStruct((ROWS * CELLS, CH), BF),
+    partial = call(
+        spread_kernel,
+        struct((ROWS * CELLS, CH), F32),
         scratch=[pltpu.VMEM((3, 768, CH), BF)],
-        n_in=7,
-    )(hg, got, across, by_ox, corners, cot, conv_weight)
+        n_in=5,
+    )(hg, got, across, cot, conv_weight)
+    input_grad = call(input_kernel, jax.ShapeDtypeStruct((ROWS * CELLS, CH), BF), n_in=4)(
+        partial, by_ox, corners, conv_weight
+    )
     return (input_grad.reshape(1, ROWS, CELLS, CH), weight_out, flux_out)
 
 
@@ -480,4 +516,5 @@
         P(OY, "ox"),
     )
     out_specs = (P("ens", OY, "ox", None), P(OY + ("ox",), None), P())
+
     return jax.shard_map(body, mesh=fine, in_specs=in_specs, out_specs=out_specs, check_vma=False)

time: 95.8 us -> 92.3 us (0.963)
  waiting for transfers between devices: 15.1 us -> 4.97 us
  blocking collectives: 26.7 us -> 35.7 us
  starting transfers between devices: 39.3 us -> 38.2 us
    all_to_all x0 -> x1, blocking collectives: none -> 8.97 us  [body(): arrived = lax.all_to_all(packed, 'ox', 0, 0, tiled=True)]
    ppermute x4, waiting for transfers between devices: 9.25 us -> 2.8 us  [the longest x1 2.79 us: body(): corners = lax.ppermute(corners, OY, SWAP)]
    all_to_all x1 -> x0, starting transfers between devices: 4.82 us -> none  [body(): arrived = lax.all_to_all(packed, 'ox', 0, 0, tiled=True)]
    all_to_all x1 -> x0, waiting for transfers between devices: 3.69 us -> none  [body(): arrived = lax.all_to_all(packed, 'ox', 0, 0, tiled=True)]
    all_to_all x1, starting transfers between devices: 3.37 us -> 6.43 us  [body(): by_rest = lax.all_to_all(packed, ('ens', 'yh'), 0, 0, tiled=True)]
    pallas_call x10 -> x12, Pallas kernels: 10.5 us -> 10.2 us  [placed(): run(*[pltpu.with_memory_space_constraint(a, s.memory_space) if s is not S...]
  transfers between devices with their start and end apart: 7 -> 6, of which waited for: 4 -> 2; matrix products, arithmetic and copies ran while one was open for 2% -> 0% of each run, Pallas kernels for 4% -> 5%
where the time goes in v3:
time: 92.3 us; the launch traced here: 91.7 us
  starting transfers between devices  38.2 us (41%)
  blocking collectives  35.7 us (39%)
  Pallas kernels  10.2 us (11%)
  waiting for transfers between devices  4.97 us (5%)
  between operations  1.4 us (2%)
  local copies, waits for them, and re-layouts  1.39 us (2%)
    ppermute x1, starting transfers between devices, body(): outer = lax.ppermute(up, OY, SWAP)  16.3 us
    all_to_all x1, blocking collectives, body(): by_ox = lax.all_to_all(packed, 'ox', 0, 0, tiled=True)  14.2 us
    all_to_all x1, blocking collectives, body(): by_z = lax.all_to_all(packed, 'z', 0, 0, tiled=True)  12.5 us
    pallas_call x12, Pallas kernels, placed(): run(*[pltpu.with_memory_space_constraint(a, s.memory_space) if s is not S...  10.2 us
    all_to_all x1, blocking collectives, body(): arrived = lax.all_to_all(packed, 'ox', 0, 0, tiled=True)  8.97 us
    ppermute x1, starting transfers between devices, body(): corners = lax.ppermute(corners, OY, SWAP)  7.94 us
    all_to_all x1, starting transfers between devices, body(): by_rest = lax.all_to_all(packed, ('ens', 'yh'), 0, 0, tiled=True)  6.43 us
    ppermute x1, starting transfers between devices, body(): across = lax.ppermute(zrow, OY, SWAP)  3.64 us
  transfers between devices with their start and end apart: 6, of which 2 were waited for; matrix products, arithmetic and copies ran while one was open for 0% of the time, Pallas kernels for 5%

profile of v3, /device:TPU:2, one launch (start us, length us, event | category | flops | bytes accessed | tf_op | source)
XLA Modules:
  0.0 91.7 jit_solution(16752539479429039205)
XLA Ops:
  0.6 1.1 %shard_map.122 = (bf16[512,128]{1,0:T(8,128)(2,1)S(1)}, bf16[512,128]{1,0:T(8,128)(2,1)S(1)}, bf16[512,256]{1,0:T(8,128)(2,1)S(1)}) custom-call(bf16[512,256]{1,0:T(8,128)(2,1)} %bitcast.8, bf16[64,4,128]{2,1,0:T(4,128)(2,1)} %bitcast.11), custom_call_target="tpu_custom_call" | custom-call | tf_op jit(solution)/shard_map/pallas_call | solution.py:39
  1.7 1.9 %collective-permute-start.1 = (bf16[512,128]{1,0:T(8,128)(2,1)S(1)}, bf16[512,128]{1,0:T(8,128)(2,1)S(1)}, u32[]{:S(2)}, u32[]{:S(2)}) collective-permute-start(bf16[512,128]{1,0:T(8,128)(2,1)S(1)} %get-tuple-element.23), channel_id=1, source_target_pairs={{0,4},{4,0},{1,5},{5,1},{2,6},{6,2},{3,7},{7,3},{8,12},{12,8},{9,1... | collective-permute-start | bytes 393224 | tf_op jit(solution)/shard_map/ppermute | solution.py:442
  3.6 16.3 %collective-permute-start = (bf16[512,128]{1,0:T(8,128)(2,1)S(1)}, bf16[512,128]{1,0:T(8,128)(2,1)S(1)}, u32[]{:S(2)}, u32[]{:S(2)}) collective-permute-start(bf16[512,128]{1,0:T(8,128)(2,1)S(1)} %get-tuple-element.22.up), channel_id=1, source_target_pairs={{0,124},{4,8},{8,4},{12,16},{16,12},{20,24},{24,20},{28,32},{32,28... | collective-permute-start | bytes 393224 | tf_op jit(solution)/shard_map/ppermute | solution.py:441
  20.6 0.0 copy-start
  20.6 0.7 copy-done
  21.3 0.7 copy-done.1
  22.0 2.4 %shard_map.121 = (bf16[64,128]{1,0:T(8,128)(2,1)S(1)}, s32[64,128]{1,0:T(8,128)S(1)}, bf16[16,64]{1,0:T(8,128)(2,1)S(1)}, bf16[512,256]{1,0:T(8,128)(2,1)S(1)}, ...) custom-call(s32[4,4,128]{2,1,0:T(4,128)S(1)} %bitcast.6, ...), custom_call_target="tpu_custom_call" | custom-call | tf_op jit(solution)/shard_map/pallas_call | solution.py:39
  24.4 0.2 shard_map.123
  24.6 9.0 %all_to_all.20.arrived = bf16[4,48,256]{2,1,0:T(8,128)(2,1)S(1)} all-to-all(bf16[4,48,256]{2,1,0:T(8,128)(2,1)S(1)} %shard_map.123), channel_id=1, replica_groups=mesh['ens'=4,'yh'=2,'z'=8,'core'=2,'ox'=4] {'ox'}, dimensions={0} | all-to-all | bytes 196608 | tf_op jit(solution)/shard_map/all_to_all | solution.py:457
  33.5 2.9 %shard_map.124 = (bf16[512,256]{1,0:T(8,128)(2,1)S(1)}, bf16[1424,256]{1,0:T(8,128)(2,1)S(1)}, f32[1288,256]{1,0:T(8,128)S(1)}) custom-call(bf16[16,64]{1,0:T(8,128)(2,1)S(1)} %get-tuple-element.19.gather, s32[64,128]{1,0:T(8,128)S(1)} %get-tuple-element.20.offset, bf16[512,256]{1,0:T(8,128)(2,1)S(1)} %get-tuple-element.21.state, ...), custom_call_target="tpu_custom_call" | custom-call | tf_op jit(solution)/shard_map/pallas_call | solution.py:39
  36.5 1.9 %collective-permute-start.2 = (bf16[1424,256]{1,0:T(8,128)(2,1)S(1)}, bf16[1424,256]{1,0:T(8,128)(2,1)S(1)}, u32[]{:S(2)}, u32[]{:S(2)}) collective-permute-start(bf16[1424,256]{1,0:T(8,128)(2,1)S(1)} %get-tuple-element.31), channel_id=1, source_target_pairs={{0,4},{4,0},{1,5},{5,1},{2,6},{6,2},{3,7},{7,3},{8,12},{12,8},{9,1... | collective-permute-start | bytes 2187272 | tf_op jit(solution)/shard_map/ppermute | solution.py:473
  38.4 2.2 %collective-permute-done.2.got = bf16[1424,256]{1,0:T(8,128)(2,1)S(1)} collective-permute-done((bf16[1424,256]{1,0:T(8,128)(2,1)S(1)}, bf16[1424,256]{1,0:T(8,128)(2,1)S(1)}, u32[]{:S(2)}, u32[]{:S(2)}) %collective-permute-start.2) | collective-permute-done | bytes 729120 | tf_op jit(solution)/shard_map/ppermute | solution.py:473
  40.6 0.3 shard_map.127
  40.9 14.2 %all_to_all.21.arrived.got = bf16[4,336,256]{2,1,0:T(8,128)(2,1)S(1)} all-to-all(bf16[4,336,256]{2,1,0:T(8,128)(2,1)S(1)} %shard_map.127), channel_id=1, replica_groups=mesh['ens'=4,'yh'=2,'z'=8,'core'=2,'ox'=4] {'ox'}, dimensions={0} | all-to-all | bytes 1376256 | tf_op jit(solution)/shard_map/all_to_all | solution.py:482
  55.1 0.1 shard_map.130
  55.2 12.5 %all_to_all.22.got = bf16[8,48,256]{2,1,0:T(8,128)(2,1)S(1)} all-to-all(bf16[8,48,256]{2,1,0:T(8,128)(2,1)S(1)} %shard_map.130), channel_id=1, replica_groups=mesh['ens'=4,'yh'=2,'z'=8,'core'=2,'ox'=4] {'z'}, dimensions={0} | all-to-all | bytes 393216 | tf_op jit(solution)/shard_map/all_to_all | solution.py:486
  67.7 0.7 shard_map.131
  68.4 6.4 %all-to-all-start.3 = ((bf16[8,32,256]{2,1,0:T(8,128)(2,1)}), bf16[8,32,256]{2,1,0:T(8,128)(2,1)S(1)}, u32[]{:S(2)}, u32[]{:S(2)}) async-start(bf16[8,32,256]{2,1,0:T(8,128)(2,1)} %shard_map.131), calls=%async_computation.3 | async-start | bytes 262144 | tf_op jit(solution)/shard_map/all_to_all | solution.py:488
  74.8 3.6 %collective-permute-start.3 = (bf16[128,256]{1,0:T(8,128)(2,1)S(1)}, bf16[128,256]{1,0:T(8,128)(2,1)S(1)}, u32[]{:S(2)}, u32[]{:S(2)}) collective-permute-start(bf16[128,256]{1,0:T(8,128)(2,1)S(1)} %shard_map.125), channel_id=1, source_target_pairs={{0,124},{4,8},{8,4},{12,16},{16,12},{20,24},{24,20},{28,32},{32,28... | collective-permute-start | bytes 196616 | tf_op jit(solution)/shard_map/ppermute | solution.py:475
  78.5 7.9 %collective-permute-start.4 = (bf16[16,256]{1,0:T(8,128)(2,1)S(1)}, bf16[16,256]{1,0:T(8,128)(2,1)S(1)}, u32[]{:S(2)}, u32[]{:S(2)}) collective-permute-start(bf16[16,256]{1,0:T(8,128)(2,1)S(1)} %shard_map.128), channel_id=1, source_target_pairs={{0,124},{4,8},{8,4},{12,16},{16,12},{20,24},{24,20},{28,32},{32,28... | collective-permute-start | bytes 24584 | tf_op jit(solution)/shard_map/ppermute | solution.py:484
  86.5 0.8 shard_map.126.partial
  87.3 2.8 %collective-permute-done.4.corners = bf16[16,256]{1,0:T(8,128)(2,1)S(1)} collective-permute-done((bf16[16,256]{1,0:T(8,128)(2,1)S(1)}, bf16[16,256]{1,0:T(8,128)(2,1)S(1)}, u32[]{:S(2)}, u32[]{:S(2)}) %collective-permute-start.4) | collective-permute-done | bytes 8224 | tf_op jit(solution)/shard_map/ppermute | solution.py:484
  90.1 1.0 %shard_map.129 = bf16[512,256]{1,0:T(8,128)(2,1)} custom-call(f32[512,256]{1,0:T(8,128)S(1)} %shard_map.126.partial, bf16[4,336,256]{2,1,0:T(8,128)(2,1)S(1)} %all_to_all.21.arrived.got, bf16[16,256]{1,0:T(8,128)(2,1)S(1)} %collective-permute-done.4.corners, bf16[9,256,256]{2,1,0:T(8,128)(2,1)S(1)} %get-tuple-element.26.conv), custom_call_target="tpu_custom_call" | custom-call | tf_op jit(solution)/shard_map/pallas_call | solution.py:39
  91.1 0.6 shard_map.132
  (7 shorter events, 0.0 us)
Async XLA Ops:
  1.7 22.7 %collective-permute-start.1 = (bf16[512,128]{1,0:T(8,128)(2,1)S(1)}, bf16[512,128]{1,0:T(8,128)(2,1)S(1)}, u32[]{:S(2)}, u32[]{:S(2)}) collective-permute-start(bf16[512,128]{1,0:T(8,128)(2,1)S(1)} %get-tuple-element.23), channel_id=1, source_target_pairs={{0,4},{4,0},{1,5},{5,1},{2,6},{6,2},{3,7},{7,3},{8,12},{12,8},{9,1... | collective-permute-start | bytes 393224 | tf_op jit(solution)/shard_map/ppermute | solution.py:442
  3.6 20.8 %collective-permute-start = (bf16[512,128]{1,0:T(8,128)(2,1)S(1)}, bf16[512,128]{1,0:T(8,128)(2,1)S(1)}, u32[]{:S(2)}, u32[]{:S(2)}) collective-permute-start(bf16[512,128]{1,0:T(8,128)(2,1)S(1)} %get-tuple-element.22.up), channel_id=1, source_target_pairs={{0,124},{4,8},{8,4},{12,16},{16,12},{20,24},{24,20},{28,32},{32,28... | collective-permute-start | bytes 393224 | tf_op jit(solution)/shard_map/ppermute | solution.py:441
  20.6 0.7 copy-start
  21.3 0.7 copy-start.1
  36.5 4.1 %collective-permute-start.2 = (bf16[1424,256]{1,0:T(8,128)(2,1)S(1)}, bf16[1424,256]{1,0:T(8,128)(2,1)S(1)}, u32[]{:S(2)}, u32[]{:S(2)}) collective-permute-start(bf16[1424,256]{1,0:T(8,128)(2,1)S(1)} %get-tuple-element.31), channel_id=1, source_target_pairs={{0,4},{4,0},{1,5},{5,1},{2,6},{6,2},{3,7},{7,3},{8,12},{12,8},{9,1... | collective-permute-start | bytes 2187272 | tf_op jit(solution)/shard_map/ppermute | solution.py:473
  68.4 22.7 %all-to-all-start.3 = ((bf16[8,32,256]{2,1,0:T(8,128)(2,1)}), bf16[8,32,256]{2,1,0:T(8,128)(2,1)S(1)}, u32[]{:S(2)}, u32[]{:S(2)}) async-start(bf16[8,32,256]{2,1,0:T(8,128)(2,1)} %shard_map.131), calls=%async_computation.3 | async-start | bytes 262144 | tf_op jit(solution)/shard_map/all_to_all | solution.py:488
  74.8 11.6 %collective-permute-start.3 = (bf16[128,256]{1,0:T(8,128)(2,1)S(1)}, bf16[128,256]{1,0:T(8,128)(2,1)S(1)}, u32[]{:S(2)}, u32[]{:S(2)}) collective-permute-start(bf16[128,256]{1,0:T(8,128)(2,1)S(1)} %shard_map.125), channel_id=1, source_target_pairs={{0,124},{4,8},{8,4},{12,16},{16,12},{20,24},{24,20},{28,32},{32,28... | collective-permute-start | bytes 196616 | tf_op jit(solution)/shard_map/ppermute | solution.py:475
  78.5 11.6 %collective-permute-start.4 = (bf16[16,256]{1,0:T(8,128)(2,1)S(1)}, bf16[16,256]{1,0:T(8,128)(2,1)S(1)}, u32[]{:S(2)}, u32[]{:S(2)}) collective-permute-start(bf16[16,256]{1,0:T(8,128)(2,1)S(1)} %shard_map.128), channel_id=1, source_target_pairs={{0,124},{4,8},{8,4},{12,16},{16,12},{20,24},{24,20},{28,32},{32,28... | collective-permute-start | bytes 24584 | tf_op jit(solution)/shard_map/ppermute | solution.py:484

commit v4 on v3

--- a/solution.py
+++ b/solution.py
@@ -17,6 +17,7 @@
 SHARE = 20
 VM = pl.BlockSpec(memory_space=pltpu.VMEM)
 HBM = pl.BlockSpec(memory_space=pltpu.HBM)
+ANY = pl.BlockSpec(memory_space=pl.ANY)
 SM = pl.BlockSpec(memory_space=pltpu.SMEM)
 
 
@@ -38,7 +39,7 @@
     def placed(*args):
         return run(
             *[
-                pltpu.with_memory_space_constraint(a, s.memory_space) if s is not SM else a
+                pltpu.with_memory_space_constraint(a, s.memory_space) if s not in (SM, ANY) else a
                 for a, s in zip(args, specs)
             ]
         )
@@ -114,15 +115,19 @@
     down[2 * CELLS : 4 * CELLS, :] = packed
 
 
-def pick_kernel(iatm, ioff, wet, *refs):
-    sources, pick, offset_out, gather_out = refs[:5], refs[5], refs[6], refs[7]
-    targets, sems = refs[8:13], refs[13]
+def pick_kernel(*refs):
+    sources, pick, offset_out, gather_out = refs[:8], refs[8], refs[9], refs[10]
+    sources, wet = sources[:2] + sources[3:], sources[2]
+    iatm, ioff, sems = refs[16:19]
+    targets = (iatm, ioff) + refs[11:16]
     copies = [
         pltpu.make_async_copy(source, target, sems.at[n])
         for n, (source, target) in enumerate(zip(sources, targets))
     ]
     for copy in copies:
         copy.start()
+    for copy in copies[:2]:
+        copy.wait()
     oy = oy_index()
     ox = lax.axis_index("ox")
     me = (oy * NLON + ox) * 64
@@ -149,7 +154,7 @@
     gather_out[...] = jnp.where(
         jnp.logical_and(jnp.logical_and(same_field, same_row), is_wet), 1.0, 0.0
     ).astype(BF)
-    for copy in copies:
+    for copy in copies[2:]:
         copy.wait()
 
 
@@ -282,7 +287,7 @@
     out[...] = jnp.where(core == 0, hg[0:CELLS, :], hg[3 * CELLS : 4 * CELLS, :])
 
 
-def merge_kernel(keep, got, hg, out, total, moved):
+def merge_kernel(keep, got, hg, out, padded, total, moved):
     ox = lax.axis_index("ox")
     core = lax.axis_index("core")
     total[...] = keep[0:1280, :] + got[0:1280, :].astype(F32)
@@ -295,6 +300,9 @@
     flux = keep[1280:1288, :] + got[1280:1296, :].astype(F32)[0:8]
     flux_high, flux_low = split_two(flux[0:4] + flux[4:8])
     inside = got[1296:1424, :]
+    padded[0:CELLS, :] = inside
+    padded[CELLS : 5 * CELLS, :] = hg[...]
+    padded[5 * CELLS : 6 * CELLS, :] = inside
     pieces = [inside] + own_rows(hg) + [inside, None, None]
     part = lax.broadcasted_iota(jnp.int32, (8, CH), 0)
     drop = jnp.where(core == 0, 0, ROWS + 1)
@@ -369,16 +377,17 @@
     flux_out[...] = piece[24:28] + piece[28:32]
 
 
-def spread_kernel(hg, got, across, cot, conv, out, shifted):
+def spread_kernel(padded, across, cot, conv, out, shifted):
     oy = oy_index()
     core = lax.axis_index("core")
     exists = jnp.where(jnp.logical_or(oy == 0, oy == 31), 0.0, 1.0)
-    inside = got[1296:1424, :].astype(F32)
+    inside = padded[0:CELLS, :].astype(F32)
     other = across[...].astype(F32) * exists
     top = jnp.where(core == 0, other, inside)
     bottom = jnp.where(core == 0, inside, other)
     nothing = jnp.zeros((8, CH), F32)
-    build_shifts(shifted, [top] + own_rows(hg) + [bottom], nothing, nothing)
+    own = [padded[r * CELLS : (r + 1) * CELLS, :] for r in range(1, ROWS + 1)]
+    build_shifts(shifted, [top] + own + [bottom], nothing, nothing)
     for half in range(2):
         acc = cot[half * 256 : half * 256 + 256, :].astype(F32)
         for t in range(9):
@@ -445,8 +454,12 @@
         pick_kernel,
         (struct((64, 128), BF), struct((64, 128), jnp.int32), struct((16, 64), BF))
         + tuple(struct(a.shape, a.dtype) for a in needed),
-        scratch=[pltpu.SemaphoreType.DMA((5,))],
-        specs=[SM] * 3 + [HBM] * 5,
+        scratch=[
+            pltpu.SMEM((4, 4, 128), jnp.int32),
+            pltpu.SMEM((4, 4, 128), jnp.int32),
+            pltpu.SemaphoreType.DMA((7,)),
+        ],
+        specs=[HBM] * 2 + [SM] + [HBM] * 5,
     )(
         intersection_atm.transpose(1, 2, 0),
         intersection_offset.transpose(1, 2, 0),
@@ -473,9 +486,9 @@
     got = lax.ppermute(send, "core", [(0, 1), (1, 0)])
     zrow = call(row_kernel, struct((CELLS, CH), BF), n_in=1)(hg)
     across = lax.ppermute(zrow, OY, SWAP)
-    packed = call(
+    packed, padded = call(
         merge_kernel,
-        struct((NLON, 336, CH), BF),
+        (struct((NLON, 336, CH), BF), struct((768, CH), BF)),
         scratch=[pltpu.VMEM((1280, CH), F32), pltpu.VMEM((1280, CH), F32)],
         n_in=3,
     )(keep, got, hg)
@@ -493,8 +506,8 @@
         spread_kernel,
         struct((ROWS * CELLS, CH), F32),
         scratch=[pltpu.VMEM((3, 768, CH), BF)],
-        n_in=5,
-    )(hg, got, across, cot, conv_weight)
+        n_in=4,
+    )(padded, across, cot, conv_weight)
     input_grad = call(input_kernel, jax.ShapeDtypeStruct((ROWS * CELLS, CH), BF), n_in=4)(
         partial, by_ox, corners, conv_weight
     )

time: 92.3 us -> 92.3 us (level)
  waiting for transfers between devices: 4.97 us -> 6.73 us
  local copies, waits for them, and re-layouts: 1.39 us -> 0 us
    ppermute x1, waiting for transfers between devices: 0.01 us -> 1.75 us  [body(): outer = lax.ppermute(up, OY, SWAP)]
    unnamed x4 -> x0, local copies, waits for them, and re-layouts: 1.39 us -> none
  transfers between devices with their start and end apart: 6 -> 6, of which waited for: 2 -> 3; matrix products, arithmetic and copies ran while one was open for 0% -> 0% of each run, Pallas kernels for 5% -> 4%
where the time goes in v4:
time: 92.3 us; the launch traced here: 91.7 us
  starting transfers between devices  38.6 us (42%)
  blocking collectives  35.7 us (39%)
  Pallas kernels  9.34 us (10%)
  waiting for transfers between devices  6.73 us (7%)
  between operations  1.38 us (1%)
    ppermute x1, starting transfers between devices, body(): outer = lax.ppermute(up, OY, SWAP)  16.3 us
    all_to_all x1, blocking collectives, body(): by_ox = lax.all_to_all(packed, 'ox', 0, 0, tiled=True)  14.2 us
    all_to_all x1, blocking collectives, body(): by_z = lax.all_to_all(packed, 'z', 0, 0, tiled=True)  12.5 us
    pallas_call x12, Pallas kernels, placed(): run(*[pltpu.with_memory_space_constraint(a, s.memory_space) if s not in (...  9.34 us
    all_to_all x1, blocking collectives, body(): arrived = lax.all_to_all(packed, 'ox', 0, 0, tiled=True)  8.96 us
    ppermute x1, starting transfers between devices, body(): corners = lax.ppermute(corners, OY, SWAP)  7.94 us
    all_to_all x1, starting transfers between devices, body(): by_rest = lax.all_to_all(packed, ('ens', 'yh'), 0, 0, tiled=True)  6.86 us
    ppermute x1, starting transfers between devices, body(): across = lax.ppermute(zrow, OY, SWAP)  3.64 us
  transfers between devices with their start and end apart: 6, of which 3 were waited for; matrix products, arithmetic and copies ran while one was open for 0% of the time, Pallas kernels for 4%

profile of v4, /device:TPU:2, one launch (start us, length us, event | category | flops | bytes accessed | tf_op | source)
XLA Modules:
  0.0 91.7 jit_solution(1547605750359049915)
XLA Ops:
  0.6 1.1 %shard_map.122 = (bf16[512,128]{1,0:T(8,128)(2,1)S(1)}, bf16[512,128]{1,0:T(8,128)(2,1)S(1)}, bf16[512,256]{1,0:T(8,128)(2,1)S(1)}) custom-call(bf16[512,256]{1,0:T(8,128)(2,1)} %bitcast.6, bf16[64,4,128]{2,1,0:T(4,128)(2,1)} %bitcast.9), custom_call_target="tpu_custom_call" | custom-call | tf_op jit(solution)/shard_map/pallas_call | solution.py:40
  1.7 1.9 %collective-permute-start.1 = (bf16[512,128]{1,0:T(8,128)(2,1)S(1)}, bf16[512,128]{1,0:T(8,128)(2,1)S(1)}, u32[]{:S(2)}, u32[]{:S(2)}) collective-permute-start(bf16[512,128]{1,0:T(8,128)(2,1)S(1)} %get-tuple-element.25), channel_id=1, source_target_pairs={{0,4},{4,0},{1,5},{5,1},{2,6},{6,2},{3,7},{7,3},{8,12},{12,8},{9,1... | collective-permute-start | bytes 393224 | tf_op jit(solution)/shard_map/ppermute | solution.py:451
  3.6 16.3 %collective-permute-start = (bf16[512,128]{1,0:T(8,128)(2,1)S(1)}, bf16[512,128]{1,0:T(8,128)(2,1)S(1)}, u32[]{:S(2)}, u32[]{:S(2)}) collective-permute-start(bf16[512,128]{1,0:T(8,128)(2,1)S(1)} %get-tuple-element.24.up), channel_id=1, source_target_pairs={{0,124},{4,8},{8,4},{12,16},{16,12},{20,24},{24,20},{28,32},{32,28... | collective-permute-start | bytes 393224 | tf_op jit(solution)/shard_map/ppermute | solution.py:450
  20.6 1.6 %shard_map.121 = (bf16[64,128]{1,0:T(8,128)(2,1)S(1)}, s32[64,128]{1,0:T(8,128)S(1)}, bf16[16,64]{1,0:T(8,128)(2,1)S(1)}, bf16[512,256]{1,0:T(8,128)(2,1)S(1)}, ...) custom-call(s32[4,4,128]{2,1,0:T(4,128)} %bitcast.10, ...), custom_call_target="tpu_custom_call" | custom-call | tf_op jit(solution)/shard_map/pallas_call | solution.py:40
  22.2 1.8 %collective-permute-done.outer = bf16[512,128]{1,0:T(8,128)(2,1)S(1)} collective-permute-done((bf16[512,128]{1,0:T(8,128)(2,1)S(1)}, bf16[512,128]{1,0:T(8,128)(2,1)S(1)}, u32[]{:S(2)}, u32[]{:S(2)}) %collective-permute-start) | collective-permute-done | bytes 131104 | tf_op jit(solution)/shard_map/ppermute | solution.py:450
  24.0 0.2 shard_map.123
  24.1 9.0 %all_to_all.20.arrived = bf16[4,48,256]{2,1,0:T(8,128)(2,1)S(1)} all-to-all(bf16[4,48,256]{2,1,0:T(8,128)(2,1)S(1)} %shard_map.123), channel_id=1, replica_groups=mesh['ens'=4,'yh'=2,'z'=8,'core'=2,'ox'=4] {'ox'}, dimensions={0} | all-to-all | bytes 196608 | tf_op jit(solution)/shard_map/all_to_all | solution.py:470
  33.1 2.9 %shard_map.124 = (bf16[512,256]{1,0:T(8,128)(2,1)S(1)}, bf16[1424,256]{1,0:T(8,128)(2,1)S(1)}, f32[1288,256]{1,0:T(8,128)S(1)}) custom-call(bf16[16,64]{1,0:T(8,128)(2,1)S(1)} %get-tuple-element.21.gather, s32[64,128]{1,0:T(8,128)S(1)} %get-tuple-element.22.offset, bf16[512,256]{1,0:T(8,128)(2,1)S(1)} %get-tuple-element.23.state, ...), custom_call_target="tpu_custom_call" | custom-call | tf_op jit(solution)/shard_map/pallas_call | solution.py:40
  36.0 1.9 %collective-permute-start.2 = (bf16[1424,256]{1,0:T(8,128)(2,1)S(1)}, bf16[1424,256]{1,0:T(8,128)(2,1)S(1)}, u32[]{:S(2)}, u32[]{:S(2)}) collective-permute-start(bf16[1424,256]{1,0:T(8,128)(2,1)S(1)} %get-tuple-element.33), channel_id=1, source_target_pairs={{0,4},{4,0},{1,5},{5,1},{2,6},{6,2},{3,7},{7,3},{8,12},{12,8},{9,1... | collective-permute-start | bytes 2187272 | tf_op jit(solution)/shard_map/ppermute | solution.py:486
  37.9 2.2 %collective-permute-done.2.got = bf16[1424,256]{1,0:T(8,128)(2,1)S(1)} collective-permute-done((bf16[1424,256]{1,0:T(8,128)(2,1)S(1)}, bf16[1424,256]{1,0:T(8,128)(2,1)S(1)}, u32[]{:S(2)}, u32[]{:S(2)}) %collective-permute-start.2) | collective-permute-done | bytes 729120 | tf_op jit(solution)/shard_map/ppermute | solution.py:486
  40.1 0.3 shard_map.125
  40.4 14.2 %all_to_all.21.arrived.got = bf16[4,336,256]{2,1,0:T(8,128)(2,1)S(1)} all-to-all(bf16[4,336,256]{2,1,0:T(8,128)(2,1)S(1)} %get-tuple-element.36), channel_id=1, replica_groups=mesh['ens'=4,'yh'=2,'z'=8,'core'=2,'ox'=4] {'ox'}, dimensions={0} | all-to-all | bytes 1376256 | tf_op jit(solution)/shard_map/all_to_all | solution.py:495
  54.6 0.1 shard_map.130
  54.7 12.5 %all_to_all.22.got = bf16[8,48,256]{2,1,0:T(8,128)(2,1)S(1)} all-to-all(bf16[8,48,256]{2,1,0:T(8,128)(2,1)S(1)} %shard_map.130), channel_id=1, replica_groups=mesh['ens'=4,'yh'=2,'z'=8,'core'=2,'ox'=4] {'z'}, dimensions={0} | all-to-all | bytes 393216 | tf_op jit(solution)/shard_map/all_to_all | solution.py:499
  67.2 0.7 shard_map.131
  67.9 6.9 %all-to-all-start.3 = ((bf16[8,32,256]{2,1,0:T(8,128)(2,1)}), bf16[8,32,256]{2,1,0:T(8,128)(2,1)S(1)}, u32[]{:S(2)}, u32[]{:S(2)}) async-start(bf16[8,32,256]{2,1,0:T(8,128)(2,1)} %shard_map.131), calls=%async_computation.3 | async-start | bytes 262144 | tf_op jit(solution)/shard_map/all_to_all | solution.py:501
  74.8 3.6 %collective-permute-start.3 = (bf16[128,256]{1,0:T(8,128)(2,1)S(1)}, bf16[128,256]{1,0:T(8,128)(2,1)S(1)}, u32[]{:S(2)}, u32[]{:S(2)}) collective-permute-start(bf16[128,256]{1,0:T(8,128)(2,1)S(1)} %shard_map.126), channel_id=1, source_target_pairs={{0,124},{4,8},{8,4},{12,16},{16,12},{20,24},{24,20},{28,32},{32,28... | collective-permute-start | bytes 196616 | tf_op jit(solution)/shard_map/ppermute | solution.py:488
  78.5 7.9 %collective-permute-start.4 = (bf16[16,256]{1,0:T(8,128)(2,1)S(1)}, bf16[16,256]{1,0:T(8,128)(2,1)S(1)}, u32[]{:S(2)}, u32[]{:S(2)}) collective-permute-start(bf16[16,256]{1,0:T(8,128)(2,1)S(1)} %shard_map.128), channel_id=1, source_target_pairs={{0,124},{4,8},{8,4},{12,16},{16,12},{20,24},{24,20},{28,32},{32,28... | collective-permute-start | bytes 24584 | tf_op jit(solution)/shard_map/ppermute | solution.py:497
  86.4 0.0 collective-permute-done.3.across
  86.4 0.8 shard_map.127.partial
  87.2 2.8 %collective-permute-done.4.corners = bf16[16,256]{1,0:T(8,128)(2,1)S(1)} collective-permute-done((bf16[16,256]{1,0:T(8,128)(2,1)S(1)}, bf16[16,256]{1,0:T(8,128)(2,1)S(1)}, u32[]{:S(2)}, u32[]{:S(2)}) %collective-permute-start.4) | collective-permute-done | bytes 8224 | tf_op jit(solution)/shard_map/ppermute | solution.py:497
  90.0 1.0 %shard_map.129 = bf16[512,256]{1,0:T(8,128)(2,1)} custom-call(f32[512,256]{1,0:T(8,128)S(1)} %shard_map.127.partial, bf16[4,336,256]{2,1,0:T(8,128)(2,1)S(1)} %all_to_all.21.arrived.got, bf16[16,256]{1,0:T(8,128)(2,1)S(1)} %collective-permute-done.4.corners, bf16[9,256,256]{2,1,0:T(8,128)(2,1)S(1)} %get-tuple-element.28.conv), custom_call_target="tpu_custom_call" | custom-call | tf_op jit(solution)/shard_map/pallas_call | solution.py:40
  91.1 0.0 all-to-all-done.3.got
  91.1 0.6 shard_map.132
  (3 shorter events, 0.0 us)
Async XLA Ops:
  1.7 20.5 %collective-permute-start.1 = (bf16[512,128]{1,0:T(8,128)(2,1)S(1)}, bf16[512,128]{1,0:T(8,128)(2,1)S(1)}, u32[]{:S(2)}, u32[]{:S(2)}) collective-permute-start(bf16[512,128]{1,0:T(8,128)(2,1)S(1)} %get-tuple-element.25), channel_id=1, source_target_pairs={{0,4},{4,0},{1,5},{5,1},{2,6},{6,2},{3,7},{7,3},{8,12},{12,8},{9,1... | collective-permute-start | bytes 393224 | tf_op jit(solution)/shard_map/ppermute | solution.py:451
  3.6 20.3 %collective-permute-start = (bf16[512,128]{1,0:T(8,128)(2,1)S(1)}, bf16[512,128]{1,0:T(8,128)(2,1)S(1)}, u32[]{:S(2)}, u32[]{:S(2)}) collective-permute-start(bf16[512,128]{1,0:T(8,128)(2,1)S(1)} %get-tuple-element.24.up), channel_id=1, source_target_pairs={{0,124},{4,8},{8,4},{12,16},{16,12},{20,24},{24,20},{28,32},{32,28... | collective-permute-start | bytes 393224 | tf_op jit(solution)/shard_map/ppermute | solution.py:450
  36.0 4.1 %collective-permute-start.2 = (bf16[1424,256]{1,0:T(8,128)(2,1)S(1)}, bf16[1424,256]{1,0:T(8,128)(2,1)S(1)}, u32[]{:S(2)}, u32[]{:S(2)}) collective-permute-start(bf16[1424,256]{1,0:T(8,128)(2,1)S(1)} %get-tuple-element.33), channel_id=1, source_target_pairs={{0,4},{4,0},{1,5},{5,1},{2,6},{6,2},{3,7},{7,3},{8,12},{12,8},{9,1... | collective-permute-start | bytes 2187272 | tf_op jit(solution)/shard_map/ppermute | solution.py:486
  67.9 23.2 %all-to-all-start.3 = ((bf16[8,32,256]{2,1,0:T(8,128)(2,1)}), bf16[8,32,256]{2,1,0:T(8,128)(2,1)S(1)}, u32[]{:S(2)}, u32[]{:S(2)}) async-start(bf16[8,32,256]{2,1,0:T(8,128)(2,1)} %shard_map.131), calls=%async_computation.3 | async-start | bytes 262144 | tf_op jit(solution)/shard_map/all_to_all | solution.py:501
  74.8 11.6 %collective-permute-start.3 = (bf16[128,256]{1,0:T(8,128)(2,1)S(1)}, bf16[128,256]{1,0:T(8,128)(2,1)S(1)}, u32[]{:S(2)}, u32[]{:S(2)}) collective-permute-start(bf16[128,256]{1,0:T(8,128)(2,1)S(1)} %shard_map.126), channel_id=1, source_target_pairs={{0,124},{4,8},{8,4},{12,16},{16,12},{20,24},{24,20},{28,32},{32,28... | collective-permute-start | bytes 196616 | tf_op jit(solution)/shard_map/ppermute | solution.py:488
  78.5 11.6 %collective-permute-start.4 = (bf16[16,256]{1,0:T(8,128)(2,1)S(1)}, bf16[16,256]{1,0:T(8,128)(2,1)S(1)}, u32[]{:S(2)}, u32[]{:S(2)}) collective-permute-start(bf16[16,256]{1,0:T(8,128)(2,1)S(1)} %shard_map.128), channel_id=1, source_target_pairs={{0,124},{4,8},{8,4},{12,16},{16,12},{20,24},{24,20},{28,32},{32,28... | collective-permute-start | bytes 24584 | tf_op jit(solution)/shard_map/ppermute | solution.py:497

commit v5 on v4

--- a/solution.py
+++ b/solution.py
@@ -15,6 +15,7 @@
 CH = 256
 NLON = 4
 SHARE = 20
+SCALE = 1.0 / 512.0
 VM = pl.BlockSpec(memory_space=pltpu.VMEM)
 HBM = pl.BlockSpec(memory_space=pltpu.HBM)
 ANY = pl.BlockSpec(memory_space=pl.ANY)
@@ -118,8 +119,9 @@
 def pick_kernel(*refs):
     sources, pick, offset_out, gather_out = refs[:8], refs[8], refs[9], refs[10]
     sources, wet = sources[:2] + sources[3:], sources[2]
-    iatm, ioff, sems = refs[16:19]
-    targets = (iatm, ioff) + refs[11:16]
+    iatm, ioff, mix, sems = refs[16:20]
+    act_base, cot, conv, flux_weight, regrid = refs[11:16]
+    targets = (iatm, ioff, cot, conv, mix, flux_weight, regrid)
     copies = [
         pltpu.make_async_copy(source, target, sems.at[n])
         for n, (source, target) in enumerate(zip(sources, targets))
@@ -156,6 +158,7 @@
     ).astype(BF)
     for copy in copies[2:]:
         copy.wait()
+    act_base[...] = dot(cot[...], mix[...], ((1,), (1,)))
 
 
 def pack_kernel(pick, state, outer, inner, up, out):
@@ -200,16 +203,16 @@
     arrived,
     cot,
     conv,
-    mix,
+    act_base,
     flux_weight,
     regrid,
     hg_out,
     send_out,
-    keep_out,
+    grads,
+    flux_out,
     shifted,
     turned,
     hidden,
-    grads,
 ):
     ox = lax.axis_index("ox")
     core = lax.axis_index("core")
@@ -230,9 +233,11 @@
         [flux[f // 2][:, (f % 2) * 128 : (f % 2) * 128 + 128] for f in range(4)], axis=0
     ).astype(BF)
     contribution = jnp.zeros((64, 128), F32)
-    for m in range(16):
+    for m in range(8):
         product = dot(blocks, regrid[m], ((1,), (1,)))
-        contribution = jnp.where(offset[...] == m, product, contribution)
+        for side in range(2):
+            part = product[:, side * 128 : side * 128 + 128]
+            contribution = jnp.where(offset[...] == 2 * m + side, part, contribution)
     contribution = contribution.astype(BF)
     cells = dot(gather[...], contribution, ((1,), (0,)))
     cells_high, cells_low = split_two(cells)
@@ -244,8 +249,7 @@
         lo, hi = r * CELLS, (r + 1) * CELLS
         mine = lax.rem(pair_row, 16) // 4 == r
         weights = jnp.where(mine, field_weights, 0.0).astype(BF)
-        act_grad = dot(cot[lo:hi, :], mix[...], ((1,), (1,)))
-        act_grad = act_grad + dot(cells_pair, weights, ((0,), (0,)))
+        act_grad = act_base[lo:hi, :] + dot(cells_pair, weights, ((0,), (0,)))
         value = hidden[lo:hi, :]
         gate = jax.nn.sigmoid(value)
         activation = (value * gate).astype(BF)
@@ -255,26 +259,23 @@
         flux_part = flux_part + jnp.where(
             mine, dot(cells_pair, activation, ((1,), (0,))), 0.0
         )
-    scale = 1.0 / 512.0
     flux_total = jnp.zeros((4, CH), F32)
     for part in range(8):
         flux_total = flux_total + flux_part[part * 4 : part * 4 + 4]
-    flux_high, flux_low = split_two(flux_total * scale)
+    flux_high, flux_low = split_two(flux_total)
     flux_rows = jnp.concatenate([flux_high.astype(F32), flux_low.astype(F32)], axis=0)
     for q in range(3):
         turned[q] = shifted[q].T
     for t in range(9):
         start = (t // 3) * CELLS
         product = dot(turned[t % 3, :, start : start + 512], hg_out[...], ((1,), (0,)))
-        grads[t * CH : (t + 1) * CH, :] = product * scale
+        grads[t * CH : (t + 1) * CH, :] = product
     product = dot(turned[3, :, 0:512], cot[...], ((1,), (0,)))
-    grads[9 * CH : 10 * CH, :] = product * scale
+    grads[9 * CH : 10 * CH, :] = product
     for m in range(16):
-        mine = pl.multiple_of(m * 160 + core * 80, 8)
         other = pl.multiple_of(m * 160 + 80 - core * 80, 8)
-        keep_out[m * 80 : m * 80 + 80, :] = grads[pl.ds(mine, 80), :]
         send_out[m * 80 : m * 80 + 80, :] = grads[pl.ds(other, 80), :].astype(BF)
-    keep_out[1280:1288, :] = flux_rows
+    flux_out[...] = flux_rows
     send_out[1280:1296, :] = jnp.concatenate(
         [flux_rows, jnp.zeros((8, CH), F32)], axis=0
     ).astype(BF)
@@ -287,17 +288,20 @@
     out[...] = jnp.where(core == 0, hg[0:CELLS, :], hg[3 * CELLS : 4 * CELLS, :])
 
 
-def merge_kernel(keep, got, hg, out, padded, total, moved):
+def merge_kernel(grads, flux_rows, got, hg, out, padded, total, moved):
     ox = lax.axis_index("ox")
     core = lax.axis_index("core")
-    total[...] = keep[0:1280, :] + got[0:1280, :].astype(F32)
+    for m in range(16):
+        lo, hi = m * 80, m * 80 + 80
+        mine = pl.multiple_of(m * 160 + core * 80, 8)
+        total[lo:hi, :] = grads[pl.ds(mine, 80), :] + got[lo:hi, :].astype(F32)
     for c in range(NLON):
         for z in range(8):
             for yh in range(2):
                 m = yh * 8 + z
                 to = c * 320 + (z * 2 + yh) * SHARE
                 moved[to : to + SHARE, :] = total[m * 80 + c * SHARE : m * 80 + c * SHARE + SHARE, :]
-    flux = keep[1280:1288, :] + got[1280:1296, :].astype(F32)[0:8]
+    flux = flux_rows[...] + got[1280:1296, :].astype(F32)[0:8]
     flux_high, flux_low = split_two(flux[0:4] + flux[4:8])
     inside = got[1296:1424, :]
     padded[0:CELLS, :] = inside
@@ -360,11 +364,9 @@
     piece = got[0].astype(F32)
     for s in range(1, 8):
         piece = piece + got[s].astype(F32)
-    high, low = split_two(piece[40:44] + piece[44:48])
-    flux = jnp.concatenate([high.astype(F32), low.astype(F32)], axis=0)
-    pad = jnp.zeros((4, CH), F32)
+    flux = piece[40:44] + piece[44:48]
     for yh in range(2):
-        rows = jnp.concatenate([piece[yh * SHARE : yh * SHARE + SHARE], pad, flux], axis=0).astype(BF)
+        rows = jnp.concatenate([piece[yh * SHARE : yh * SHARE + SHARE], flux], axis=0).astype(BF)
         for e in range(4):
             out[e * 2 + yh] = rows
 
@@ -373,8 +375,8 @@
     piece = got[0].astype(F32)
     for s in range(1, 8):
         piece = piece + got[s].astype(F32)
-    weight_out[...] = piece[0:SHARE]
-    flux_out[...] = piece[24:28] + piece[28:32]
+    weight_out[...] = piece[0:SHARE] * SCALE
+    flux_out[...] = piece[SHARE : SHARE + 4] * SCALE
 
 
 def spread_kernel(padded, across, cot, conv, out, shifted):
@@ -449,14 +451,17 @@
     )(state, flux_cot.reshape(64, 4, 128))
     outer = lax.ppermute(up, OY, SWAP)
     inner = lax.ppermute(down, "core", [(0, 1), (1, 0)])
+    regrid_weights = regrid_weights.reshape(8, 256, 128)
     needed = (cot, conv_weight, mix_weight, flux_weight, regrid_weights)
-    pick, offset, gather, cot, conv_weight, mix_weight, flux_weight, regrid_weights = call(
+    pick, offset, gather, act_base, cot, conv_weight, flux_weight, regrid_weights = call(
         pick_kernel,
         (struct((64, 128), BF), struct((64, 128), jnp.int32), struct((16, 64), BF))
-        + tuple(struct(a.shape, a.dtype) for a in needed),
+        + (struct((ROWS * CELLS, CH), F32),)
+        + tuple(struct(a.shape, a.dtype) for a in needed if a is not mix_weight),
         scratch=[
             pltpu.SMEM((4, 4, 128), jnp.int32),
             pltpu.SMEM((4, 4, 128), jnp.int32),
+            pltpu.VMEM((CH, CH), BF),
             pltpu.SemaphoreType.DMA((7,)),
         ],
         specs=[HBM] * 2 + [SM] + [HBM] * 5,
@@ -468,21 +473,21 @@
     )
     packed = call(pack_kernel, struct((NLON, 48, CH), BF), n_in=5)(pick, state, outer, inner, up)
     arrived = lax.all_to_all(packed, "ox", 0, 0, tiled=True)
-    hg, send, keep = call(
+    hg, send, grads, flux_rows = call(
         main_kernel,
         (
             struct((ROWS * CELLS, CH), BF),
             struct((1424, CH), BF),
-            struct((1288, CH), F32),
+            struct((2560, CH), F32),
+            struct((8, CH), F32),
         ),
         scratch=[
             pltpu.VMEM((3, 768, CH), BF),
             pltpu.VMEM((4, CH, 768), BF),
             pltpu.VMEM((512, CH), F32),
-            pltpu.VMEM((2560, CH), F32),
         ],
         n_in=11,
-    )(gather, offset, state, outer, inner, arrived, cot, conv_weight, mix_weight, flux_weight, regrid_weights)
+    )(gather, offset, state, outer, inner, arrived, cot, conv_weight, act_base, flux_weight, regrid_weights)
     got = lax.ppermute(send, "core", [(0, 1), (1, 0)])
     zrow = call(row_kernel, struct((CELLS, CH), BF), n_in=1)(hg)
     across = lax.ppermute(zrow, OY, SWAP)
@@ -490,14 +495,14 @@
         merge_kernel,
         (struct((NLON, 336, CH), BF), struct((768, CH), BF)),
         scratch=[pltpu.VMEM((1280, CH), F32), pltpu.VMEM((1280, CH), F32)],
-        n_in=3,
-    )(keep, got, hg)
+        n_in=4,
+    )(grads, flux_rows, got, hg)
     by_ox = lax.all_to_all(packed, "ox", 0, 0, tiled=True)
     corners = call(corner_kernel, struct((16, CH), BF), n_in=1)(by_ox)
     corners = lax.ppermute(corners, OY, SWAP)
     packed = call(ox_sum_kernel, struct((8, 48, CH), BF), n_in=1)(by_ox)
     by_z = lax.all_to_all(packed, "z", 0, 0, tiled=True)
-    packed = call(z_sum_kernel, struct((8, 32, CH), BF), n_in=1)(by_z)
+    packed = call(z_sum_kernel, struct((8, 24, CH), BF), n_in=1)(by_z)
     by_rest = lax.all_to_all(packed, ("ens", "yh"), 0, 0, tiled=True)
     weight_out, flux_out = call(
         last_sum_kernel, (jax.ShapeDtypeStruct((SHARE, CH), F32), jax.ShapeDtypeStruct((4, CH), F32)), n_in=1

time: 92.3 us -> 91.8 us (level)
  no operation moved by 1% of the time
where the time goes in v5:
time: 91.8 us; the launch traced here: 91.3 us
  starting transfers between devices  38.6 us (42%)
  blocking collectives  35.7 us (39%)
  Pallas kernels  9.18 us (10%)
  waiting for transfers between devices  6.46 us (7%)
  between operations  1.39 us (2%)
    ppermute x1, starting transfers between devices, body(): outer = lax.ppermute(up, OY, SWAP)  16.3 us
    all_to_all x1, blocking collectives, body(): by_ox = lax.all_to_all(packed, 'ox', 0, 0, tiled=True)  14.2 us
    all_to_all x1, blocking collectives, body(): by_z = lax.all_to_all(packed, 'z', 0, 0, tiled=True)  12.5 us
    pallas_call x12, Pallas kernels, placed(): run(*[pltpu.with_memory_space_constraint(a, s.memory_space) if s not in (...  9.18 us
    all_to_all x1, blocking collectives, body(): arrived = lax.all_to_all(packed, 'ox', 0, 0, tiled=True)  8.96 us
    ppermute x1, starting transfers between devices, body(): corners = lax.ppermute(corners, OY, SWAP)  7.94 us
    all_to_all x1, starting transfers between devices, body(): by_rest = lax.all_to_all(packed, ('ens', 'yh'), 0, 0, tiled=True)  6.83 us
    ppermute x1, starting transfers between devices, body(): across = lax.ppermute(zrow, OY, SWAP)  3.64 us
  transfers between devices with their start and end apart: 6, of which 3 were waited for; matrix products, arithmetic and copies ran while one was open for 0% of the time, Pallas kernels for 4%

profile of v5, /device:TPU:2, one launch (start us, length us, event | category | flops | bytes accessed | tf_op | source)
XLA Modules:
  0.0 91.3 jit_solution(7837662778788318866)
XLA Ops:
  0.6 1.1 %shard_map.122 = (bf16[512,128]{1,0:T(8,128)(2,1)S(1)}, bf16[512,128]{1,0:T(8,128)(2,1)S(1)}, bf16[512,256]{1,0:T(8,128)(2,1)S(1)}) custom-call(bf16[512,256]{1,0:T(8,128)(2,1)} %bitcast.8, bf16[64,4,128]{2,1,0:T(4,128)(2,1)} %bitcast.11), custom_call_target="tpu_custom_call" | custom-call | tf_op jit(solution)/shard_map/pallas_call | solution.py:41
  1.7 1.9 %collective-permute-start.1 = (bf16[512,128]{1,0:T(8,128)(2,1)S(1)}, bf16[512,128]{1,0:T(8,128)(2,1)S(1)}, u32[]{:S(2)}, u32[]{:S(2)}) collective-permute-start(bf16[512,128]{1,0:T(8,128)(2,1)S(1)} %get-tuple-element.26), channel_id=1, source_target_pairs={{0,4},{4,0},{1,5},{5,1},{2,6},{6,2},{3,7},{7,3},{8,12},{12,8},{9,1... | collective-permute-start | bytes 393224 | tf_op jit(solution)/shard_map/ppermute | solution.py:453
  3.6 16.3 %collective-permute-start = (bf16[512,128]{1,0:T(8,128)(2,1)S(1)}, bf16[512,128]{1,0:T(8,128)(2,1)S(1)}, u32[]{:S(2)}, u32[]{:S(2)}) collective-permute-start(bf16[512,128]{1,0:T(8,128)(2,1)S(1)} %get-tuple-element.25.up), channel_id=1, source_target_pairs={{0,124},{4,8},{8,4},{12,16},{16,12},{20,24},{24,20},{28,32},{32,28... | collective-permute-start | bytes 393224 | tf_op jit(solution)/shard_map/ppermute | solution.py:452
  20.6 1.9 %shard_map.121 = (bf16[64,128]{1,0:T(8,128)(2,1)S(1)}, s32[64,128]{1,0:T(8,128)S(1)}, bf16[16,64]{1,0:T(8,128)(2,1)S(1)}, f32[512,256]{1,0:T(8,128)S(1)}, bf16[5...) custom-call(s32[4,4,128]{2,1,0:T(4,128)} %bitcast.12, ...), custom_call_target="tpu_custom_call" | custom-call | tf_op jit(solution)/shard_map/pallas_call | solution.py:41
  22.5 0.0 collective-permute-done.1.inner
  22.5 1.5 %collective-permute-done.outer = bf16[512,128]{1,0:T(8,128)(2,1)S(1)} collective-permute-done((bf16[512,128]{1,0:T(8,128)(2,1)S(1)}, bf16[512,128]{1,0:T(8,128)(2,1)S(1)}, u32[]{:S(2)}, u32[]{:S(2)}) %collective-permute-start) | collective-permute-done | bytes 131104 | tf_op jit(solution)/shard_map/ppermute | solution.py:452
  24.0 0.2 shard_map.123
  24.1 9.0 %all_to_all.20.arrived = bf16[4,48,256]{2,1,0:T(8,128)(2,1)S(1)} all-to-all(bf16[4,48,256]{2,1,0:T(8,128)(2,1)S(1)} %shard_map.123), channel_id=1, replica_groups=mesh['ens'=4,'yh'=2,'z'=8,'core'=2,'ox'=4] {'ox'}, dimensions={0} | all-to-all | bytes 196608 | tf_op jit(solution)/shard_map/all_to_all | solution.py:475
  33.1 2.5 %shard_map.124 = (bf16[512,256]{1,0:T(8,128)(2,1)S(1)}, bf16[1424,256]{1,0:T(8,128)(2,1)S(1)}, f32[2560,256]{1,0:T(8,128)S(1)}, f32[8,256]{1,0:T(8,128)S(1)}) custom-call(bf16[16,64]{1,0:T(8,128)(2,1)S(1)} %get-tuple-element.22.gather, s32[64,128]{1,0:T(8,128)S(1)} %get-tuple-element.23.offset, bf16[512,256]{1,0:T(8,128)(2,1)S(1)} %get-tuple-element.24.state, ...), custom_call_target="tpu_custom_call" | custom-call | tf_op jit(solution)/shard_map/pallas_call | solution.py:41
  35.6 1.9 %collective-permute-start.2 = (bf16[1424,256]{1,0:T(8,128)(2,1)S(1)}, bf16[1424,256]{1,0:T(8,128)(2,1)S(1)}, u32[]{:S(2)}, u32[]{:S(2)}) collective-permute-start(bf16[1424,256]{1,0:T(8,128)(2,1)S(1)} %get-tuple-element.35), channel_id=1, source_target_pairs={{0,4},{4,0},{1,5},{5,1},{2,6},{6,2},{3,7},{7,3},{8,12},{12,8},{9,1... | collective-permute-start | bytes 2187272 | tf_op jit(solution)/shard_map/ppermute | solution.py:491
  37.5 2.2 %collective-permute-done.2.got = bf16[1424,256]{1,0:T(8,128)(2,1)S(1)} collective-permute-done((bf16[1424,256]{1,0:T(8,128)(2,1)S(1)}, bf16[1424,256]{1,0:T(8,128)(2,1)S(1)}, u32[]{:S(2)}, u32[]{:S(2)}) %collective-permute-start.2) | collective-permute-done | bytes 729120 | tf_op jit(solution)/shard_map/ppermute | solution.py:491
  39.7 0.3 shard_map.125
  40.0 14.2 %all_to_all.21.arrived.got = bf16[4,336,256]{2,1,0:T(8,128)(2,1)S(1)} all-to-all(bf16[4,336,256]{2,1,0:T(8,128)(2,1)S(1)} %get-tuple-element.38), channel_id=1, replica_groups=mesh['ens'=4,'yh'=2,'z'=8,'core'=2,'ox'=4] {'ox'}, dimensions={0} | all-to-all | bytes 1376256 | tf_op jit(solution)/shard_map/all_to_all | solution.py:500
  54.2 0.1 shard_map.130
  54.3 12.5 %all_to_all.22.got = bf16[8,48,256]{2,1,0:T(8,128)(2,1)S(1)} all-to-all(bf16[8,48,256]{2,1,0:T(8,128)(2,1)S(1)} %shard_map.130), channel_id=1, replica_groups=mesh['ens'=4,'yh'=2,'z'=8,'core'=2,'ox'=4] {'z'}, dimensions={0} | all-to-all | bytes 393216 | tf_op jit(solution)/shard_map/all_to_all | solution.py:504
  66.8 0.7 shard_map.131
  67.5 6.8 %all-to-all-start.3 = ((bf16[8,24,256]{2,1,0:T(8,128)(2,1)}), bf16[8,24,256]{2,1,0:T(8,128)(2,1)S(1)}, u32[]{:S(2)}, u32[]{:S(2)}) async-start(bf16[8,24,256]{2,1,0:T(8,128)(2,1)} %shard_map.131), calls=%async_computation.3 | async-start | bytes 196608 | tf_op jit(solution)/shard_map/all_to_all | solution.py:506
  74.3 3.6 %collective-permute-start.3 = (bf16[128,256]{1,0:T(8,128)(2,1)S(1)}, bf16[128,256]{1,0:T(8,128)(2,1)S(1)}, u32[]{:S(2)}, u32[]{:S(2)}) collective-permute-start(bf16[128,256]{1,0:T(8,128)(2,1)S(1)} %shard_map.126), channel_id=1, source_target_pairs={{0,124},{4,8},{8,4},{12,16},{16,12},{20,24},{24,20},{28,32},{32,28... | collective-permute-start | bytes 196616 | tf_op jit(solution)/shard_map/ppermute | solution.py:493
  78.0 7.9 %collective-permute-start.4 = (bf16[16,256]{1,0:T(8,128)(2,1)S(1)}, bf16[16,256]{1,0:T(8,128)(2,1)S(1)}, u32[]{:S(2)}, u32[]{:S(2)}) collective-permute-start(bf16[16,256]{1,0:T(8,128)(2,1)S(1)} %shard_map.128), channel_id=1, source_target_pairs={{0,124},{4,8},{8,4},{12,16},{16,12},{20,24},{24,20},{28,32},{32,28... | collective-permute-start | bytes 24584 | tf_op jit(solution)/shard_map/ppermute | solution.py:502
  86.0 0.0 collective-permute-done.3.across
  86.0 0.8 shard_map.127.partial
  86.8 2.8 %collective-permute-done.4.corners = bf16[16,256]{1,0:T(8,128)(2,1)S(1)} collective-permute-done((bf16[16,256]{1,0:T(8,128)(2,1)S(1)}, bf16[16,256]{1,0:T(8,128)(2,1)S(1)}, u32[]{:S(2)}, u32[]{:S(2)}) %collective-permute-start.4) | collective-permute-done | bytes 8224 | tf_op jit(solution)/shard_map/ppermute | solution.py:502
  89.6 1.0 %shard_map.129 = bf16[512,256]{1,0:T(8,128)(2,1)} custom-call(f32[512,256]{1,0:T(8,128)S(1)} %shard_map.127.partial, bf16[4,336,256]{2,1,0:T(8,128)(2,1)S(1)} %all_to_all.21.arrived.got, bf16[16,256]{1,0:T(8,128)(2,1)S(1)} %collective-permute-done.4.corners, bf16[9,256,256]{2,1,0:T(8,128)(2,1)S(1)} %get-tuple-element.29.conv), custom_call_target="tpu_custom_call" | custom-call | tf_op jit(solution)/shard_map/pallas_call | solution.py:41
  90.6 0.6 shard_map.132
  (3 shorter events, 0.0 us)
Async XLA Ops:
  1.7 20.8 %collective-permute-start.1 = (bf16[512,128]{1,0:T(8,128)(2,1)S(1)}, bf16[512,128]{1,0:T(8,128)(2,1)S(1)}, u32[]{:S(2)}, u32[]{:S(2)}) collective-permute-start(bf16[512,128]{1,0:T(8,128)(2,1)S(1)} %get-tuple-element.26), channel_id=1, source_target_pairs={{0,4},{4,0},{1,5},{5,1},{2,6},{6,2},{3,7},{7,3},{8,12},{12,8},{9,1... | collective-permute-start | bytes 393224 | tf_op jit(solution)/shard_map/ppermute | solution.py:453
  3.6 20.3 %collective-permute-start = (bf16[512,128]{1,0:T(8,128)(2,1)S(1)}, bf16[512,128]{1,0:T(8,128)(2,1)S(1)}, u32[]{:S(2)}, u32[]{:S(2)}) collective-permute-start(bf16[512,128]{1,0:T(8,128)(2,1)S(1)} %get-tuple-element.25.up), channel_id=1, source_target_pairs={{0,124},{4,8},{8,4},{12,16},{16,12},{20,24},{24,20},{28,32},{32,28... | collective-permute-start | bytes 393224 | tf_op jit(solution)/shard_map/ppermute | solution.py:452
  35.6 4.1 %collective-permute-start.2 = (bf16[1424,256]{1,0:T(8,128)(2,1)S(1)}, bf16[1424,256]{1,0:T(8,128)(2,1)S(1)}, u32[]{:S(2)}, u32[]{:S(2)}) collective-permute-start(bf16[1424,256]{1,0:T(8,128)(2,1)S(1)} %get-tuple-element.35), channel_id=1, source_target_pairs={{0,4},{4,0},{1,5},{5,1},{2,6},{6,2},{3,7},{7,3},{8,12},{12,8},{9,1... | collective-permute-start | bytes 2187272 | tf_op jit(solution)/shard_map/ppermute | solution.py:491
  67.5 23.1 %all-to-all-start.3 = ((bf16[8,24,256]{2,1,0:T(8,128)(2,1)}), bf16[8,24,256]{2,1,0:T(8,128)(2,1)S(1)}, u32[]{:S(2)}, u32[]{:S(2)}) async-start(bf16[8,24,256]{2,1,0:T(8,128)(2,1)} %shard_map.131), calls=%async_computation.3 | async-start | bytes 196608 | tf_op jit(solution)/shard_map/all_to_all | solution.py:506
  74.3 11.6 %collective-permute-start.3 = (bf16[128,256]{1,0:T(8,128)(2,1)S(1)}, bf16[128,256]{1,0:T(8,128)(2,1)S(1)}, u32[]{:S(2)}, u32[]{:S(2)}) collective-permute-start(bf16[128,256]{1,0:T(8,128)(2,1)S(1)} %shard_map.126), channel_id=1, source_target_pairs={{0,124},{4,8},{8,4},{12,16},{16,12},{20,24},{24,20},{28,32},{32,28... | collective-permute-start | bytes 196616 | tf_op jit(solution)/shard_map/ppermute | solution.py:493
  78.0 11.6 %collective-permute-start.4 = (bf16[16,256]{1,0:T(8,128)(2,1)S(1)}, bf16[16,256]{1,0:T(8,128)(2,1)S(1)}, u32[]{:S(2)}, u32[]{:S(2)}) collective-permute-start(bf16[16,256]{1,0:T(8,128)(2,1)S(1)} %shard_map.128), channel_id=1, source_target_pairs={{0,124},{4,8},{8,4},{12,16},{16,12},{20,24},{24,20},{28,32},{32,28... | collective-permute-start | bytes 24584 | tf_op jit(solution)/shard_map/ppermute | solution.py:502

commit v6 on v5

--- a/solution.py
+++ b/solution.py
@@ -26,13 +26,14 @@
     return lax.axis_index("yh") * 16 + lax.axis_index("z") * 2 + lax.axis_index("core")
 
 
-def call(kernel, outs, scratch=(), specs=None, n_in=None):
+def call(kernel, outs, scratch=(), specs=None, n_in=None, outs_at=None, aliases={}):
     specs = specs if specs is not None else [VM] * n_in
     run = pl.pallas_call(
         kernel,
         out_shape=outs,
         in_specs=specs,
-        out_specs=jax.tree.map(lambda _: VM, outs),
+        out_specs=outs_at if outs_at is not None else jax.tree.map(lambda _: VM, outs),
+        input_output_aliases=aliases,
         scratch_shapes=list(scratch),
         compiler_params=pltpu.CompilerParams(vmem_limit_bytes=24 << 20),
     )
@@ -281,6 +282,9 @@
     ).astype(BF)
     first, last = hg_out[0:CELLS, :], hg_out[3 * CELLS : 4 * CELLS, :]
     send_out[1296:1424, :] = jnp.where(core == 0, last, first)
+    outer_row = jnp.where(core == 0, first, last)
+    ends = [edge_cells([outer_row], edge) for edge in range(2)]
+    send_out[1424:1440, :] = jnp.concatenate(ends + [jnp.zeros((14, CH), F32)], axis=0).astype(BF)
 
 
 def row_kernel(hg, out):
@@ -312,6 +316,9 @@
     drop = jnp.where(core == 0, 0, ROWS + 1)
     first = jnp.where(part == drop, 0.0, edge_cells(pieces, 0))
     last = jnp.where(part == drop, 0.0, edge_cells(pieces, 1))
+    ends = got[1424:1440, :].astype(F32)
+    first = jnp.where(part == ROWS + 2, ends[0:1], first)
+    last = jnp.where(part == ROWS + 2, ends[1:2], last)
     for c in range(NLON):
         to_right = jnp.where(lax.rem(ox + 1, NLON) == c, 1.0, 0.0)
         to_left = jnp.where(lax.rem(ox + NLON - 1, NLON) == c, 1.0, 0.0)
@@ -329,17 +336,6 @@
     return left, right
 
 
-def corner_kernel(arrived, out):
-    core = lax.axis_index("core")
-    left, right = side_cells(arrived)
-    pair = jnp.where(
-        core == 0,
-        jnp.concatenate([left[1:2], right[1:2]], axis=0),
-        jnp.concatenate([left[4:5], right[4:5]], axis=0),
-    )
-    out[...] = jnp.concatenate([pair, jnp.zeros((14, CH), F32)], axis=0).astype(BF)
-
-
 def sum_flux(pieces):
     total = pieces[0]
     for piece in pieces[1:]:
@@ -354,29 +350,58 @@
             piece = piece + got[s, z * 40 : z * 40 + 40, :].astype(F32)
         out[z, 0:40, :] = piece.astype(BF)
     flux = sum_flux([got[s, 320:336, :].astype(F32)[0:8] for s in range(NLON)])
-    high, low = split_two(flux)
-    rows = jnp.concatenate([high.astype(F32), low.astype(F32)], axis=0).astype(BF)
+    left, right = side_cells(got)
+    ends = jnp.concatenate(
+        [flux, left[ROWS + 2 : ROWS + 3], right[ROWS + 2 : ROWS + 3], jnp.zeros((2, CH), F32)],
+        axis=0,
+    ).astype(BF)
     for z in range(8):
-        out[z, 40:48, :] = rows
+        out[z, 40:48, :] = ends
 
 
 def z_sum_kernel(got, out):
     piece = got[0].astype(F32)
     for s in range(1, 8):
         piece = piece + got[s].astype(F32)
-    flux = piece[40:44] + piece[44:48]
+    high, low = split_two(piece[40:44])
+    source = lax.rem(lax.axis_index("z") + jnp.where(lax.axis_index("core") == 0, 7, 1), 8)
+    ends = got[source, 32:48, :].astype(F32)[12:14]
+    tail = [ends, jnp.zeros((2, CH), F32), high.astype(F32), low.astype(F32)]
     for yh in range(2):
-        rows = jnp.concatenate([piece[yh * SHARE : yh * SHARE + SHARE], flux], axis=0).astype(BF)
+        rows = jnp.concatenate([piece[yh * SHARE : yh * SHARE + SHARE]] + tail, axis=0).astype(BF)
         for e in range(4):
             out[e * 2 + yh] = rows
 
 
-def last_sum_kernel(got, weight_out, flux_out):
+def last_sum_kernel(got, slabs, conv, _, weight_out, flux_out, out, stage, sems):
+    oy = oy_index()
+    core = lax.axis_index("core")
+    z = lax.axis_index("z")
+    yh = lax.axis_index("yh")
+    wraps = jnp.where(core == 0, z == 0, z == 7)
+    index = lax.axis_index("ens") * 2 + jnp.where(wraps, 1 - yh, yh)
+    exists = jnp.where(jnp.logical_or(oy == 0, oy == 31), 0.0, 1.0)
+    ends = got[index, 16:32, :].astype(F32)[4:6] * exists
+    ends = jnp.concatenate([ends, jnp.zeros((14, CH), F32)], axis=0).astype(BF)
+    slab = lax.broadcasted_iota(jnp.int32, (16, CH), 0)
+    copies = []
+    for side in range(2):
+        tap = jnp.where(core == 0, 8, 2) - 2 * side
+        added = dot(ends, conv[tap], ((1,), (1,)))[side : side + 1]
+        value = slabs[side * 16 : side * 16 + 16, :]
+        stage[side] = jnp.where(slab == side * 15, value + added, value).astype(BF)
+        to = pl.multiple_of(core * (3 * CELLS) + side * (CELLS - 16), 16)
+        copies.append(
+            pltpu.make_async_copy(stage.at[side], out.at[pl.ds(to, 16), :], sems.at[side])
+        )
+        copies[-1].start()
     piece = got[0].astype(F32)
     for s in range(1, 8):
         piece = piece + got[s].astype(F32)
     weight_out[...] = piece[0:SHARE] * SCALE
-    flux_out[...] = piece[SHARE : SHARE + 4] * SCALE
+    flux_out[...] = (piece[24:28] + piece[28:32]) * SCALE
+    for copy in copies:
+        copy.wait()
 
 
 def spread_kernel(padded, across, cot, conv, out, shifted):
@@ -398,27 +423,24 @@
         out[half * 256 : half * 256 + 256, :] = acc
 
 
-def input_kernel(partial, arrived, corners, conv, out):
-    oy = oy_index()
-    core = lax.axis_index("core")
-    exists = jnp.where(jnp.logical_or(oy == 0, oy == 31), 0.0, 1.0)
-    corner = corners[...].astype(F32) * exists
-    part = lax.broadcasted_iota(jnp.int32, (8, CH), 0)
-    at = jnp.where(core == 0, 0, ROWS + 1)
+def input_kernel(partial, arrived, conv, out, slabs):
+    core = lax.axis_index("core")
     out[...] = partial[...].astype(BF)
     slab = lax.broadcasted_iota(jnp.int32, (16, CH), 0)
     for side, cells in enumerate(side_cells(arrived)):
-        cells = jnp.where(part == at, corner[side : side + 1], cells)
         cells = jnp.concatenate([cells, jnp.zeros((8, CH), F32)], axis=0).astype(BF)
         added = jnp.zeros((ROWS, CH), F32)
         for p in (-1, 0, 1):
             product = dot(cells, conv[3 * (p + 1) + 2 - 2 * side], ((1,), (1,)))
             added = added + product[1 - p : 1 - p + ROWS]
+        values = []
         for r in range(ROWS):
             to = r * CELLS + side * (CELLS - 16)
             value = partial[to : to + 16, :]
             value = jnp.where(slab == side * 15, value + added[r : r + 1], value)
             out[to : to + 16, :] = value.astype(BF)
+            values.append(value)
+        slabs[side * 16 : side * 16 + 16, :] = jnp.where(core == 0, values[0], values[3])
 
 
 def body(
@@ -477,7 +499,7 @@
         main_kernel,
         (
             struct((ROWS * CELLS, CH), BF),
-            struct((1424, CH), BF),
+            struct((1440, CH), BF),
             struct((2560, CH), F32),
             struct((8, CH), F32),
         ),
@@ -498,24 +520,30 @@
         n_in=4,
     )(grads, flux_rows, got, hg)
     by_ox = lax.all_to_all(packed, "ox", 0, 0, tiled=True)
-    corners = call(corner_kernel, struct((16, CH), BF), n_in=1)(by_ox)
-    corners = lax.ppermute(corners, OY, SWAP)
     packed = call(ox_sum_kernel, struct((8, 48, CH), BF), n_in=1)(by_ox)
     by_z = lax.all_to_all(packed, "z", 0, 0, tiled=True)
-    packed = call(z_sum_kernel, struct((8, 24, CH), BF), n_in=1)(by_z)
+    packed = call(z_sum_kernel, struct((8, 32, CH), BF), n_in=1)(by_z)
     by_rest = lax.all_to_all(packed, ("ens", "yh"), 0, 0, tiled=True)
-    weight_out, flux_out = call(
-        last_sum_kernel, (jax.ShapeDtypeStruct((SHARE, CH), F32), jax.ShapeDtypeStruct((4, CH), F32)), n_in=1
-    )(by_rest)
     partial = call(
         spread_kernel,
         struct((ROWS * CELLS, CH), F32),
         scratch=[pltpu.VMEM((3, 768, CH), BF)],
         n_in=4,
     )(padded, across, cot, conv_weight)
-    input_grad = call(input_kernel, jax.ShapeDtypeStruct((ROWS * CELLS, CH), BF), n_in=4)(
-        partial, by_ox, corners, conv_weight
-    )
+    plain = jax.ShapeDtypeStruct
+    input_grad, slabs = call(
+        input_kernel,
+        (plain((ROWS * CELLS, CH), BF), struct((32, CH), F32)),
+        n_in=3,
+    )(partial, by_ox, conv_weight)
+    weight_out, flux_out, input_grad = call(
+        last_sum_kernel,
+        (plain((SHARE, CH), F32), plain((4, CH), F32), plain((ROWS * CELLS, CH), BF)),
+        scratch=[pltpu.VMEM((2, 16, CH), BF), pltpu.SemaphoreType.DMA((2,))],
+        specs=[VM, VM, VM, HBM],
+        outs_at=(VM, VM, HBM),
+        aliases={3: 2},
+    )(by_rest, slabs, conv_weight, input_grad)
     return (input_grad.reshape(1, ROWS, CELLS, CH), weight_out, flux_out)
 
 

time: 91.8 us -> 91.4 us (level)
  the two profiles are of different devices: /device:TPU:2 before, /device:TPU:32 now
where the time goes in v6:
time: 91.4 us; the launch traced here: 91 us
  blocking collectives  43.3 us (47%)
  starting transfers between devices  23.6 us (26%)
  waiting for transfers between devices  12.8 us (14%)
  Pallas kernels  9.92 us (11%)
  between operations  1.37 us (1%)
    all_to_all x1, blocking collectives, body(): by_z = lax.all_to_all(packed, 'z', 0, 0, tiled=True)  19.3 us
    all_to_all x1, blocking collectives, body(): by_ox = lax.all_to_all(packed, 'ox', 0, 0, tiled=True)  14.2 us
    ppermute x1, starting transfers between devices, body(): outer = lax.ppermute(up, OY, SWAP)  10.6 us
    ppermute x1, waiting for transfers between devices, body(): across = lax.ppermute(zrow, OY, SWAP)  10.4 us
    pallas_call x11, Pallas kernels, placed(): run(*[pltpu.with_memory_space_constraint(a, s.memory_space) if s not in (...  9.92 us
    all_to_all x1, blocking collectives, body(): arrived = lax.all_to_all(packed, 'ox', 0, 0, tiled=True)  9.89 us
    all_to_all x1, starting transfers between devices, body(): by_rest = lax.all_to_all(packed, ('ens', 'yh'), 0, 0, tiled=True)  7.2 us
    ppermute x1, waiting for transfers between devices, body(): got = lax.ppermute(send, 'core', [(0, 1), (1, 0)])  2.18 us
  transfers between devices with their start and end apart: 5, of which 3 were waited for; matrix products, arithmetic and copies ran while one was open for 0% of the time, Pallas kernels for 4%

profile of v6, /device:TPU:32, one launch (start us, length us, event | category | flops | bytes accessed | tf_op | source)
XLA Modules:
  0.0 91.0 jit_solution(3911984186383591185)
XLA Ops:
  0.6 1.1 %shard_map.122 = (bf16[512,128]{1,0:T(8,128)(2,1)S(1)}, bf16[512,128]{1,0:T(8,128)(2,1)S(1)}, bf16[512,256]{1,0:T(8,128)(2,1)S(1)}) custom-call(bf16[512,256]{1,0:T(8,128)(2,1)} %bitcast.9, bf16[64,4,128]{2,1,0:T(4,128)(2,1)} %bitcast.11), custom_call_target="tpu_custom_call" | custom-call | tf_op jit(solution)/shard_map/pallas_call | solution.py:42
  1.7 1.9 %collective-permute-start.1 = (bf16[512,128]{1,0:T(8,128)(2,1)S(1)}, bf16[512,128]{1,0:T(8,128)(2,1)S(1)}, u32[]{:S(2)}, u32[]{:S(2)}) collective-permute-start(bf16[512,128]{1,0:T(8,128)(2,1)S(1)} %get-tuple-element.29), channel_id=1, source_target_pairs={{0,4},{4,0},{1,5},{5,1},{2,6},{6,2},{3,7},{7,3},{8,12},{12,8},{9,1... | collective-permute-start | bytes 393224 | tf_op jit(solution)/shard_map/ppermute | solution.py:475
  3.6 10.6 %collective-permute-start = (bf16[512,128]{1,0:T(8,128)(2,1)S(1)}, bf16[512,128]{1,0:T(8,128)(2,1)S(1)}, u32[]{:S(2)}, u32[]{:S(2)}) collective-permute-start(bf16[512,128]{1,0:T(8,128)(2,1)S(1)} %get-tuple-element.28.up), channel_id=1, source_target_pairs={{0,124},{4,8},{8,4},{12,16},{16,12},{20,24},{24,20},{28,32},{32,28... | collective-permute-start | bytes 393224 | tf_op jit(solution)/shard_map/ppermute | solution.py:474
  14.9 1.9 %shard_map.121 = (bf16[64,128]{1,0:T(8,128)(2,1)S(1)}, s32[64,128]{1,0:T(8,128)S(1)}, bf16[16,64]{1,0:T(8,128)(2,1)S(1)}, f32[512,256]{1,0:T(8,128)S(1)}, bf16[5...) custom-call(s32[4,4,128]{2,1,0:T(4,128)} %bitcast.12, ...), custom_call_target="tpu_custom_call" | custom-call | tf_op jit(solution)/shard_map/pallas_call | solution.py:42
  16.8 0.0 collective-permute-done.1.inner
  16.8 0.2 collective-permute-done.outer
  17.0 0.2 shard_map.123
  17.1 9.9 %all_to_all.20.arrived = bf16[4,48,256]{2,1,0:T(8,128)(2,1)S(1)} all-to-all(bf16[4,48,256]{2,1,0:T(8,128)(2,1)S(1)} %shard_map.123), channel_id=1, replica_groups=mesh['ens'=4,'yh'=2,'z'=8,'core'=2,'ox'=4] {'ox'}, dimensions={0} | all-to-all | bytes 196608 | tf_op jit(solution)/shard_map/all_to_all | solution.py:497
  27.0 2.5 %shard_map.124 = (bf16[512,256]{1,0:T(8,128)(2,1)S(1)}, bf16[1440,256]{1,0:T(8,128)(2,1)S(1)}, f32[2560,256]{1,0:T(8,128)S(1)}, f32[8,256]{1,0:T(8,128)S(1)}) custom-call(bf16[16,64]{1,0:T(8,128)(2,1)S(1)} %get-tuple-element.25.gather, s32[64,128]{1,0:T(8,128)S(1)} %get-tuple-element.26.offset, bf16[512,256]{1,0:T(8,128)(2,1)S(1)} %get-tuple-element.27.state, ...), custom_call_target="tpu_custom_call" | custom-call | tf_op jit(solution)/shard_map/pallas_call | solution.py:42
  29.5 1.9 %collective-permute-start.2 = (bf16[1440,256]{1,0:T(8,128)(2,1)S(1)}, bf16[1440,256]{1,0:T(8,128)(2,1)S(1)}, u32[]{:S(2)}, u32[]{:S(2)}) collective-permute-start(bf16[1440,256]{1,0:T(8,128)(2,1)S(1)} %get-tuple-element.38), channel_id=1, source_target_pairs={{0,4},{4,0},{1,5},{5,1},{2,6},{6,2},{3,7},{7,3},{8,12},{12,8},{9,1... | collective-permute-start | bytes 2211848 | tf_op jit(solution)/shard_map/ppermute | solution.py:513
  31.4 2.2 %collective-permute-done.2.got = bf16[1440,256]{1,0:T(8,128)(2,1)S(1)} collective-permute-done((bf16[1440,256]{1,0:T(8,128)(2,1)S(1)}, bf16[1440,256]{1,0:T(8,128)(2,1)S(1)}, u32[]{:S(2)}, u32[]{:S(2)}) %collective-permute-start.2) | collective-permute-done | bytes 737312 | tf_op jit(solution)/shard_map/ppermute | solution.py:513
  33.6 0.3 shard_map.125
  33.9 14.2 %all_to_all.21.got.arrived = bf16[4,336,256]{2,1,0:T(8,128)(2,1)S(1)} all-to-all(bf16[4,336,256]{2,1,0:T(8,128)(2,1)S(1)} %get-tuple-element.40), channel_id=1, replica_groups=mesh['ens'=4,'yh'=2,'z'=8,'core'=2,'ox'=4] {'ox'}, dimensions={0} | all-to-all | bytes 1376256 | tf_op jit(solution)/shard_map/all_to_all | solution.py:522
  48.1 0.1 shard_map.126
  48.2 19.3 %all_to_all.22.got = bf16[8,48,256]{2,1,0:T(8,128)(2,1)S(1)} all-to-all(bf16[8,48,256]{2,1,0:T(8,128)(2,1)S(1)} %shard_map.126), channel_id=1, replica_groups=mesh['ens'=4,'yh'=2,'z'=8,'core'=2,'ox'=4] {'z'}, dimensions={0} | all-to-all | bytes 393216 | tf_op jit(solution)/shard_map/all_to_all | solution.py:524
  67.5 0.7 shard_map.127
  68.2 7.2 %all-to-all-start.3 = ((bf16[8,32,256]{2,1,0:T(8,128)(2,1)}), bf16[8,32,256]{2,1,0:T(8,128)(2,1)S(1)}, u32[]{:S(2)}, u32[]{:S(2)}) async-start(bf16[8,32,256]{2,1,0:T(8,128)(2,1)} %shard_map.127), calls=%async_computation.3 | async-start | bytes 262144 | tf_op jit(solution)/shard_map/all_to_all | solution.py:526
  75.4 1.9 %collective-permute-start.3 = (bf16[128,256]{1,0:T(8,128)(2,1)S(1)}, bf16[128,256]{1,0:T(8,128)(2,1)S(1)}, u32[]{:S(2)}, u32[]{:S(2)}) collective-permute-start(bf16[128,256]{1,0:T(8,128)(2,1)S(1)} %shard_map.128), channel_id=1, source_target_pairs={{0,124},{4,8},{8,4},{12,16},{16,12},{20,24},{24,20},{28,32},{32,28... | collective-permute-start | bytes 196616 | tf_op jit(solution)/shard_map/ppermute | solution.py:515
  77.3 10.4 %collective-permute-done.3.across = bf16[128,256]{1,0:T(8,128)(2,1)S(1)} collective-permute-done((bf16[128,256]{1,0:T(8,128)(2,1)S(1)}, bf16[128,256]{1,0:T(8,128)(2,1)S(1)}, u32[]{:S(2)}, u32[]{:S(2)}) %collective-permute-start.3) | collective-permute-done | bytes 65568 | tf_op jit(solution)/shard_map/ppermute | solution.py:515
  87.7 0.8 shard_map.129.partial
  88.5 1.0 %shard_map.130 = (bf16[512,256]{1,0:T(8,128)(2,1)}, f32[32,256]{1,0:T(8,128)S(1)}) custom-call(f32[512,256]{1,0:T(8,128)S(1)} %shard_map.129.partial, bf16[4,336,256]{2,1,0:T(8,128)(2,1)S(1)} %all_to_all.21.got.arrived, bf16[9,256,256]{2,1,0:T(8,128)(2,1)S(1)} %get-tuple-element.32.conv), custom_call_target="tpu_custom_call" | custom-call | tf_op jit(solution)/shard_map/pallas_call | solution.py:42
  89.5 0.0 all-to-all-done.3.got
  89.5 1.4 %shard_map.131 = (f32[20,256]{1,0:T(8,128)}, f32[4,256]{1,0:T(4,128)}, bf16[512,256]{1,0:T(8,128)(2,1)}) custom-call(bf16[8,32,256]{2,1,0:T(8,128)(2,1)S(1)} %all-to-all-done.3.got, f32[32,256]{1,0:T(8,128)S(1)} %get-tuple-element.42.slabs, bf16[9,256,256]{2,1,0:T(8,128)(2,1)S(1)} %get-tuple-element.32.conv, ...), custom_call_target="tpu_custom_call", output_to_operand_aliasing={{2}: (3, {})} | custom-call | tf_op jit(solution)/shard_map/pallas_call | solution.py:42
  (1 shorter events, 0.0 us)
Async XLA Ops:
  1.7 15.0 %collective-permute-start.1 = (bf16[512,128]{1,0:T(8,128)(2,1)S(1)}, bf16[512,128]{1,0:T(8,128)(2,1)S(1)}, u32[]{:S(2)}, u32[]{:S(2)}) collective-permute-start(bf16[512,128]{1,0:T(8,128)(2,1)S(1)} %get-tuple-element.29), channel_id=1, source_target_pairs={{0,4},{4,0},{1,5},{5,1},{2,6},{6,2},{3,7},{7,3},{8,12},{12,8},{9,1... | collective-permute-start | bytes 393224 | tf_op jit(solution)/shard_map/ppermute | solution.py:475
  3.6 13.3 %collective-permute-start = (bf16[512,128]{1,0:T(8,128)(2,1)S(1)}, bf16[512,128]{1,0:T(8,128)(2,1)S(1)}, u32[]{:S(2)}, u32[]{:S(2)}) collective-permute-start(bf16[512,128]{1,0:T(8,128)(2,1)S(1)} %get-tuple-element.28.up), channel_id=1, source_target_pairs={{0,124},{4,8},{8,4},{12,16},{16,12},{20,24},{24,20},{28,32},{32,28... | collective-permute-start | bytes 393224 | tf_op jit(solution)/shard_map/ppermute | solution.py:474
  29.5 4.1 %collective-permute-start.2 = (bf16[1440,256]{1,0:T(8,128)(2,1)S(1)}, bf16[1440,256]{1,0:T(8,128)(2,1)S(1)}, u32[]{:S(2)}, u32[]{:S(2)}) collective-permute-start(bf16[1440,256]{1,0:T(8,128)(2,1)S(1)} %get-tuple-element.38), channel_id=1, source_target_pairs={{0,4},{4,0},{1,5},{5,1},{2,6},{6,2},{3,7},{7,3},{8,12},{12,8},{9,1... | collective-permute-start | bytes 2211848 | tf_op jit(solution)/shard_map/ppermute | solution.py:513
  68.2 21.4 %all-to-all-start.3 = ((bf16[8,32,256]{2,1,0:T(8,128)(2,1)}), bf16[8,32,256]{2,1,0:T(8,128)(2,1)S(1)}, u32[]{:S(2)}, u32[]{:S(2)}) async-start(bf16[8,32,256]{2,1,0:T(8,128)(2,1)} %shard_map.127), calls=%async_computation.3 | async-start | bytes 262144 | tf_op jit(solution)/shard_map/all_to_all | solution.py:526
  75.4 12.3 %collective-permute-start.3 = (bf16[128,256]{1,0:T(8,128)(2,1)S(1)}, bf16[128,256]{1,0:T(8,128)(2,1)S(1)}, u32[]{:S(2)}, u32[]{:S(2)}) collective-permute-start(bf16[128,256]{1,0:T(8,128)(2,1)S(1)} %shard_map.128), channel_id=1, source_target_pairs={{0,124},{4,8},{8,4},{12,16},{16,12},{20,24},{24,20},{28,32},{32,28... | collective-permute-start | bytes 196616 | tf_op jit(solution)/shard_map/ppermute | solution.py:515
